TPU v7x, 32 devices: a whole 2x2x4 slice. The times are simulated.
32 devices in a mesh: dp: 32 (over z, y, x, core).
Axes of the slice: x: 2, y: 2, z: 4, core: 2. Of those that a mesh axis runs over, the one named last changes fastest.
Arguments:
- tokens: bfloat16 [6144, 768], P('dp'), may hold values from -6 to 6
- seq_ids: int32 [6144], P('dp'), may hold values from -1 to 1, as said below
- positions: int32 [6144], P('dp'), may hold values from 0 to 191, as said below
- cotangent: bfloat16 [6144, 768], P('dp'), may hold values from -6 to 6
- attn_gain: bfloat16 [768], P('dp'), may hold values from 0.099609375 to 1.8984375
- w_query: bfloat16 [768, 768], P('dp'), may hold values from -0.21875 to 0.21875
- w_key: bfloat16 [768, 768], P('dp'), may hold values from -0.21875 to 0.21875
- w_value: bfloat16 [768, 768], P('dp'), may hold values from -0.21875 to 0.21875
- w_output: bfloat16 [768, 768], P(None, 'dp'), may hold values from -0.875 to 0.875
- mlp_gain: bfloat16 [768], P('dp'), may hold values from 0.099609375 to 1.8984375
- w_gate: bfloat16 [768, 3072], P('dp'), may hold values from -0.21875 to 0.21875
- w_up: bfloat16 [768, 3072], P('dp'), may hold values from -0.21875 to 0.21875
- w_down: bfloat16 [3072, 768], P(None, 'dp'), may hold values from -0.109375 to 0.109375
Outputs:
- out: bfloat16 [6144, 768], P('dp')
- d_tokens: bfloat16 [6144, 768], P('dp')
- d_attn_gain: float32 [768], P('dp')
- d_w_query: float32 [768, 768], P('dp')
- d_w_key: float32 [768, 768], P('dp')
- d_w_value: float32 [768, 768], P('dp')
- d_w_output: float32 [768, 768], P(None, 'dp')
- d_mlp_gain: float32 [768], P('dp')
- d_w_gate: float32 [768, 3072], P('dp')
- d_w_up: float32 [768, 3072], P('dp')
- d_w_down: float32 [3072, 768], P(None, 'dp')
Inputs may be any that keep to these rules, and one draw needn't show every extreme that they name: `seq_ids`: in each aligned block of 192 slots (the slots of one device) the live slots come first: sequence 0, then possibly sequence 1, then empty slots (-1). Each sequence has at least 24 slots, each block at least 96 live slots, and some block is entirely live. `positions`: A token's position counts from 0 at its sequence's first slot and rises by one a slot; empty slots hold 0.
All inputs are finite; a program needn't handle non-finite values.
Results may differ from a plain program's by a relative error of at most 0.013.
Values may be sent and summed in bfloat16 or wider, within the bound.
No kernel may reach another device: no remote copies, remote signals or barrier semaphores. Data moves between devices by JAX's collectives and lax.ppermute only.
A program may use at most 128 MiB of HBM per device.

v0:
```python
import math

import jax
import jax.numpy as jnp
import numpy as np
from jax import lax
from jax.experimental import pallas as pl
from jax.experimental.pallas import tpu as pltpu
from jax.sharding import PartitionSpec as P


HD = 64
LOW = (2, 1)
PARTS = 2
VMEM = 20 * 2**20
EPS = 1e-05
MASKED = -1e30
THETA = 10000.0


f32 = jnp.float32
bf16 = jnp.bfloat16


def gather_orders(n):
    if n == 32:
        return (16, 8, 2, 4, 1), (16, 8, 4, 2, 1)
    bits = [1 << k for k in range(n.bit_length() - 1)]
    order = tuple(reversed(bits))
    return order, order


def nn(a, b):
    return jnp.dot(a, b, preferred_element_type=f32)


def nt(a, b):
    return lax.dot_general(a, b, (((1,), (1,)), ((), ())), preferred_element_type=f32)


def call(kernel, outs, *args, grant=VMEM, **kw):
    out_shape = [jax.ShapeDtypeStruct(s, d) for s, d in outs]
    vmem = pl.BlockSpec(memory_space=pltpu.VMEM)
    smem = pl.BlockSpec(memory_space=pltpu.SMEM)
    return pl.pallas_call(
        kernel,
        out_shape=out_shape,
        in_specs=[smem if v.size == 1 else vmem for v in args],
        out_specs=[vmem] * len(outs),
        compiler_params=pltpu.CompilerParams(vmem_limit_bytes=grant),
        **kw,
    )(*args)


def moved(f, v, select):
    high = v.astype(bf16)
    return f(high, select) + f((v - high.astype(f32)).astype(bf16), select)


def split_nn(v, parts, cols):
    half = parts[0].shape[0]
    return nn(v[:, :half], parts[0][:, cols]) + nn(v[:, half:], parts[1][:, cols])


def split_nt(v, parts, cols):
    return jnp.concatenate([nt(v, p[:, cols]) for p in parts], axis=1)


def allowed_of(seq_row_ref, seq_col_ref):
    row, col = seq_row_ref[...], seq_col_ref[...]
    t = row.shape[1]
    i = lax.broadcasted_iota(jnp.int32, (t, t), 0)
    j = lax.broadcasted_iota(jnp.int32, (t, t), 1)
    return ((col == row) & (col >= 0) & (j <= i)) | (i == j)


def swap_halves(v):
    lane = lax.broadcasted_iota(jnp.int32, v.shape, 1)
    first = (lane % HD) < (HD // 2)
    return jnp.where(first, pltpu.roll(v, 2 * HD - HD // 2, 1), pltpu.roll(v, HD // 2, 1))


def pack_kernel(me, attn_gain, mlp_gain, wq, wk, wv, wo, wgate, wup, wdown, qk, vo, keep, send):
    rows, d = wq.shape
    qk[:, :d] = wq[...]
    qk[:, d : 2 * d] = wk[...]
    spot = lax.broadcasted_iota(jnp.int32, (rows, rows), 0) == lax.broadcasted_iota(jnp.int32, (rows, rows), 1)
    column = lambda ref: jnp.sum(jnp.where(spot, ref[...].astype(f32), 0.0), axis=1, keepdims=True)
    lane = lax.broadcasted_iota(jnp.int32, (rows, 128), 1)
    both = jnp.where(lane == 0, column(attn_gain), jnp.where(lane == 1, column(mlp_gain), 0.0))
    qk[:, 2 * d :] = both.astype(bf16)
    vo[:, :d] = wv[...]
    vo[:, d:] = wo[...]
    low = me[0] % (2 * LOW[0])
    hidden = wgate.shape[1] // 4
    fc = hidden // PARTS
    for ref, flip in ((keep, 0), (send, LOW[0])):
        for i, other in enumerate((0, LOW[1])):
            base = (low ^ (flip + other)) * hidden
            for c in range(PARTS):
                for m, w in enumerate((wgate, wup, wdown)):
                    at = i * 3 * hidden + (c * 3 + m) * fc
                    ref[:, at : at + fc] = w[:, pl.ds(pl.multiple_of(base + c * fc, 128), fc)]


def unpack_kernel(me, *refs):
    parts, outs = refs[:4], refs[4:]
    low = me[0] % (2 * LOW[0])
    hidden = outs[0].shape[1] // 4
    fc = hidden // PARTS
    for ref, flip in zip(parts, (0, LOW[1], LOW[0], LOW[0] + LOW[1])):
        base = (low ^ flip) * hidden
        for c in range(PARTS):
            for m, out in enumerate(outs):
                at = (c * 3 + m) * fc
                out[:, pl.ds(pl.multiple_of(base + c * fc, 128), fc)] = ref[:, at : at + fc].astype(f32)


def prep_kernel(me, tokens, cot, places, live, xp, gb, gbg, own_sel, group_sel, change):
    d = tokens.shape[1]
    rows = places[4, 0]
    share = 2 * LOW[0]
    own = (places[0:1] ^ me[0]) * rows + places[1:2]
    group = (places[2:3] ^ (me[0] - me[0] % share)) * rows + places[3:4]
    source = lax.broadcasted_iota(jnp.int32, (d, d), 0)
    own_sel[...] = (source == own).astype(bf16)
    group_sel[...] = (source == group).astype(bf16)
    own_col = jnp.broadcast_to(own.astype(f32), (128, d)).T[:, 0:1]
    change[...] = (own_col == group.astype(f32)).astype(bf16)
    xp[...] = nn(tokens[...], own_sel[...]).astype(bf16)
    gb[...] = (nn(cot[...], own_sel[...]) * live[...]).astype(bf16)
    gbg[...] = (nn(cot[...], group_sel[...]) * live[...]).astype(bf16)


def attn_kernel(xp, qk0, qk1, vo0, vo1, cos, sin, seq_row, seq_col, n1t, qr, kr, vb, ob, gains, n1):
    d = xp.shape[1]
    qk, vo = (qk0, qk1), (vo0, vo1)
    gt = jnp.concatenate([p[:, 2 * d :] for p in qk], axis=0).astype(f32).T
    gains[...] = gt[0:8]
    x = xp[...].astype(f32)
    r1 = lax.rsqrt(jnp.mean(x * x, axis=-1, keepdims=True) + EPS)
    normed = x * r1 * gt[0:1]
    n1[...] = normed.astype(bf16)
    n1t[...] = normed.T.astype(bf16)
    allowed = allowed_of(seq_row, seq_col)
    pair = 2 * HD
    low = lax.broadcasted_iota(jnp.int32, (x.shape[0], pair), 1) < HD
    scale = HD ** -0.5
    for b in range(d // 256):
        cols = slice(b * 256, (b + 1) * 256)
        q2 = split_nn(n1, qk, cols)
        k2 = split_nn(n1, qk, slice(d + b * 256, d + (b + 1) * 256))
        vb[:, cols] = split_nn(n1, vo, cols).astype(bf16)
        for h in range(2):
            here = slice(h * pair, (h + 1) * pair)
            there = slice(b * 256 + h * pair, b * 256 + (h + 1) * pair)
            q, k = q2[:, here], k2[:, here]
            qr[:, there] = (q * cos[...] + swap_halves(q) * sin[...]).astype(bf16)
            kr[:, there] = (k * cos[...] + swap_halves(k) * sin[...]).astype(bf16)
    for b in range(d // pair):
        cols = slice(b * pair, (b + 1) * pair)
        q, k, v = qr[:, cols], kr[:, cols], vb[:, cols]
        outs = []
        for mine in (low, ~low):
            s = nt(jnp.where(mine, q, jnp.zeros_like(q)), k)
            logits = jnp.where(allowed, s * scale, MASKED)
            e = jnp.exp(logits - jnp.max(logits, axis=-1, keepdims=True))
            p = e / jnp.sum(e, axis=-1, keepdims=True)
            outs.append(nn(p.astype(bf16), v))
        ob[:, cols] = jnp.where(low, outs[0], outs[1]).astype(bf16)


def mid_kernel(xp, ob, vo0, vo1, gains, change, hmid, n2g):
    d = xp.shape[1]
    h = xp[...].astype(f32) + split_nt(ob[...], (vo0, vo1), slice(d, 2 * d))
    hmid[...] = h
    r2 = lax.rsqrt(jnp.mean(h * h, axis=-1, keepdims=True) + EPS)
    n2g[...] = nn((h * r2 * gains[1:2]).astype(bf16), change[...]).astype(bf16)


def ff_kernel(n2, gb, *refs):
    ws, (act, both, keep, send, acc) = refs[:PARTS], refs[PARTS:]
    half = n2.shape[0] // 2
    for c, w in enumerate(ws):
        fc = w.shape[1] // 3
        gate = nn(n2[...], w[:, :fc])
        up = nn(n2[...], w[:, fc : 2 * fc])
        dact = nn(gb[...], w[:, 2 * fc :])
        sig = jax.nn.sigmoid(gate)
        silu = gate * sig
        act[:, c * fc : (c + 1) * fc] = (silu * up).astype(bf16)
        at = 2 * c * fc
        both[:, at : at + fc] = (dact * up * sig * (1.0 + gate * (1.0 - sig))).astype(bf16)
        both[:, at + fc : at + 2 * fc] = (dact * silu).astype(bf16)
        part = nt(both[:, at : at + 2 * fc], w[:, : 2 * fc])
        acc[...] = part if c == 0 else acc[...] + part
    keep[...] = acc[:half].astype(bf16)
    send[...] = acc[half:].astype(bf16)


def ff_grad_kernel(n2, gb, act, both, *refs):
    n2t, gbt = refs[-2:]
    n2t[...] = n2[...].astype(f32).T.astype(bf16)
    gbt[...] = gb[...].astype(f32).T.astype(bf16)
    for c in range(PARTS):
        keep, send = refs[2 * c : 2 * c + 2]
        fc = keep.shape[1] // 3
        runs = 2 ** c
        run = n2t.shape[0] // (2 * runs)
        for left, right, cols in (
            (n2t, both[:, 2 * c * fc : 2 * (c + 1) * fc], slice(0, 2 * fc)),
            (gbt, act[:, c * fc : (c + 1) * fc], slice(2 * fc, 3 * fc)),
        ):
            dw = nn(left[...], right).astype(bf16)
            for r in range(runs):
                keep[r * run : (r + 1) * run, cols] = dw[2 * r * run : (2 * r + 1) * run]
                send[r * run : (r + 1) * run, cols] = dw[(2 * r + 1) * run : (2 * r + 2) * run]


def ff_out_kernel(act, *refs):
    ws, (keep, send) = refs[:PARTS], refs[PARTS:]
    half = act.shape[0] // 2
    fc = ws[0].shape[1] // 3
    for ref, rows in ((keep, slice(0, half)), (send, slice(half, 2 * half))):
        ref[...] = sum(nt(act[rows, c * fc : (c + 1) * fc], w[:, 2 * fc :]) for c, w in enumerate(ws)).astype(bf16)


def back_kernel(k1, g1, g2, hmid, gb, gains, vo0, vo1, ob, change, dh, dob, keep, send, dgain):
    t, d = hmid.shape
    half = d // 2
    total = k1[:t].astype(f32) + g1[:t].astype(f32) + g2[...].astype(f32)
    dn2 = moved(nt, total, change[...])
    h = hmid[...]
    r2 = lax.rsqrt(jnp.mean(h * h, axis=-1, keepdims=True) + EPS)
    dgain[...] = jnp.broadcast_to(jnp.sum(dn2 * h * r2, axis=0, keepdims=True), dgain.shape)
    dn2 = dn2 * gains[1:2]
    out = gb[...].astype(f32) + r2 * dn2 - h * (r2 * r2 * r2) * jnp.mean(dn2 * h, axis=-1, keepdims=True)
    dh[...] = out
    dob[...] = split_nn(out.astype(bf16), (vo0, vo1), slice(d, 2 * d)).astype(bf16)
    dw = nn(out.T.astype(bf16), ob[...]).astype(bf16)
    keep[...] = dw[:half]
    send[...] = dw[half:]


def attn_back_kernel(qr, kr, vb, dob, n1t, cos, sin, seq_row, seq_col, dq, dk, dv, keep, send):
    t, d = qr.shape
    half = d // 2
    pair = 2 * HD
    allowed = allowed_of(seq_row, seq_col)
    low = lax.broadcasted_iota(jnp.int32, (t, pair), 1) < HD
    scale = HD ** -0.5
    for b in range(d // pair):
        cols = slice(b * pair, (b + 1) * pair)
        q, k, v, do = qr[:, cols], kr[:, cols], vb[:, cols], dob[:, cols]
        dqs, dks, dvs = [], [], []
        for mine in (low, ~low):
            s = nt(jnp.where(mine, q, jnp.zeros_like(q)), k)
            logits = jnp.where(allowed, s * scale, MASKED)
            e = jnp.exp(logits - jnp.max(logits, axis=-1, keepdims=True))
            p = e / jnp.sum(e, axis=-1, keepdims=True)
            dp = nt(jnp.where(mine, do, jnp.zeros_like(do)), v)
            dlogit = p * (dp - jnp.sum(dp * p, axis=-1, keepdims=True))
            ds = jnp.where(allowed, dlogit * scale, 0.0)
            dvs.append(nn(p.T.astype(bf16), do))
            dqs.append(nn(ds.astype(bf16), k))
            dks.append(nn(ds.T.astype(bf16), q))
        dv[:, cols] = jnp.where(low, dvs[0], dvs[1]).astype(bf16)
        for grads, ref in ((dqs, dq), (dks, dk)):
            g = jnp.where(low, grads[0], grads[1])
            ref[:, cols] = (g * cos[...] - swap_halves(g) * sin[...]).astype(bf16)
    for part, ref in enumerate((dv, dq)):
        for b in range(d // 256):
            dw = nn(n1t[...], ref[:, b * 256 : (b + 1) * 256]).astype(bf16)
            cols = slice(part * d + b * 256, part * d + (b + 1) * 256)
            keep[:, cols] = dw[:half]
            send[:, cols] = dw[half:]


def last_kernel(dq, dk, dv, qk0, qk1, vo0, vo1, n1t, xp, dh, gains, dgain2, own_sel, dtok, keep, send):
    _, d = xp.shape
    half = d // 2
    qk, vo = (qk0, qk1), (vo0, vo1)
    dn1 = (split_nt(dq[...], qk, slice(0, d)) + split_nt(dk[...], qk, slice(d, 2 * d))
           + split_nt(dv[...], vo, slice(0, d)))
    dw = nn(n1t[...], dk[...]).astype(bf16)
    keep[:, :d] = dw[:half]
    send[:, :d] = dw[half:]
    x = xp[...].astype(f32)
    r1 = lax.rsqrt(jnp.mean(x * x, axis=-1, keepdims=True) + EPS)
    dgain1 = jnp.sum(dn1 * x * r1, axis=0, keepdims=True)
    row = lax.broadcasted_iota(jnp.int32, (128, d), 0)
    both = jnp.where(row == 0, dgain1, jnp.where(row == 1, dgain2[0:1], 0.0)).T.astype(bf16)
    keep[:, d:] = both[:half]
    send[:, d:] = both[half:]
    g = dn1 * gains[0:1]
    out = dh[...] + r1 * g - x * (r1 * r1 * r1) * jnp.mean(g * x, axis=-1, keepdims=True)
    dtok[...] = nt(out.astype(bf16), own_sel[...]).astype(bf16)


def out_kernel(k1, g1, g2, hmid, own_sel, group_sel, out):
    t = hmid.shape[0]
    total = k1[:t].astype(f32) + g1[:t].astype(f32) + g2[...].astype(f32)
    out[...] = (moved(nt, total, group_sel[...]) + moved(nt, hmid[...], own_sel[...])).astype(bf16)


def make_on_device(n):
    first, second = gather_orders(n)
    axis_bits = tuple(reversed(first))
    axis_of = {b: i for i, b in enumerate(axis_bits)}
    k = len(axis_bits)
    assert axis_bits[0] == first[-1] == second[-1]
    high = sorted((b for b in first if b not in LOW), reverse=True)
    ff_orders = (tuple(high), (high[-1],) + tuple(high[:-1]))
    ff_bits = tuple(reversed(high)) + tuple(reversed(LOW))
    ff_axis = {b: i for i, b in enumerate(ff_bits)}

    def swap(a, b):
        return lax.ppermute(a, "dp", [(i, i ^ b) for i in range(n)])

    def gather(shard, order):
        a = shard.reshape((1,) * k + shard.shape)
        for i, b in enumerate(order):
            got = swap(a, b)
            if i == k - 1:
                return tuple(v.reshape((n * shard.shape[0] // 2,) + shard.shape[1:]) for v in (a, got))
            a = jnp.concatenate([a, got], axis=axis_of[b])

    def reduce(keep, send, steps, axis, last):
        for i, b in enumerate(steps):
            got = swap(send, b)
            if i == len(steps) - 1:
                return (keep.astype(f32) + got.astype(f32)).astype(last)
            ax = axis[steps[i + 1]]
            part = lambda v, at: lax.slice_in_dim(v, at, at + 1, axis=ax).astype(f32)
            send, keep = (
                (part(keep, 1) + part(got, 1)).astype(bf16),
                (part(keep, 0) + part(got, 0)).astype(bf16),
            )

    def scatter(keep, send, order):
        rows, cols = keep.shape[0] * 2 // n, keep.shape[1]
        shape = (1,) + (2,) * (k - 1) + (rows, cols)
        a = reduce(keep.reshape(shape), send.reshape(shape), tuple(reversed(order)), axis_of, f32)
        return a.reshape(rows, cols)

    def on_device(tokens, seq_ids, positions, cotangent, attn_gain, w_query, w_key, w_value, w_output,
                  mlp_gain, w_gate, w_up, w_down):
        toks, d = tokens.shape
        rows = d // n
        ff = w_gate.shape[1]
        share = 2 ** len(LOW)
        fc = ff // share // PARTS
        half = d // 2
        me = lax.axis_index("dp")

        def places_of(bits):
            slot = np.arange(d) // rows
            return sum(((slot >> (k - 1 - i)) & 1) * b for i, b in enumerate(bits)), np.arange(d) % rows

        places = jnp.asarray(np.stack([*places_of(axis_bits), *places_of(ff_bits), np.full(d, rows)]), jnp.int32)
        me1 = me[None]
        odd = {b: (me & b) != 0 for b in LOW}

        def pick(b, x, y):
            return jnp.where(odd[b], y, x), jnp.where(odd[b], x, y)

        shards = [((rows, 2 * d + 128), bf16), ((rows, 2 * d), bf16)] + [((rows, 2 * ff * 3 // share), bf16)] * 2
        part_qk, part_vo, keep, send = call(
            pack_kernel, shards, me1, attn_gain[None, :], mlp_gain[None, :], w_query, w_key, w_value, w_output.T,
            w_gate, w_up, w_down.T, grant=3 * VMEM)
        lead = lambda v: v.reshape((1,) * k + v.shape)
        a = jnp.concatenate(pick(LOW[0], lead(keep), lead(swap(send, LOW[0]))), axis=ff_axis[LOW[0]])
        mine = ff * 3 // share
        got = swap(a[..., mine:], LOW[1])
        a = jnp.concatenate(pick(LOW[1], a[..., :mine], got), axis=ff_axis[LOW[1]])
        qk = gather(part_qk, first)
        vo = gather(part_vo, second)
        wff = []
        for c in range(PARTS):
            w = a[..., c * 3 * fc : (c + 1) * 3 * fc]
            for b in ff_orders[c]:
                got = swap(w, b)
                w = jnp.concatenate([w, got], axis=ff_axis[b])
            wff.append(w.reshape(d, 3 * fc))
        freq = jnp.exp(jnp.arange(HD // 2, dtype=f32) * (-2.0 * math.log(THETA) / HD))
        angles = positions.astype(f32)[:, None] * freq[None, :]
        cosine, sine = jnp.cos(angles), jnp.sin(angles)
        cos2 = jnp.concatenate([cosine] * 4, axis=1)
        sin2 = jnp.concatenate([-sine, sine, -sine, sine], axis=1)
        seq_row, seq_col = seq_ids[None, :], seq_ids[:, None]
        act, mat, wide = ((toks, d), bf16), ((d, toks), bf16), ((toks, d), f32)

        def group_gather(v):
            for b in LOW:
                got = swap(v, b)
                v = jnp.concatenate([v, got], axis=0)
            return v

        def group_halve(keep, send):
            g1 = swap(send, LOW[1])
            v = (keep[toks:].astype(f32) + g1[toks:].astype(f32)).astype(bf16)
            return keep, g1, swap(v, LOW[0])

        live = (seq_col >= 0).astype(f32)
        square = ((d, d), bf16)
        xp, gb, gbg, own_sel, group_sel, change = call(
            prep_kernel, [act, act, act, square, square, square], me1, tokens, cotangent, places, live)
        gb4 = group_gather(gbg)
        n1t, qr, kr, vb, ob, gains, _ = call(
            attn_kernel, [mat, act, act, act, act, ((8, d), f32), act],
            xp, *qk, *vo, cos2, sin2, seq_row, seq_col)
        hmid, n2g = call(mid_kernel, [wide, act], xp, ob, *vo, gains, change)
        n24 = group_gather(n2g)
        tg = share * toks
        hidden = PARTS * fc
        pairs = [((tg // 2, d), bf16)] * 2
        acts, both, keep, send = call(
            ff_kernel, [((tg, hidden), bf16), ((tg, 2 * hidden), bf16)] + pairs, n24, gb4, *wff,
            scratch_shapes=[pltpu.VMEM((tg, d), f32)])
        dn2 = group_halve(keep, send)
        grads = call(
            ff_grad_kernel, [((half, 3 * fc), bf16)] * (2 * PARTS), n24, gb4, acts, both,
            scratch_shapes=[pltpu.VMEM((d, tg), bf16)] * 2)
        y = group_halve(*call(ff_out_kernel, pairs, acts, *wff))
        parts = []
        for c in range(PARTS):
            steps = tuple(reversed(ff_orders[c]))
            shape = tuple(1 if b == steps[0] else 2 for b in ff_bits) + (rows, 3 * fc)
            parts.append(reduce(*(v.reshape(shape) for v in grads[2 * c : 2 * c + 2]), steps, ff_axis, bf16))
        a = jnp.concatenate(parts, axis=-1).reshape(2, 2, rows, mine)
        pair1 = pick(LOW[1], a[0], a[1])
        got1 = swap(pair1[1], LOW[1])
        kept, sent = zip(*(pick(LOW[0], v[0], v[1]) for v in (pair1[0], got1)))
        got2 = swap(jnp.stack(sent), LOW[0])
        d_gate, d_up, d_down = call(
            unpack_kernel, [((rows, ff), f32)] * 3, me1, *kept, got2[0], got2[1])
        dh, dob, keep, send, dgain2 = call(
            back_kernel, [wide, act, ((half, d), bf16), ((half, d), bf16), ((8, d), f32)],
            *dn2, hmid, gb, gains, *vo, ob, change)
        d_wo = scatter(keep, send, second)
        dq, dk, dv, keep, send = call(
            attn_back_kernel, [act, act, act, ((half, 2 * d), bf16), ((half, 2 * d), bf16)],
            qr, kr, vb, dob, n1t, cos2, sin2, seq_row, seq_col)
        d_vq = scatter(keep, send, first)
        dtok, keep, send = call(
            last_kernel, [act, ((half, d + 128), bf16), ((half, d + 128), bf16)],
            dq, dk, dv, *qk, *vo, n1t, xp, dh, gains, dgain2, own_sel)
        d_kg = scatter(keep, send, second)
        (out,) = call(out_kernel, [act], *y, hmid, own_sel, group_sel)
        return (out, dtok, d_kg[:, d], d_vq[:, d:], d_kg[:, :d], d_vq[:, :d], d_wo.T, d_kg[:, d + 1],
                d_gate, d_up, d_down.T)

    return on_device


def solution(mesh):
    rows, cols, vec = P("dp", None), P(None, "dp"), P("dp")
    in_specs = (rows, vec, vec, rows, vec, rows, rows, rows, cols, vec, rows, rows, cols)
    out_specs = (rows, rows, vec, rows, rows, rows, cols, vec, rows, rows, cols)
    n = mesh.shape["dp"]
    return jax.shard_map(make_on_device(n), mesh=mesh, in_specs=in_specs, out_specs=out_specs, check_vma=False)
```

profile of v0, /device:TPU:0, one launch (start us, length us, event | category | flops | bytes accessed | tf_op | source)
XLA Modules:
  0.0 223.7 jit_solution(2296931484991575521)
XLA Ops:
  2.6 4.1 %collective-permute-start.5 = (bf16[1,1,1,1,1,24,1536]{6,5,4,3,2,1,0:T(8,128)(2,1)}, bf16[1,1,1,1,1,24,1536]{6,5,4,3,2,1,0:T(8,128)(2,1)S(1)}, u32[]{:S(2)}, u32[]{:S(2)}) collective-permute-start(bf16[1,1,1,1,1,24,1536]{6,5,4,3,2,1,0:T(8,128)(2,1)} %bitcast.81), channel_id=1, source_target_pairs={{0,16},{1,17},{2,18},{3,19},{4,20},{5,21},{6,22},{7,23},{8,24},{9,... | collective-permute-start | bytes 221192 | tf_op jit(solution)/shard_map/ppermute | solution.py:318
  21.1 4.2 %collective-permute-done.6 = bf16[1,1,1,1,2,24,1536]{6,5,4,3,2,1,0:T(8,128)(2,1)S(1)} collective-permute-done((bf16[1,1,1,1,2,24,1536]{6,5,4,3,2,1,0:T(8,128)(2,1)S(1)}, bf16[1,1,1,1,2,24,1536]{6,5,4,3,2,1,0:T(8,128)(2,1)S(1)}, u32[]{:S(2)}, u32[]{:S(2)}) %collective-permute-start.6) | collective-permute-done | bytes 147488 | tf_op jit(solution)/shard_map/ppermute | solution.py:318
  28.7 6.1 %collective-permute-done.2 = bf16[1,1,1,2,2,24,1664]{6,5,4,3,2,1,0:T(8,128)(2,1)S(1)} collective-permute-done((bf16[1,1,1,2,2,24,1664]{6,5,4,3,2,1,0:T(8,128)(2,1)S(1)}, bf16[1,1,1,2,2,24,1664]{6,5,4,3,2,1,0:T(8,128)(2,1)S(1)}, u32[]{:S(2)}, u32[]{:S(2)}) %collective-permute-start.2) | collective-permute-done | bytes 319520 | tf_op jit(solution)/shard_map/ppermute | solution.py:318
  38.5 2.6 %collective-permute-start.16 = (bf16[1,1,1,2,2,24,1152]{6,5,4,3,2,1,0:T(8,128)(2,1)S(1)}, bf16[1,1,1,2,2,24,1152]{6,5,4,3,2,1,0:T(8,128)(2,1)S(1)}, u32[]{:S(2)}, u32[]{:S(2)}) collective-permute-start(bf16[1,1,1,2,2,24,1152]{6,5,4,3,2,1,0:T(8,128)(2,1)S(1)} %get-tuple-element.124), channel_id=1, source_target_pairs={{0,16},{1,17},{2,18},{3,19},{4,20},{5,21},{6,22},{7,23},{8,24},{9,... | collective-permute-start | bytes 663560 | tf_op jit(solution)/shard_map/ppermute | solution.py:318
  41.0 12.3 %collective-permute-done.19 = bf16[1,1,1,2,2,24,1152]{6,5,4,3,2,1,0:T(8,128)(2,1)S(1)} collective-permute-done((bf16[1,1,1,2,2,24,1152]{6,5,4,3,2,1,0:T(8,128)(2,1)S(1)}, bf16[1,1,1,2,2,24,1152]{6,5,4,3,2,1,0:T(8,128)(2,1)S(1)}, u32[]{:S(2)}, u32[]{:S(2)}) %collective-permute-start.19) | collective-permute-done | bytes 221216 | tf_op jit(solution)/shard_map/ppermute | solution.py:318
  62.5 11.1 %collective-permute-done.20 = bf16[2,1,1,2,2,24,1152]{6,5,4,3,2,1,0:T(8,128)(2,1)} collective-permute-done((bf16[2,1,1,2,2,24,1152]{6,5,4,3,2,1,0:T(8,128)(2,1)}, bf16[2,1,1,2,2,24,1152]{6,5,4,3,2,1,0:T(8,128)(2,1)}, u32[]{:S(2)}, u32[]{:S(2)}) %collective-permute-start.20) | collective-permute-done | bytes 442400 | tf_op jit(solution)/shard_map/ppermute | solution.py:318
  76.2 5.1 %collective-permute-done.17 = bf16[1,1,2,2,2,24,1152]{6,5,4,3,2,1,0:T(8,128)(2,1)} collective-permute-done((bf16[1,1,2,2,2,24,1152]{6,5,4,3,2,1,0:T(8,128)(2,1)}, bf16[1,1,2,2,2,24,1152]{6,5,4,3,2,1,0:T(8,128)(2,1)}, u32[]{:S(2)}, u32[]{:S(2)}) %collective-permute-start.17) | collective-permute-done | bytes 442400 | tf_op jit(solution)/shard_map/ppermute | solution.py:318
  83.2 5.6 %shard_map.223 = (bf16[768,192]{1,0:T(8,128)(2,1)S(1)}, bf16[192,768]{1,0:T(8,128)(2,1)S(1)}, bf16[192,768]{1,0:T(8,128)(2,1)S(1)}, bf16[192,768]{1,0:T(8,128)(2...) custom-call(bf16[192,768]{1,0:T(8,128)(2,1)S(1)} %copy-done.3, ...), custom_call_target="tpu_custom_call" | custom-call | tf_op jit(solution)/shard_map/pallas_call | solution.py:45
  93.6 4.3 %collective-permute-done.10 = bf16[192,768]{1,0:T(8,128)(2,1)S(1)} collective-permute-done((bf16[192,768]{1,0:T(8,128)(2,1)S(1)}, bf16[192,768]{1,0:T(8,128)(2,1)S(1)}, u32[]{:S(2)}, u32[]{:S(2)}) %collective-permute-start.10) | collective-permute-done | bytes 294944 | tf_op jit(solution)/shard_map/ppermute | solution.py:318
  104.1 7.2 %shard_map.225 = (bf16[768,768]{1,0:T(8,128)(2,1)S(1)}, bf16[768,1536]{1,0:T(8,128)(2,1)S(1)}, bf16[384,768]{1,0:T(8,128)(2,1)S(1)}, bf16[384,768]{1,0:T(8,128)(2,1)S(1)}) custom-call(bf16[768,768]{1,0:T(8,128)(2,1)S(1)} %constant_dynamic-update-slice_fusion.n2, bf16[768,768]{1,0:T(8,128)(2,1)S(1)} %constant_dynamic-update-slice_fusion.3.gb, ...), custom_call_target="tpu_custom_call" | custom-call | tf_op jit(solution)/shard_map/pallas_call | solution.py:45
  111.4 3.3 %shard_map.231 = (bf16[384,1152]{1,0:T(8,128)(2,1)S(1)}, bf16[384,1152]{1,0:T(8,128)(2,1)S(1)}, bf16[384,1152]{1,0:T(8,128)(2,1)S(1)}, bf16[384,1152]{1,0:T(8,128)(2,1)S(1)}) custom-call(bf16[768,768]{1,0:T(8,128)(2,1)S(1)} %constant_dynamic-update-slice_fusion.n2, bf16[768,768]{1,0:T(8,128)(2,1)S(1)} %constant_dynamic-update-slice_fusion.3.gb, ...), custom_call_target="tpu_custom_call" | custom-call | tf_op jit(solution)/shard_map/pallas_call | solution.py:45
  120.8 6.6 %collective-permute-done.25.g2 = bf16[192,768]{1,0:T(8,128)(2,1)S(1)} collective-permute-done((bf16[192,768]{1,0:T(8,128)(2,1)S(1)}, bf16[192,768]{1,0:T(8,128)(2,1)S(1)}, u32[]{:S(2)}, u32[]{:S(2)}) %collective-permute-start.25) | collective-permute-done | bytes 294944 | tf_op jit(solution)/shard_map/ppermute | solution.py:318
  129.7 7.1 %collective-permute-done.41 = bf16[1,2,2,2,2,24,1152]{6,5,4,3,2,1,0:T(8,128)(2,1)S(1)} collective-permute-done((bf16[1,2,2,2,2,24,1152]{6,5,4,3,2,1,0:T(8,128)(2,1)S(1)}, bf16[1,2,2,2,2,24,1152]{6,5,4,3,2,1,0:T(8,128)(2,1)S(1)}, u32[]{:S(2)}, u32[]{:S(2)}) %collective-permute-start.41) | collective-permute-done | bytes 884768 | tf_op jit(solution)/shard_map/ppermute | solution.py:318
  140.8 7.3 %shard_map.229 = (bf16[192,768]{1,0:T(8,128)(2,1)S(1)}, bf16[192,768]{1,0:T(8,128)(2,1)S(1)}, bf16[192,768]{1,0:T(8,128)(2,1)S(1)}, bf16[384,1536]{1,0:T(8,128)(2,1)S(1)}, bf16[384,1536]{1,0:T(8,128)(2,1)S(1)}) custom-call(bf16[192,768]{1,0:T(8,128)(2,1)S(1)} %get-tuple-element.71.qr, bf16[192,768]{1,0:T(8,128)(2,1)S(1)} %get-tuple-element.72.kr, ...), custom_call_target="tpu_custom_call" | custom-call | tf_op jit(solution)/shard_map/pallas_call | solution.py:45
  148.1 4.6 %shard_map.230 = (bf16[192,768]{1,0:T(8,128)(2,1)}, bf16[384,896]{1,0:T(8,128)(2,1)S(1)}, bf16[384,896]{1,0:T(8,128)(2,1)S(1)}) custom-call(bf16[192,768]{1,0:T(8,128)(2,1)S(1)} %get-tuple-element.79.dq, bf16[192,768]{1,0:T(8,128)(2,1)S(1)} %get-tuple-element.80.dk, bf16[192,768]{1,0:T(8,128)(2,1)S(1)} %get-tuple-element.81.dv, ...), custom_call_target="tpu_custom_call" | custom-call | tf_op jit(solution)/shard_map/pallas_call | solution.py:45
  153.2 2.4 %shard_map.227 = bf16[192,768]{1,0:T(8,128)(2,1)} custom-call(bf16[384,768]{1,0:T(8,128)(2,1)S(1)} %get-tuple-element.66.k1, bf16[384,768]{1,0:T(8,128)(2,1)S(1)} %collective-permute-done.22.g1, bf16[192,768]{1,0:T(8,128)(2,1)S(1)} %collective-permute-done.23.g2, f32[192,768]{1,0:T(8,128)S(1)} %get-tuple-element.68.hmid, ...), custom_call_target="tpu_custom_call" | custom-call | tf_op jit(solution)/shard_map/pallas_call | solution.py:45
  157.5 10.2 %collective-permute-done.45 = bf16[2,1,1,2,2,24,1152]{6,5,4,3,2,1,0:T(8,128)(2,1)S(1)} collective-permute-done((bf16[2,1,1,2,2,24,1152]{6,5,4,3,2,1,0:T(8,128)(2,1)S(1)}, bf16[2,1,1,2,2,24,1152]{6,5,4,3,2,1,0:T(8,128)(2,1)S(1)}, u32[]{:S(2)}, u32[]{:S(2)}) %collective-permute-start.45) | collective-permute-done | bytes 442400 | tf_op jit(solution)/shard_map/ppermute | solution.py:318
  171.1 2.7 %collective-permute-done.46 = bf16[1,1,1,2,2,24,1152]{6,5,4,3,2,1,0:T(8,128)(2,1)S(1)} collective-permute-done((bf16[1,1,1,2,2,24,1152]{6,5,4,3,2,1,0:T(8,128)(2,1)S(1)}, bf16[1,1,1,2,2,24,1152]{6,5,4,3,2,1,0:T(8,128)(2,1)S(1)}, u32[]{:S(2)}, u32[]{:S(2)}) %collective-permute-start.46) | collective-permute-done | bytes 221216 | tf_op jit(solution)/shard_map/ppermute | solution.py:318
  179.1 3.3 %collective-permute-done.38 = bf16[1,1,1,2,2,24,768]{6,5,4,3,2,1,0:T(8,128)(2,1)S(1)} collective-permute-done((bf16[1,1,1,2,2,24,768]{6,5,4,3,2,1,0:T(8,128)(2,1)S(1)}, bf16[1,1,1,2,2,24,768]{6,5,4,3,2,1,0:T(8,128)(2,1)S(1)}, u32[]{:S(2)}, u32[]{:S(2)}) %collective-permute-start.38) | collective-permute-done | bytes 147488 | tf_op jit(solution)/shard_map/ppermute | solution.py:318
  182.5 2.7 %collective-permute-done.27 = bf16[1,2,1,2,2,24,896]{6,5,4,3,2,1,0:T(8,128)(2,1)S(1)} collective-permute-done((bf16[1,2,1,2,2,24,896]{6,5,4,3,2,1,0:T(8,128)(2,1)S(1)}, bf16[1,2,1,2,2,24,896]{6,5,4,3,2,1,0:T(8,128)(2,1)S(1)}, u32[]{:S(2)}, u32[]{:S(2)}) %collective-permute-start.27) | collective-permute-done | bytes 344096 | tf_op jit(solution)/shard_map/ppermute | solution.py:318
  192.8 11.2 %collective-permute-done.32 = bf16[1,1,2,2,2,24,1536]{6,5,4,3,2,1,0:T(8,128)(2,1)S(1)} collective-permute-done((bf16[1,1,2,2,2,24,1536]{6,5,4,3,2,1,0:T(8,128)(2,1)S(1)}, bf16[1,1,2,2,2,24,1536]{6,5,4,3,2,1,0:T(8,128)(2,1)S(1)}, u32[]{:S(2)}, u32[]{:S(2)}) %collective-permute-start.32) | collective-permute-done | bytes 589856 | tf_op jit(solution)/shard_map/ppermute | solution.py:318
  206.4 5.5 %collective-permute-done.33 = bf16[1,1,1,2,2,24,1536]{6,5,4,3,2,1,0:T(8,128)(2,1)S(1)} collective-permute-done((bf16[1,1,1,2,2,24,1536]{6,5,4,3,2,1,0:T(8,128)(2,1)S(1)}, bf16[1,1,1,2,2,24,1536]{6,5,4,3,2,1,0:T(8,128)(2,1)S(1)}, u32[]{:S(2)}, u32[]{:S(2)}) %collective-permute-start.33) | collective-permute-done | bytes 294944 | tf_op jit(solution)/shard_map/ppermute | solution.py:318
  212.7 4.5 %collective-permute-done.34 = bf16[1,1,1,1,2,24,1536]{6,5,4,3,2,1,0:T(8,128)(2,1)S(1)} collective-permute-done((bf16[1,1,1,1,2,24,1536]{6,5,4,3,2,1,0:T(8,128)(2,1)S(1)}, bf16[1,1,1,1,2,24,1536]{6,5,4,3,2,1,0:T(8,128)(2,1)S(1)}, u32[]{:S(2)}, u32[]{:S(2)}) %collective-permute-start.34) | collective-permute-done | bytes 147488 | tf_op jit(solution)/shard_map/ppermute | solution.py:318
  218.0 5.0 %collective-permute-done.35 = bf16[1,1,1,1,1,24,1536]{6,5,4,3,2,1,0:T(8,128)(2,1)S(1)} collective-permute-done((bf16[1,1,1,1,1,24,1536]{6,5,4,3,2,1,0:T(8,128)(2,1)S(1)}, bf16[1,1,1,1,1,24,1536]{6,5,4,3,2,1,0:T(8,128)(2,1)S(1)}, u32[]{:S(2)}, u32[]{:S(2)}) %collective-permute-start.35) | collective-permute-done | bytes 73760 | tf_op jit(solution)/shard_map/ppermute | solution.py:318
  (206 shorter events, 83.4 us)
Async XLA Ops:
  2.6 15.2 %collective-permute-start.5 = (bf16[1,1,1,1,1,24,1536]{6,5,4,3,2,1,0:T(8,128)(2,1)}, bf16[1,1,1,1,1,24,1536]{6,5,4,3,2,1,0:T(8,128)(2,1)S(1)}, u32[]{:S(2)}, u32[]{:S(2)}) collective-permute-start(bf16[1,1,1,1,1,24,1536]{6,5,4,3,2,1,0:T(8,128)(2,1)} %bitcast.81), channel_id=1, source_target_pairs={{0,16},{1,17},{2,18},{3,19},{4,20},{5,21},{6,22},{7,23},{8,24},{9,... | collective-permute-start | bytes 221192 | tf_op jit(solution)/shard_map/ppermute | solution.py:318
  17.6 57.4 %collective-permute-start.12 = (bf16[192,768]{1,0:T(8,128)(2,1)}, bf16[192,768]{1,0:T(8,128)(2,1)}, u32[]{:S(2)}, u32[]{:S(2)}) collective-permute-start(bf16[192,768]{1,0:T(8,128)(2,1)} %get-tuple-element.62), channel_id=1, source_target_pairs={{0,2},{1,3},{2,0},{3,1},{4,6},{5,7},{6,4},{7,5},{8,10},{9,11},{10,... | collective-permute-start | bytes 884744 | tf_op jit(solution)/shard_map/ppermute | solution.py:318
  34.9 21.3 %collective-permute-start.3 = (bf16[1,1,2,2,2,24,1664]{6,5,4,3,2,1,0:T(8,128)(2,1)S(1)}, bf16[1,1,2,2,2,24,1664]{6,5,4,3,2,1,0:T(8,128)(2,1)S(1)}, u32[]{:S(2)}, u32[]{:S(2)}) collective-permute-start(bf16[1,1,2,2,2,24,1664]{6,5,4,3,2,1,0:T(8,128)(2,1)S(1)} %pad_maximum_fusion.6), channel_id=1, source_target_pairs={{0,4},{1,5},{2,6},{3,7},{4,0},{5,1},{6,2},{7,3},{8,12},{9,13},{10,... | collective-permute-start | bytes 1916936 | tf_op jit(solution)/shard_map/ppermute | solution.py:318
  36.3 17.1 %collective-permute-start.19 = (bf16[1,1,1,2,2,24,1152]{6,5,4,3,2,1,0:T(8,128)(2,1)S(1)}, bf16[1,1,1,2,2,24,1152]{6,5,4,3,2,1,0:T(8,128)(2,1)S(1)}, u32[]{:S(2)}, u32[]{:S(2)}) collective-permute-start(bf16[1,1,1,2,2,24,1152]{6,5,4,3,2,1,0:T(8,128)(2,1)S(1)} %get-tuple-element.123), channel_id=1, source_target_pairs={{0,4},{1,5},{2,6},{3,7},{4,0},{5,1},{6,2},{7,3},{8,12},{9,13},{10,... | collective-permute-start | bytes 663560 | tf_op jit(solution)/shard_map/ppermute | solution.py:318
  37.2 20.2 %collective-permute-start.8 = (bf16[1,2,1,2,2,24,1536]{6,5,4,3,2,1,0:T(8,128)(2,1)S(1)}, bf16[1,2,1,2,2,24,1536]{6,5,4,3,2,1,0:T(8,128)(2,1)S(1)}, u32[]{:S(2)}, u32[]{:S(2)}) collective-permute-start(bf16[1,2,1,2,2,24,1536]{6,5,4,3,2,1,0:T(8,128)(2,1)S(1)} %pad_maximum_fusion.7), channel_id=1, source_target_pairs={{0,2},{1,3},{2,0},{3,1},{4,6},{5,7},{6,4},{7,5},{8,10},{9,11},{10,... | collective-permute-start | bytes 1769480 | tf_op jit(solution)/shard_map/ppermute | solution.py:318
  38.5 19.7 %collective-permute-start.16 = (bf16[1,1,1,2,2,24,1152]{6,5,4,3,2,1,0:T(8,128)(2,1)S(1)}, bf16[1,1,1,2,2,24,1152]{6,5,4,3,2,1,0:T(8,128)(2,1)S(1)}, u32[]{:S(2)}, u32[]{:S(2)}) collective-permute-start(bf16[1,1,1,2,2,24,1152]{6,5,4,3,2,1,0:T(8,128)(2,1)S(1)} %get-tuple-element.124), channel_id=1, source_target_pairs={{0,16},{1,17},{2,18},{3,19},{4,20},{5,21},{6,22},{7,23},{8,24},{9,... | collective-permute-start | bytes 663560 | tf_op jit(solution)/shard_map/ppermute | solution.py:318
  54.2 19.4 %collective-permute-start.20 = (bf16[2,1,1,2,2,24,1152]{6,5,4,3,2,1,0:T(8,128)(2,1)}, bf16[2,1,1,2,2,24,1152]{6,5,4,3,2,1,0:T(8,128)(2,1)}, u32[]{:S(2)}, u32[]{:S(2)}) collective-permute-start(bf16[2,1,1,2,2,24,1152]{6,5,4,3,2,1,0:T(8,128)(2,1)} %pad_maximum_fusion.11), channel_id=1, source_target_pairs={{0,16},{1,17},{2,18},{3,19},{4,20},{5,21},{6,22},{7,23},{8,24},{9,... | collective-permute-start | bytes 1327112 | tf_op jit(solution)/shard_map/ppermute | solution.py:318
  57.4 25.8 %collective-permute-start.4 = (bf16[1,2,2,2,2,24,1664]{6,5,4,3,2,1,0:T(8,128)(2,1)}, bf16[1,2,2,2,2,24,1664]{6,5,4,3,2,1,0:T(8,128)(2,1)}, u32[]{:S(2)}, u32[]{:S(2)}) collective-permute-start(bf16[1,2,2,2,2,24,1664]{6,5,4,3,2,1,0:T(8,128)(2,1)} %pad_maximum_fusion.2), channel_id=1, source_target_pairs={{0,1},{1,0},{2,3},{3,2},{4,5},{5,4},{6,7},{7,6},{8,9},{9,8},{10,11... | collective-permute-start | bytes 3833864 | tf_op jit(solution)/shard_map/ppermute | solution.py:318
  57.5 25.6 %collective-permute-start.9 = (bf16[1,2,2,2,2,24,1536]{6,5,4,3,2,1,0:T(8,128)(2,1)S(1)}, bf16[1,2,2,2,2,24,1536]{6,5,4,3,2,1,0:T(8,128)(2,1)S(1)}, u32[]{:S(2)}, u32[]{:S(2)}) collective-permute-start(bf16[1,2,2,2,2,24,1536]{6,5,4,3,2,1,0:T(8,128)(2,1)S(1)} %pad_maximum_fusion.3), channel_id=1, source_target_pairs={{0,1},{1,0},{2,3},{3,2},{4,5},{5,4},{6,7},{7,6},{8,9},{9,8},{10,11... | collective-permute-start | bytes 3538952 | tf_op jit(solution)/shard_map/ppermute | solution.py:318
  59.0 22.3 %collective-permute-start.17 = (bf16[1,1,2,2,2,24,1152]{6,5,4,3,2,1,0:T(8,128)(2,1)}, bf16[1,1,2,2,2,24,1152]{6,5,4,3,2,1,0:T(8,128)(2,1)}, u32[]{:S(2)}, u32[]{:S(2)}) collective-permute-start(bf16[1,1,2,2,2,24,1152]{6,5,4,3,2,1,0:T(8,128)(2,1)} %pad_maximum_fusion.10), channel_id=1, source_target_pairs={{0,8},{1,9},{2,10},{3,11},{4,12},{5,13},{6,14},{7,15},{8,0},{9,1},... | collective-permute-start | bytes 1327112 | tf_op jit(solution)/shard_map/ppermute | solution.py:318
  74.9 24.5 %collective-permute-start.21 = (bf16[2,1,2,2,2,24,1152]{6,5,4,3,2,1,0:T(8,128)(2,1)S(1)}, bf16[2,1,2,2,2,24,1152]{6,5,4,3,2,1,0:T(8,128)(2,1)S(1)}, u32[]{:S(2)}, u32[]{:S(2)}) collective-permute-start(bf16[2,1,2,2,2,24,1152]{6,5,4,3,2,1,0:T(8,128)(2,1)S(1)} %pad_maximum_fusion.5), channel_id=1, source_target_pairs={{0,8},{1,9},{2,10},{3,11},{4,12},{5,13},{6,14},{7,15},{8,0},{9,1},... | collective-permute-start | bytes 2654216 | tf_op jit(solution)/shard_map/ppermute | solution.py:318
  76.1 17.4 %collective-permute-start.13 = (bf16[384,768]{1,0:T(8,128)(2,1)S(1)}, bf16[384,768]{1,0:T(8,128)(2,1)S(1)}, u32[]{:S(2)}, u32[]{:S(2)}) collective-permute-start(bf16[384,768]{1,0:T(8,128)(2,1)S(1)} %pad_maximum_fusion.9), channel_id=1, source_target_pairs={{0,1},{1,0},{2,3},{3,2},{4,5},{5,4},{6,7},{7,6},{8,9},{9,8},{10,11... | collective-permute-start | bytes 1769480 | tf_op jit(solution)/shard_map/ppermute | solution.py:318
  82.4 20.3 %collective-permute-start.18 = (bf16[1,2,2,2,2,24,1152]{6,5,4,3,2,1,0:T(8,128)(2,1)S(1)}, bf16[1,2,2,2,2,24,1152]{6,5,4,3,2,1,0:T(8,128)(2,1)S(1)}, u32[]{:S(2)}, u32[]{:S(2)}) collective-permute-start(bf16[1,2,2,2,2,24,1152]{6,5,4,3,2,1,0:T(8,128)(2,1)S(1)} %pad_maximum_fusion.4), channel_id=1, source_target_pairs={{0,4},{1,5},{2,6},{3,7},{4,0},{5,1},{6,2},{7,3},{8,12},{9,13},{10,... | collective-permute-start | bytes 2654216 | tf_op jit(solution)/shard_map/ppermute | solution.py:318
  114.7 22.1 %collective-permute-start.41 = (bf16[1,2,2,2,2,24,1152]{6,5,4,3,2,1,0:T(8,128)(2,1)S(1)}, bf16[1,2,2,2,2,24,1152]{6,5,4,3,2,1,0:T(8,128)(2,1)S(1)}, u32[]{:S(2)}, u32[]{:S(2)}) collective-permute-start(bf16[1,2,2,2,2,24,1152]{6,5,4,3,2,1,0:T(8,128)(2,1)S(1)} %bitcast.73), channel_id=1, source_target_pairs={{0,4},{1,5},{2,6},{3,7},{4,0},{5,1},{6,2},{7,3},{8,12},{9,13},{10,... | collective-permute-start | bytes 2654216 | tf_op jit(solution)/shard_map/ppermute | solution.py:318
  117.4 21.8 %collective-permute-start.44 = (bf16[2,1,2,2,2,24,1152]{6,5,4,3,2,1,0:T(8,128)(2,1)S(1)}, bf16[2,1,2,2,2,24,1152]{6,5,4,3,2,1,0:T(8,128)(2,1)S(1)}, u32[]{:S(2)}, u32[]{:S(2)}) collective-permute-start(bf16[2,1,2,2,2,24,1152]{6,5,4,3,2,1,0:T(8,128)(2,1)S(1)} %bitcast.72), channel_id=1, source_target_pairs={{0,8},{1,9},{2,10},{3,11},{4,12},{5,13},{6,14},{7,15},{8,0},{9,1},... | collective-permute-start | bytes 2654216 | tf_op jit(solution)/shard_map/ppermute | solution.py:318
  119.3 33.4 %collective-permute-start.23 = (bf16[192,768]{1,0:T(8,128)(2,1)S(1)}, bf16[192,768]{1,0:T(8,128)(2,1)S(1)}, u32[]{:S(2)}, u32[]{:S(2)}) collective-permute-start(bf16[192,768]{1,0:T(8,128)(2,1)S(1)} %add_convert_fusion.13), channel_id=1, source_target_pairs={{0,2},{1,3},{2,0},{3,1},{4,6},{5,7},{6,4},{7,5},{8,10},{9,11},{10,... | collective-permute-start | bytes 884744 | tf_op jit(solution)/shard_map/ppermute | solution.py:318
  129.6 39.3 %collective-permute-start.36 = (bf16[1,2,2,2,2,24,768]{6,5,4,3,2,1,0:T(8,128)(2,1)S(1)}, bf16[1,2,2,2,2,24,768]{6,5,4,3,2,1,0:T(8,128)(2,1)S(1)}, u32[]{:S(2)}, u32[]{:S(2)}) collective-permute-start(bf16[1,2,2,2,2,24,768]{6,5,4,3,2,1,0:T(8,128)(2,1)S(1)} %bitcast.75), channel_id=1, source_target_pairs={{0,1},{1,0},{2,3},{3,2},{4,5},{5,4},{6,7},{7,6},{8,9},{9,8},{10,11... | collective-permute-start | bytes 1769480 | tf_op jit(solution)/shard_map/ppermute | solution.py:318
  137.0 18.6 %collective-permute-start.42 = (bf16[1,1,2,2,2,24,1152]{6,5,4,3,2,1,0:T(8,128)(2,1)S(1)}, bf16[1,1,2,2,2,24,1152]{6,5,4,3,2,1,0:T(8,128)(2,1)S(1)}, u32[]{:S(2)}, u32[]{:S(2)}) collective-permute-start(bf16[1,1,2,2,2,24,1152]{6,5,4,3,2,1,0:T(8,128)(2,1)S(1)} %get-tuple-element.104), channel_id=1, source_target_pairs={{0,8},{1,9},{2,10},{3,11},{4,12},{5,13},{6,14},{7,15},{8,0},{9,1},... | collective-permute-start | bytes 1327112 | tf_op jit(solution)/shard_map/ppermute | solution.py:318
  139.5 28.2 %collective-permute-start.45 = (bf16[2,1,1,2,2,24,1152]{6,5,4,3,2,1,0:T(8,128)(2,1)S(1)}, bf16[2,1,1,2,2,24,1152]{6,5,4,3,2,1,0:T(8,128)(2,1)S(1)}, u32[]{:S(2)}, u32[]{:S(2)}) collective-permute-start(bf16[2,1,1,2,2,24,1152]{6,5,4,3,2,1,0:T(8,128)(2,1)S(1)} %get-tuple-element.106), channel_id=1, source_target_pairs={{0,16},{1,17},{2,18},{3,19},{4,20},{5,21},{6,22},{7,23},{8,24},{9,... | collective-permute-start | bytes 1327112 | tf_op jit(solution)/shard_map/ppermute | solution.py:318
  152.7 21.4 %collective-permute-start.26 = (bf16[1,2,2,2,2,24,896]{6,5,4,3,2,1,0:T(8,128)(2,1)S(1)}, bf16[1,2,2,2,2,24,896]{6,5,4,3,2,1,0:T(8,128)(2,1)S(1)}, u32[]{:S(2)}, u32[]{:S(2)}) collective-permute-start(bf16[1,2,2,2,2,24,896]{6,5,4,3,2,1,0:T(8,128)(2,1)S(1)} %bitcast.74), channel_id=1, source_target_pairs={{0,1},{1,0},{2,3},{3,2},{4,5},{5,4},{6,7},{7,6},{8,9},{9,8},{10,11... | collective-permute-start | bytes 2064392 | tf_op jit(solution)/shard_map/ppermute | solution.py:318
  152.7 34.8 %collective-permute-start.31 = (bf16[1,2,2,2,2,24,1536]{6,5,4,3,2,1,0:T(8,128)(2,1)S(1)}, bf16[1,2,2,2,2,24,1536]{6,5,4,3,2,1,0:T(8,128)(2,1)S(1)}, u32[]{:S(2)}, u32[]{:S(2)}) collective-permute-start(bf16[1,2,2,2,2,24,1536]{6,5,4,3,2,1,0:T(8,128)(2,1)S(1)} %bitcast.71), channel_id=1, source_target_pairs={{0,1},{1,0},{2,3},{3,2},{4,5},{5,4},{6,7},{7,6},{8,9},{9,8},{10,11... | collective-permute-start | bytes 3538952 | tf_op jit(solution)/shard_map/ppermute | solution.py:318
  155.7 15.3 %collective-permute-start.43 = (bf16[1,1,1,2,2,24,1152]{6,5,4,3,2,1,0:T(8,128)(2,1)S(1)}, bf16[1,1,1,2,2,24,1152]{6,5,4,3,2,1,0:T(8,128)(2,1)S(1)}, u32[]{:S(2)}, u32[]{:S(2)}) collective-permute-start(bf16[1,1,1,2,2,24,1152]{6,5,4,3,2,1,0:T(8,128)(2,1)S(1)} %add_convert_fusion.18), channel_id=1, source_target_pairs={{0,16},{1,17},{2,18},{3,19},{4,20},{5,21},{6,22},{7,23},{8,24},{9,... | collective-permute-start | bytes 663560 | tf_op jit(solution)/shard_map/ppermute | solution.py:318
  186.9 18.8 %collective-permute-start.40 = (bf16[1,1,1,1,1,24,768]{6,5,4,3,2,1,0:T(8,128)(2,1)S(1)}, bf16[1,1,1,1,1,24,768]{6,5,4,3,2,1,0:T(8,128)(2,1)S(1)}, u32[]{:S(2)}, u32[]{:S(2)}) collective-permute-start(bf16[1,1,1,1,1,24,768]{6,5,4,3,2,1,0:T(8,128)(2,1)S(1)} %add_convert_fusion.34), channel_id=1, source_target_pairs={{0,16},{1,17},{2,18},{3,19},{4,20},{5,21},{6,22},{7,23},{8,24},{9,... | collective-permute-start | bytes 110600 | tf_op jit(solution)/shard_map/ppermute | solution.py:318
  187.8 16.1 %collective-permute-start.32 = (bf16[1,1,2,2,2,24,1536]{6,5,4,3,2,1,0:T(8,128)(2,1)S(1)}, bf16[1,1,2,2,2,24,1536]{6,5,4,3,2,1,0:T(8,128)(2,1)S(1)}, u32[]{:S(2)}, u32[]{:S(2)}) collective-permute-start(bf16[1,1,2,2,2,24,1536]{6,5,4,3,2,1,0:T(8,128)(2,1)S(1)} %get-tuple-element.102), channel_id=1, source_target_pairs={{0,4},{1,5},{2,6},{3,7},{4,0},{5,1},{6,2},{7,3},{8,12},{9,13},{10,... | collective-permute-start | bytes 1769480 | tf_op jit(solution)/shard_map/ppermute | solution.py:318
  (53 other events, 403.9 us)
where the time goes:
time: 224 us
  waiting for transfers between devices  112 us (50%)
  starting transfers between devices  43.2 us (19%)
  Pallas kernels  40.1 us (18%)
  other arithmetic  15.3 us (7%)
  local copies, waits for them, and re-layouts  11.2 us (5%)
    ppermute x49, waiting for transfers between devices, swap(): return lax.ppermute(a, 'dp', [(i, i ^ b) for i in range(n)])  112 us
    ppermute x49, starting transfers between devices, swap(): return lax.ppermute(a, 'dp', [(i, i ^ b) for i in range(n)])  43.2 us
    pallas_call x12, Pallas kernels, call(): pl.pallas_call(kernel, out_shape=out_shape, in_specs=[smem if v.size == 1...  40.1 us
    unnamed x60, local copies, waits for them, and re-layouts  8.24 us
    concatenate x6, other arithmetic, on_device(): w = jnp.concatenate([w, got], axis=ff_axis[b])  6.56 us
  transfers between devices with their start and end apart: 49, of which 25 were waited for; matrix products, arithmetic and copies ran while one was open for 9% of the time, Pallas kernels for 14%

commit v1 on v0

--- a/solution.py
+++ b/solution.py
@@ -38,14 +38,15 @@
     return lax.dot_general(a, b, (((1,), (1,)), ((), ())), preferred_element_type=f32)
 
 
-def call(kernel, outs, *args, grant=VMEM, **kw):
+def call(kernel, outs, *args, fetch=True, grant=VMEM, **kw):
     out_shape = [jax.ShapeDtypeStruct(s, d) for s, d in outs]
     vmem = pl.BlockSpec(memory_space=pltpu.VMEM)
     smem = pl.BlockSpec(memory_space=pltpu.SMEM)
+    hbm = pl.BlockSpec(memory_space=pltpu.HBM)
     return pl.pallas_call(
         kernel,
         out_shape=out_shape,
-        in_specs=[smem if v.size == 1 else vmem for v in args],
+        in_specs=[smem if v.size == 1 else vmem if fetch else hbm for v in args],
         out_specs=[vmem] * len(outs),
         compiler_params=pltpu.CompilerParams(vmem_limit_bytes=grant),
         **kw,
@@ -66,12 +67,20 @@
     return jnp.concatenate([nt(v, p[:, cols]) for p in parts], axis=1)
 
 
-def allowed_of(seq_row_ref, seq_col_ref):
-    row, col = seq_row_ref[...], seq_col_ref[...]
+def column_of(row):
     t = row.shape[1]
     i = lax.broadcasted_iota(jnp.int32, (t, t), 0)
     j = lax.broadcasted_iota(jnp.int32, (t, t), 1)
-    return ((col == row) & (col >= 0) & (j <= i)) | (i == j)
+    return jnp.sum(jnp.where(i == j, row.astype(f32), 0.0), axis=1, keepdims=True)
+
+
+def allowed_of(seq_ref):
+    row = seq_ref[...].astype(f32)
+    col = column_of(row)
+    t = row.shape[1]
+    i = lax.broadcasted_iota(jnp.int32, (t, t), 0)
+    j = lax.broadcasted_iota(jnp.int32, (t, t), 1)
+    return ((col == row) & (col >= 0.0) & (j <= i)) | (i == j)
 
 
 def swap_halves(v):
@@ -80,31 +89,34 @@
     return jnp.where(first, pltpu.roll(v, 2 * HD - HD // 2, 1), pltpu.roll(v, HD // 2, 1))
 
 
-def pack_kernel(me, attn_gain, mlp_gain, wq, wk, wv, wo, wgate, wup, wdown, qk, vo, keep, send):
+def pack_kernel(me, attn_gain, mlp_gain, wq, wk, wv, wo, wgate, wup, wdown, qk, vo, keep, send, gain1, gain2, sems):
     rows, d = wq.shape
-    qk[:, :d] = wq[...]
-    qk[:, d : 2 * d] = wk[...]
-    spot = lax.broadcasted_iota(jnp.int32, (rows, rows), 0) == lax.broadcasted_iota(jnp.int32, (rows, rows), 1)
-    column = lambda ref: jnp.sum(jnp.where(spot, ref[...].astype(f32), 0.0), axis=1, keepdims=True)
-    lane = lax.broadcasted_iota(jnp.int32, (rows, 128), 1)
-    both = jnp.where(lane == 0, column(attn_gain), jnp.where(lane == 1, column(mlp_gain), 0.0))
-    qk[:, 2 * d :] = both.astype(bf16)
-    vo[:, :d] = wv[...]
-    vo[:, d:] = wo[...]
     low = me[0] % (2 * LOW[0])
     hidden = wgate.shape[1] // 4
     fc = hidden // PARTS
+    moves = [(attn_gain, gain1), (mlp_gain, gain2), (wq, qk.at[:, :d]), (wk, qk.at[:, d : 2 * d]),
+             (wv, vo.at[:, :d]), (wo, vo.at[:, d:])]
     for ref, flip in ((keep, 0), (send, LOW[0])):
         for i, other in enumerate((0, LOW[1])):
             base = (low ^ (flip + other)) * hidden
             for c in range(PARTS):
                 for m, w in enumerate((wgate, wup, wdown)):
                     at = i * 3 * hidden + (c * 3 + m) * fc
-                    ref[:, at : at + fc] = w[:, pl.ds(pl.multiple_of(base + c * fc, 128), fc)]
+                    moves.append((w.at[:, pl.ds(pl.multiple_of(base + c * fc, 128), fc)], ref.at[:, at : at + fc]))
+    copies = [pltpu.make_async_copy(src, dst, sems.at[i]) for i, (src, dst) in enumerate(moves)]
+    for copy in copies:
+        copy.start()
+    for copy in copies[:2]:
+        copy.wait()
+    lane = lax.broadcasted_iota(jnp.int32, (rows, 128), 1)
+    both = jnp.where(lane == 0, column_of(gain1[...]), jnp.where(lane == 1, column_of(gain2[...]), 0.0))
+    qk[:, 2 * d :] = both.astype(bf16)
+    for copy in copies[2:]:
+        copy.wait()
 
 
 def unpack_kernel(me, *refs):
-    parts, outs = refs[:4], refs[4:]
+    parts, outs = [ref.at[i] for ref in refs[:2] for i in range(2)], refs[2:]
     low = me[0] % (2 * LOW[0])
     hidden = outs[0].shape[1] // 4
     fc = hidden // PARTS
@@ -116,7 +128,7 @@
                 out[:, pl.ds(pl.multiple_of(base + c * fc, 128), fc)] = ref[:, at : at + fc].astype(f32)
 
 
-def prep_kernel(me, tokens, cot, places, live, xp, gb, gbg, own_sel, group_sel, change):
+def prep_kernel(me, tokens, cot, places, seq, cosine, sine, xp, gb, gbg, own_sel, group_sel, change, cos, sin):
     d = tokens.shape[1]
     rows = places[4, 0]
     share = 2 * LOW[0]
@@ -128,11 +140,48 @@
     own_col = jnp.broadcast_to(own.astype(f32), (128, d)).T[:, 0:1]
     change[...] = (own_col == group.astype(f32)).astype(bf16)
     xp[...] = nn(tokens[...], own_sel[...]).astype(bf16)
-    gb[...] = (nn(cot[...], own_sel[...]) * live[...]).astype(bf16)
-    gbg[...] = (nn(cot[...], group_sel[...]) * live[...]).astype(bf16)
-
-
-def attn_kernel(xp, qk0, qk1, vo0, vo1, cos, sin, seq_row, seq_col, n1t, qr, kr, vb, ob, gains, n1):
+    live = (column_of(seq[...]) >= 0.0).astype(f32)
+    gb[...] = (nn(cot[...], own_sel[...]) * live).astype(bf16)
+    gbg[...] = (nn(cot[...], group_sel[...]) * live).astype(bf16)
+    c, z = cosine[...], sine[...]
+    cos[...] = jnp.concatenate([c, c, c, c], axis=1)
+    sin[...] = jnp.concatenate([-z, z, -z, z], axis=1)
+
+
+def fold_kernel(me, kept, got, keep, send):
+    b = (me[0] // LOW[0]) % 2
+    half = keep.shape[2]
+    for at, ref in ((b, kept), (1 - b, got)):
+        keep[pl.ds(at, 1)] = ref[:, :half][None]
+        send[pl.ds(at, 1)] = ref[:, half:][None]
+
+
+def fold2_kernel(me, kept, got, *parts):
+    b = me[0] % 2
+    cols = parts[0].shape[3]
+    for c, out in enumerate(parts):
+        for at, ref in ((b, kept), (1 - b, got)):
+            out[pl.ds(at, 1)] = ref[:, :, c * cols : (c + 1) * cols][None]
+
+
+def unfold_kernel(me, *refs):
+    terms, (keep, send) = refs[:-2], refs[-2:]
+    b = me[0] % 2
+    cols = terms[0].shape[3]
+    for c in range(PARTS):
+        for at, ref in ((b, keep), (1 - b, send)):
+            total = sum(v[pl.ds(at, 1)].astype(f32) for v in terms[2 * c : 2 * c + 2])
+            ref[:, :, c * cols : (c + 1) * cols] = total[0].astype(bf16)
+
+
+def unfold2_kernel(me, kept, got, keep, send):
+    b = (me[0] // LOW[0]) % 2
+    for i, ref in enumerate((kept, got)):
+        keep[i : i + 1] = ref[pl.ds(b, 1)]
+        send[i : i + 1] = ref[pl.ds(1 - b, 1)]
+
+
+def attn_kernel(xp, qk0, qk1, vo0, vo1, cos, sin, seq_row, n1t, qr, kr, vb, ob, gains, n1):
     d = xp.shape[1]
     qk, vo = (qk0, qk1), (vo0, vo1)
     gt = jnp.concatenate([p[:, 2 * d :] for p in qk], axis=0).astype(f32).T
@@ -142,7 +191,7 @@
     normed = x * r1 * gt[0:1]
     n1[...] = normed.astype(bf16)
     n1t[...] = normed.T.astype(bf16)
-    allowed = allowed_of(seq_row, seq_col)
+    allowed = allowed_of(seq_row)
     pair = 2 * HD
     low = lax.broadcasted_iota(jnp.int32, (x.shape[0], pair), 1) < HD
     scale = HD ** -0.5
@@ -178,8 +227,12 @@
     n2g[...] = nn((h * r2 * gains[1:2]).astype(bf16), change[...]).astype(bf16)
 
 
-def ff_kernel(n2, gb, *refs):
-    ws, (act, both, keep, send, acc) = refs[:PARTS], refs[PARTS:]
+def ff_kernel(*refs):
+    pieces, ws, (act, both, keep, send, n2, gb, acc) = refs[:8], refs[8 : 8 + PARTS], refs[8 + PARTS :]
+    rows = pieces[0].shape[0]
+    for i in range(4):
+        n2[i * rows : (i + 1) * rows] = pieces[i][...]
+        gb[i * rows : (i + 1) * rows] = pieces[4 + i][...]
     half = n2.shape[0] // 2
     for c, w in enumerate(ws):
         fc = w.shape[1] // 3
@@ -198,10 +251,13 @@
     send[...] = acc[half:].astype(bf16)
 
 
-def ff_grad_kernel(n2, gb, act, both, *refs):
-    n2t, gbt = refs[-2:]
-    n2t[...] = n2[...].astype(f32).T.astype(bf16)
-    gbt[...] = gb[...].astype(f32).T.astype(bf16)
+def ff_grad_kernel(*refs):
+    pieces, act, both, (n2t, gbt) = refs[:8], refs[8], refs[9], refs[-2:]
+    rows = pieces[0].shape[0]
+    for i in range(4):
+        n2t[:, i * rows : (i + 1) * rows] = pieces[i][...].astype(f32).T.astype(bf16)
+        gbt[:, i * rows : (i + 1) * rows] = pieces[4 + i][...].astype(f32).T.astype(bf16)
+    refs = refs[10:-2]
     for c in range(PARTS):
         keep, send = refs[2 * c : 2 * c + 2]
         fc = keep.shape[1] // 3
@@ -242,11 +298,11 @@
     send[...] = dw[half:]
 
 
-def attn_back_kernel(qr, kr, vb, dob, n1t, cos, sin, seq_row, seq_col, dq, dk, dv, keep, send):
+def attn_back_kernel(qr, kr, vb, dob, n1t, cos, sin, seq_row, dq, dk, dv, keep, send):
     t, d = qr.shape
     half = d // 2
     pair = 2 * HD
-    allowed = allowed_of(seq_row, seq_col)
+    allowed = allowed_of(seq_row)
     low = lax.broadcasted_iota(jnp.int32, (t, pair), 1) < HD
     scale = HD ** -0.5
     for b in range(d // pair):
@@ -329,7 +385,7 @@
         for i, b in enumerate(steps):
             got = swap(send, b)
             if i == len(steps) - 1:
-                return (keep.astype(f32) + got.astype(f32)).astype(last)
+                return (keep.astype(f32) + got.astype(f32)).astype(last) if last else (keep, got)
             ax = axis[steps[i + 1]]
             part = lambda v, at: lax.slice_in_dim(v, at, at + 1, axis=ax).astype(f32)
             send, keep = (
@@ -359,25 +415,20 @@
 
         places = jnp.asarray(np.stack([*places_of(axis_bits), *places_of(ff_bits), np.full(d, rows)]), jnp.int32)
         me1 = me[None]
-        odd = {b: (me & b) != 0 for b in LOW}
-
-        def pick(b, x, y):
-            return jnp.where(odd[b], y, x), jnp.where(odd[b], x, y)
-
         shards = [((rows, 2 * d + 128), bf16), ((rows, 2 * d), bf16)] + [((rows, 2 * ff * 3 // share), bf16)] * 2
         part_qk, part_vo, keep, send = call(
             pack_kernel, shards, me1, attn_gain[None, :], mlp_gain[None, :], w_query, w_key, w_value, w_output.T,
-            w_gate, w_up, w_down.T, grant=3 * VMEM)
-        lead = lambda v: v.reshape((1,) * k + v.shape)
-        a = jnp.concatenate(pick(LOW[0], lead(keep), lead(swap(send, LOW[0]))), axis=ff_axis[LOW[0]])
+            w_gate, w_up, w_down.T, fetch=False, grant=3 * VMEM,
+            scratch_shapes=[pltpu.VMEM((1, rows), bf16)] * 2 + [pltpu.SemaphoreType.DMA((6 + 12 * PARTS,))])
         mine = ff * 3 // share
-        got = swap(a[..., mine:], LOW[1])
-        a = jnp.concatenate(pick(LOW[1], a[..., :mine], got), axis=ff_axis[LOW[1]])
+        block = ((2, rows, mine), bf16)
+        keep, send = call(fold_kernel, [block] * 2, me1, keep, swap(send, LOW[0]))
+        ws = call(fold2_kernel, [((2, 2, rows, 3 * fc), bf16)] * PARTS, me1, keep, swap(send, LOW[1]))
         qk = gather(part_qk, first)
         vo = gather(part_vo, second)
         wff = []
         for c in range(PARTS):
-            w = a[..., c * 3 * fc : (c + 1) * 3 * fc]
+            w = ws[c].reshape((1,) * len(high) + (2, 2, rows, 3 * fc))
             for b in ff_orders[c]:
                 got = swap(w, b)
                 w = jnp.concatenate([w, got], axis=ff_axis[b])
@@ -385,70 +436,65 @@
         freq = jnp.exp(jnp.arange(HD // 2, dtype=f32) * (-2.0 * math.log(THETA) / HD))
         angles = positions.astype(f32)[:, None] * freq[None, :]
         cosine, sine = jnp.cos(angles), jnp.sin(angles)
-        cos2 = jnp.concatenate([cosine] * 4, axis=1)
-        sin2 = jnp.concatenate([-sine, sine, -sine, sine], axis=1)
-        seq_row, seq_col = seq_ids[None, :], seq_ids[:, None]
+        seq_row = seq_ids[None, :]
         act, mat, wide = ((toks, d), bf16), ((d, toks), bf16), ((toks, d), f32)
 
         def group_gather(v):
-            for b in LOW:
-                got = swap(v, b)
-                v = jnp.concatenate([v, got], axis=0)
-            return v
+            far = swap(v, LOW[0])
+            near = swap(v, LOW[1])
+            return v, far, near, swap(far, LOW[1])
 
         def group_halve(keep, send):
             g1 = swap(send, LOW[1])
             v = (keep[toks:].astype(f32) + g1[toks:].astype(f32)).astype(bf16)
             return keep, g1, swap(v, LOW[0])
 
-        live = (seq_col >= 0).astype(f32)
-        square = ((d, d), bf16)
-        xp, gb, gbg, own_sel, group_sel, change = call(
-            prep_kernel, [act, act, act, square, square, square], me1, tokens, cotangent, places, live)
+        square, table = ((d, d), bf16), ((toks, 2 * HD), f32)
+        xp, gb, gbg, own_sel, group_sel, change, cos2, sin2 = call(
+            prep_kernel, [act] * 3 + [square] * 3 + [table] * 2, me1, tokens, cotangent, places, seq_row, cosine, sine)
         gb4 = group_gather(gbg)
         n1t, qr, kr, vb, ob, gains, _ = call(
             attn_kernel, [mat, act, act, act, act, ((8, d), f32), act],
-            xp, *qk, *vo, cos2, sin2, seq_row, seq_col)
+            xp, *qk, *vo, cos2, sin2, seq_row)
         hmid, n2g = call(mid_kernel, [wide, act], xp, ob, *vo, gains, change)
         n24 = group_gather(n2g)
         tg = share * toks
         hidden = PARTS * fc
         pairs = [((tg // 2, d), bf16)] * 2
         acts, both, keep, send = call(
-            ff_kernel, [((tg, hidden), bf16), ((tg, 2 * hidden), bf16)] + pairs, n24, gb4, *wff,
-            scratch_shapes=[pltpu.VMEM((tg, d), f32)])
+            ff_kernel, [((tg, hidden), bf16), ((tg, 2 * hidden), bf16)] + pairs, *n24, *gb4, *wff,
+            scratch_shapes=[pltpu.VMEM((tg, d), bf16)] * 2 + [pltpu.VMEM((tg, d), f32)])
         dn2 = group_halve(keep, send)
         grads = call(
-            ff_grad_kernel, [((half, 3 * fc), bf16)] * (2 * PARTS), n24, gb4, acts, both,
+            ff_grad_kernel, [((half, 3 * fc), bf16)] * (2 * PARTS), *n24, *gb4, acts, both,
             scratch_shapes=[pltpu.VMEM((d, tg), bf16)] * 2)
         y = group_halve(*call(ff_out_kernel, pairs, acts, *wff))
         parts = []
         for c in range(PARTS):
             steps = tuple(reversed(ff_orders[c]))
             shape = tuple(1 if b == steps[0] else 2 for b in ff_bits) + (rows, 3 * fc)
-            parts.append(reduce(*(v.reshape(shape) for v in grads[2 * c : 2 * c + 2]), steps, ff_axis, bf16))
-        a = jnp.concatenate(parts, axis=-1).reshape(2, 2, rows, mine)
-        pair1 = pick(LOW[1], a[0], a[1])
-        got1 = swap(pair1[1], LOW[1])
-        kept, sent = zip(*(pick(LOW[0], v[0], v[1]) for v in (pair1[0], got1)))
-        got2 = swap(jnp.stack(sent), LOW[0])
+            parts.append(reduce(*(v.reshape(shape) for v in grads[2 * c : 2 * c + 2]), steps, ff_axis, None))
+        terms = [v.reshape(2, 2, rows, 3 * fc) for pair in parts for v in pair]
+        keep, send = call(unfold_kernel, [block] * 2, me1, *terms)
+        keep, send = call(unfold2_kernel, [block] * 2, me1, keep, swap(send, LOW[1]))
+        got = swap(send, LOW[0])
         d_gate, d_up, d_down = call(
-            unpack_kernel, [((rows, ff), f32)] * 3, me1, *kept, got2[0], got2[1])
+            unpack_kernel, [((rows, ff), f32)] * 3, me1, keep, got)
         dh, dob, keep, send, dgain2 = call(
             back_kernel, [wide, act, ((half, d), bf16), ((half, d), bf16), ((8, d), f32)],
             *dn2, hmid, gb, gains, *vo, ob, change)
         d_wo = scatter(keep, send, second)
         dq, dk, dv, keep, send = call(
             attn_back_kernel, [act, act, act, ((half, 2 * d), bf16), ((half, 2 * d), bf16)],
-            qr, kr, vb, dob, n1t, cos2, sin2, seq_row, seq_col)
+            qr, kr, vb, dob, n1t, cos2, sin2, seq_row)
         d_vq = scatter(keep, send, first)
         dtok, keep, send = call(
             last_kernel, [act, ((half, d + 128), bf16), ((half, d + 128), bf16)],
             dq, dk, dv, *qk, *vo, n1t, xp, dh, gains, dgain2, own_sel)
         d_kg = scatter(keep, send, second)
         (out,) = call(out_kernel, [act], *y, hmid, own_sel, group_sel)
-        return (out, dtok, d_kg[:, d], d_vq[:, d:], d_kg[:, :d], d_vq[:, :d], d_wo.T, d_kg[:, d + 1],
-                d_gate, d_up, d_down.T)
+        ends = (d_kg[:, d], d_vq[:, d:], d_kg[:, :d], d_vq[:, :d], d_wo.T, d_kg[:, d + 1])
+        return (out, dtok, *ends, d_gate, d_up, d_down.T)
 
     return on_device
 

time: 224 us -> 206 us (0.920)
  starting transfers between devices: 43.2 us -> 56.2 us
  local copies, waits for them, and re-layouts: 11.2 us -> 2.05 us
  waiting for transfers between devices: 112 us -> 103 us
  other arithmetic: 15.3 us -> 7.05 us
  Pallas kernels: 40.1 us -> 36.3 us
    ppermute x49 -> x51, starting transfers between devices: 43.2 us -> 56.2 us  [swap(): return lax.ppermute(a, 'dp', [(i, i ^ b) for i in range(n)])]
    ppermute x49 -> x51, waiting for transfers between devices: 112 us -> 103 us  [swap(): return lax.ppermute(a, 'dp', [(i, i ^ b) for i in range(n)])]
    unnamed x60 -> x16, local copies, waits for them, and re-layouts: 8.24 us -> 0.05 us
    concatenate x6, other arithmetic: 6.56 us -> 0.76 us  [on_device(): w = jnp.concatenate([w, got], axis=ff_axis[b])]
    pallas_call x12 -> x16, Pallas kernels: 40.1 us -> 36.3 us  [call(): pl.pallas_call(kernel, out_shape=out_shape, in_specs=[smem if v.size == 1...]
  transfers between devices with their start and end apart: 49 -> 51, of which waited for: 25 -> 24; matrix products, arithmetic and copies ran while one was open for 9% -> 4% of each run, Pallas kernels for 14% -> 13%
where the time goes in v1:
time: 206 us
  waiting for transfers between devices  103 us (50%)
  starting transfers between devices  56.2 us (27%)
  Pallas kernels  36.3 us (18%)
  other arithmetic  7.05 us (3%)
    ppermute x51, waiting for transfers between devices, swap(): return lax.ppermute(a, 'dp', [(i, i ^ b) for i in range(n)])  103 us
    ppermute x51, starting transfers between devices, swap(): return lax.ppermute(a, 'dp', [(i, i ^ b) for i in range(n)])  56.2 us
    pallas_call x16, Pallas kernels, call(): pl.pallas_call(kernel, out_shape=out_shape, in_specs=[smem if v.size == 1...  36.3 us
  transfers between devices with their start and end apart: 51, of which 24 were waited for; matrix products, arithmetic and copies ran while one was open for 4% of the time, Pallas kernels for 13%

profile of v1, /device:TPU:0, one launch (start us, length us, event | category | flops | bytes accessed | tf_op | source)
XLA Modules:
  0.0 206.1 jit_solution(4787740837472050996)
XLA Ops:
  2.8 4.1 %collective-permute-start = (bf16[1,1,1,1,1,24,1664]{6,5,4,3,2,1,0:T(8,128)(2,1)}, bf16[1,1,1,1,1,24,1664]{6,5,4,3,2,1,0:T(8,128)(2,1)S(1)}, u32[]{:S(2)}, u32[]{:S(2)}) collective-permute-start(bf16[1,1,1,1,1,24,1664]{6,5,4,3,2,1,0:T(8,128)(2,1)} %bitcast.80), channel_id=1, source_target_pairs={{0,16},{1,17},{2,18},{3,19},{4,20},{5,21},{6,22},{7,23},{8,24},{9,... | collective-permute-start | bytes 239624 | tf_op jit(solution)/shard_map/ppermute | solution.py:374
  8.7 3.7 %collective-permute-done = bf16[1,1,1,1,1,24,1664]{6,5,4,3,2,1,0:T(8,128)(2,1)S(1)} collective-permute-done((bf16[1,1,1,1,1,24,1664]{6,5,4,3,2,1,0:T(8,128)(2,1)}, bf16[1,1,1,1,1,24,1664]{6,5,4,3,2,1,0:T(8,128)(2,1)S(1)}, u32[]{:S(2)}, u32[]{:S(2)}) %collective-permute-start) | collective-permute-done | bytes 79904 | tf_op jit(solution)/shard_map/ppermute | solution.py:374
  16.4 3.5 %collective-permute-done.1 = bf16[1,1,1,1,2,24,1664]{6,5,4,3,2,1,0:T(8,128)(2,1)S(1)} collective-permute-done((bf16[1,1,1,1,2,24,1664]{6,5,4,3,2,1,0:T(8,128)(2,1)S(1)}, bf16[1,1,1,1,2,24,1664]{6,5,4,3,2,1,0:T(8,128)(2,1)S(1)}, u32[]{:S(2)}, u32[]{:S(2)}) %collective-permute-start.1) | collective-permute-done | bytes 159776 | tf_op jit(solution)/shard_map/ppermute | solution.py:374
  30.9 3.0 %collective-permute-done.7 = bf16[1,1,1,2,2,24,1536]{6,5,4,3,2,1,0:T(8,128)(2,1)S(1)} collective-permute-done((bf16[1,1,1,2,2,24,1536]{6,5,4,3,2,1,0:T(8,128)(2,1)S(1)}, bf16[1,1,1,2,2,24,1536]{6,5,4,3,2,1,0:T(8,128)(2,1)S(1)}, u32[]{:S(2)}, u32[]{:S(2)}) %collective-permute-start.7) | collective-permute-done | bytes 294944 | tf_op jit(solution)/shard_map/ppermute | solution.py:374
  34.4 4.2 %collective-permute-done.21 = bf16[1,1,1,2,2,24,1152]{6,5,4,3,2,1,0:T(8,128)(2,1)S(1)} collective-permute-done((bf16[1,1,1,2,2,24,1152]{6,5,4,3,2,1,0:T(8,128)(2,1)S(1)}, bf16[1,1,1,2,2,24,1152]{6,5,4,3,2,1,0:T(8,128)(2,1)S(1)}, u32[]{:S(2)}, u32[]{:S(2)}) %collective-permute-start.21) | collective-permute-done | bytes 221216 | tf_op jit(solution)/shard_map/ppermute | solution.py:374
  42.6 9.2 %collective-permute-done.3 = bf16[1,1,2,2,2,24,1664]{6,5,4,3,2,1,0:T(8,128)(2,1)S(1)} collective-permute-done((bf16[1,1,2,2,2,24,1664]{6,5,4,3,2,1,0:T(8,128)(2,1)S(1)}, bf16[1,1,2,2,2,24,1664]{6,5,4,3,2,1,0:T(8,128)(2,1)S(1)}, u32[]{:S(2)}, u32[]{:S(2)}) %collective-permute-start.3) | collective-permute-done | bytes 639008 | tf_op jit(solution)/shard_map/ppermute | solution.py:374
  52.7 7.7 %collective-permute-done.22 = bf16[2,1,1,2,2,24,1152]{6,5,4,3,2,1,0:T(8,128)(2,1)S(1)} collective-permute-done((bf16[2,1,1,2,2,24,1152]{6,5,4,3,2,1,0:T(8,128)(2,1)S(1)}, bf16[2,1,1,2,2,24,1152]{6,5,4,3,2,1,0:T(8,128)(2,1)S(1)}, u32[]{:S(2)}, u32[]{:S(2)}) %collective-permute-start.22) | collective-permute-done | bytes 442400 | tf_op jit(solution)/shard_map/ppermute | solution.py:374
  64.7 7.6 %collective-permute-done.13.refs_5_ = bf16[192,768]{1,0:T(8,128)(2,1)S(1)} collective-permute-done((bf16[192,768]{1,0:T(8,128)(2,1)S(1)}, bf16[192,768]{1,0:T(8,128)(2,1)S(1)}, u32[]{:S(2)}, u32[]{:S(2)}) %collective-permute-start.13) | collective-permute-done | bytes 294944 | tf_op jit(solution)/shard_map/ppermute | solution.py:374
  72.8 3.8 %shard_map.223 = (bf16[768,192]{1,0:T(8,128)(2,1)S(1)}, bf16[192,768]{1,0:T(8,128)(2,1)S(1)}, bf16[192,768]{1,0:T(8,128)(2,1)S(1)}, bf16[192,768]{1,0:T(8,128)(2...) custom-call(bf16[192,768]{1,0:T(8,128)(2,1)S(1)} %get-tuple-element.65.xp, ...), custom_call_target="tpu_custom_call" | custom-call | tf_op jit(solution)/shard_map/pallas_call | solution.py:46
  81.9 4.8 %collective-permute-done.10.refs_1_ = bf16[192,768]{1,0:T(8,128)(2,1)S(1)} collective-permute-done((bf16[192,768]{1,0:T(8,128)(2,1)S(1)}, bf16[192,768]{1,0:T(8,128)(2,1)S(1)}, u32[]{:S(2)}, u32[]{:S(2)}) %collective-permute-start.10) | collective-permute-done | bytes 294944 | tf_op jit(solution)/shard_map/ppermute | solution.py:374
  88.3 7.1 %shard_map.227 = (bf16[768,768]{1,0:T(8,128)(2,1)S(1)}, bf16[768,1536]{1,0:T(8,128)(2,1)S(1)}, bf16[384,768]{1,0:T(8,128)(2,1)S(1)}, bf16[384,768]{1,0:T(8,128)(2,1)S(1)}) custom-call(bf16[192,768]{1,0:T(8,128)(2,1)S(1)} %get-tuple-element.73.refs_0_, bf16[192,768]{1,0:T(8,128)(2,1)S(1)} %collective-permute-done.10.refs_1_, ...), custom_call_target="tpu_custom_call" | custom-call | tf_op jit(solution)/shard_map/pallas_call | solution.py:46
  95.6 3.6 %shard_map.233 = (bf16[384,1152]{1,0:T(8,128)(2,1)S(1)}, bf16[384,1152]{1,0:T(8,128)(2,1)S(1)}, bf16[384,1152]{1,0:T(8,128)(2,1)S(1)}, bf16[384,1152]{1,0:T(8,128)(2,1)S(1)}) custom-call(bf16[192,768]{1,0:T(8,128)(2,1)S(1)} %get-tuple-element.73.refs_0_, bf16[192,768]{1,0:T(8,128)(2,1)S(1)} %collective-permute-done.10.refs_1_, ...), custom_call_target="tpu_custom_call" | custom-call | tf_op jit(solution)/shard_map/pallas_call | solution.py:46
  105.3 7.7 %collective-permute-done.27.g2 = bf16[192,768]{1,0:T(8,128)(2,1)S(1)} collective-permute-done((bf16[192,768]{1,0:T(8,128)(2,1)S(1)}, bf16[192,768]{1,0:T(8,128)(2,1)S(1)}, u32[]{:S(2)}, u32[]{:S(2)}) %collective-permute-start.27) | collective-permute-done | bytes 294944 | tf_op jit(solution)/shard_map/ppermute | solution.py:374
  115.3 5.9 %collective-permute-done.43 = bf16[1,2,2,2,2,24,1152]{6,5,4,3,2,1,0:T(8,128)(2,1)S(1)} collective-permute-done((bf16[1,2,2,2,2,24,1152]{6,5,4,3,2,1,0:T(8,128)(2,1)S(1)}, bf16[1,2,2,2,2,24,1152]{6,5,4,3,2,1,0:T(8,128)(2,1)S(1)}, u32[]{:S(2)}, u32[]{:S(2)}) %collective-permute-start.43) | collective-permute-done | bytes 884768 | tf_op jit(solution)/shard_map/ppermute | solution.py:374
  123.6 3.4 %collective-permute-start.47 = (bf16[2,1,1,2,2,24,1152]{6,5,4,3,2,1,0:T(8,128)(2,1)S(1)}, bf16[2,1,1,2,2,24,1152]{6,5,4,3,2,1,0:T(8,128)(2,1)S(1)}, u32[]{:S(2)}, u32[]{:S(2)}) collective-permute-start(bf16[2,1,1,2,2,24,1152]{6,5,4,3,2,1,0:T(8,128)(2,1)S(1)} %get-tuple-element.124), channel_id=1, source_target_pairs={{0,16},{1,17},{2,18},{3,19},{4,20},{5,21},{6,22},{7,23},{8,24},{9,... | collective-permute-start | bytes 1327112 | tf_op jit(solution)/shard_map/ppermute | solution.py:374
  127.0 7.3 %shard_map.231 = (bf16[192,768]{1,0:T(8,128)(2,1)S(1)}, bf16[192,768]{1,0:T(8,128)(2,1)S(1)}, bf16[192,768]{1,0:T(8,128)(2,1)S(1)}, bf16[384,1536]{1,0:T(8,128)(2,1)S(1)}, bf16[384,1536]{1,0:T(8,128)(2,1)S(1)}) custom-call(bf16[192,768]{1,0:T(8,128)(2,1)S(1)} %get-tuple-element.87.qr, bf16[192,768]{1,0:T(8,128)(2,1)S(1)} %get-tuple-element.88.kr, ...), custom_call_target="tpu_custom_call" | custom-call | tf_op jit(solution)/shard_map/pallas_call | solution.py:46
  137.1 4.5 %collective-permute-done.44 = bf16[1,1,2,2,2,24,1152]{6,5,4,3,2,1,0:T(8,128)(2,1)S(1)} collective-permute-done((bf16[1,1,2,2,2,24,1152]{6,5,4,3,2,1,0:T(8,128)(2,1)S(1)}, bf16[1,1,2,2,2,24,1152]{6,5,4,3,2,1,0:T(8,128)(2,1)S(1)}, u32[]{:S(2)}, u32[]{:S(2)}) %collective-permute-start.44) | collective-permute-done | bytes 442400 | tf_op jit(solution)/shard_map/ppermute | solution.py:374
  142.0 10.1 %collective-permute-done.47 = bf16[2,1,1,2,2,24,1152]{6,5,4,3,2,1,0:T(8,128)(2,1)S(1)} collective-permute-done((bf16[2,1,1,2,2,24,1152]{6,5,4,3,2,1,0:T(8,128)(2,1)S(1)}, bf16[2,1,1,2,2,24,1152]{6,5,4,3,2,1,0:T(8,128)(2,1)S(1)}, u32[]{:S(2)}, u32[]{:S(2)}) %collective-permute-start.47) | collective-permute-done | bytes 442400 | tf_op jit(solution)/shard_map/ppermute | solution.py:374
  167.4 4.5 %collective-permute-done.29 = bf16[1,2,1,2,2,24,896]{6,5,4,3,2,1,0:T(8,128)(2,1)S(1)} collective-permute-done((bf16[1,2,1,2,2,24,896]{6,5,4,3,2,1,0:T(8,128)(2,1)S(1)}, bf16[1,2,1,2,2,24,896]{6,5,4,3,2,1,0:T(8,128)(2,1)S(1)}, u32[]{:S(2)}, u32[]{:S(2)}) %collective-permute-start.29) | collective-permute-done | bytes 344096 | tf_op jit(solution)/shard_map/ppermute | solution.py:374
  172.4 3.4 %collective-permute-done.50.refs_1_ = bf16[2,24,2304]{2,1,0:T(8,128)(2,1)S(1)} collective-permute-done((bf16[2,24,2304]{2,1,0:T(8,128)(2,1)S(1)}, bf16[2,24,2304]{2,1,0:T(8,128)(2,1)S(1)}, u32[]{:S(2)}, u32[]{:S(2)}) %collective-permute-start.50) | collective-permute-done | bytes 221216 | tf_op jit(solution)/shard_map/ppermute | solution.py:374
  176.8 7.4 %collective-permute-done.30 = bf16[1,1,1,2,2,24,896]{6,5,4,3,2,1,0:T(8,128)(2,1)S(1)} collective-permute-done((bf16[1,1,1,2,2,24,896]{6,5,4,3,2,1,0:T(8,128)(2,1)S(1)}, bf16[1,1,1,2,2,24,896]{6,5,4,3,2,1,0:T(8,128)(2,1)S(1)}, u32[]{:S(2)}, u32[]{:S(2)}) %collective-permute-start.30) | collective-permute-done | bytes 172064 | tf_op jit(solution)/shard_map/ppermute | solution.py:374
  188.8 3.1 %collective-permute-start.32 = (bf16[1,1,1,1,1,24,896]{6,5,4,3,2,1,0:T(8,128)(2,1)S(1)}, bf16[1,1,1,1,1,24,896]{6,5,4,3,2,1,0:T(8,128)(2,1)S(1)}, u32[]{:S(2)}, u32[]{:S(2)}) collective-permute-start(bf16[1,1,1,1,1,24,896]{6,5,4,3,2,1,0:T(8,128)(2,1)S(1)} %add_convert_fusion.30), channel_id=1, source_target_pairs={{0,16},{1,17},{2,18},{3,19},{4,20},{5,21},{6,22},{7,23},{8,24},{9,... | collective-permute-start | bytes 129032 | tf_op jit(solution)/shard_map/ppermute | solution.py:374
  195.0 3.8 %collective-permute-done.36 = bf16[1,1,1,1,2,24,1536]{6,5,4,3,2,1,0:T(8,128)(2,1)S(1)} collective-permute-done((bf16[1,1,1,1,2,24,1536]{6,5,4,3,2,1,0:T(8,128)(2,1)S(1)}, bf16[1,1,1,1,2,24,1536]{6,5,4,3,2,1,0:T(8,128)(2,1)S(1)}, u32[]{:S(2)}, u32[]{:S(2)}) %collective-permute-start.36) | collective-permute-done | bytes 147488 | tf_op jit(solution)/shard_map/ppermute | solution.py:374
  198.8 3.5 %collective-permute-start.37 = (bf16[1,1,1,1,1,24,1536]{6,5,4,3,2,1,0:T(8,128)(2,1)S(1)}, bf16[1,1,1,1,1,24,1536]{6,5,4,3,2,1,0:T(8,128)(2,1)S(1)}, u32[]{:S(2)}, u32[]{:S(2)}) collective-permute-start(bf16[1,1,1,1,1,24,1536]{6,5,4,3,2,1,0:T(8,128)(2,1)S(1)} %add_convert_fusion.28), channel_id=1, source_target_pairs={{0,16},{1,17},{2,18},{3,19},{4,20},{5,21},{6,22},{7,23},{8,24},{9,... | collective-permute-start | bytes 221192 | tf_op jit(solution)/shard_map/ppermute | solution.py:374
  (151 shorter events, 78.1 us)
Async XLA Ops:
  7.0 16.7 %collective-permute-start.16 = (bf16[24,4608]{1,0:T(8,128)(2,1)}, bf16[24,4608]{1,0:T(8,128)(2,1)S(1)}, u32[]{:S(2)}, u32[]{:S(2)}) collective-permute-start(bf16[24,4608]{1,0:T(8,128)(2,1)} %get-tuple-element.76), channel_id=1, source_target_pairs={{0,2},{1,3},{2,0},{3,1},{4,6},{5,7},{6,4},{7,5},{8,10},{9,11},{10,... | collective-permute-start | bytes 663560 | tf_op jit(solution)/shard_map/ppermute | solution.py:374
  26.9 13.5 %collective-permute-start.18 = (bf16[1,1,1,2,2,24,1152]{6,5,4,3,2,1,0:T(8,128)(2,1)S(1)}, bf16[1,1,1,2,2,24,1152]{6,5,4,3,2,1,0:T(8,128)(2,1)S(1)}, u32[]{:S(2)}, u32[]{:S(2)}) collective-permute-start(bf16[1,1,1,2,2,24,1152]{6,5,4,3,2,1,0:T(8,128)(2,1)S(1)} %bitcast.57), channel_id=1, source_target_pairs={{0,16},{1,17},{2,18},{3,19},{4,20},{5,21},{6,22},{7,23},{8,24},{9,... | collective-permute-start | bytes 663560 | tf_op jit(solution)/shard_map/ppermute | solution.py:374
  28.7 23.0 %collective-permute-start.3 = (bf16[1,1,2,2,2,24,1664]{6,5,4,3,2,1,0:T(8,128)(2,1)S(1)}, bf16[1,1,2,2,2,24,1664]{6,5,4,3,2,1,0:T(8,128)(2,1)S(1)}, u32[]{:S(2)}, u32[]{:S(2)}) collective-permute-start(bf16[1,1,2,2,2,24,1664]{6,5,4,3,2,1,0:T(8,128)(2,1)S(1)} %pad_maximum_fusion.6), channel_id=1, source_target_pairs={{0,4},{1,5},{2,6},{3,7},{4,0},{5,1},{6,2},{7,3},{8,12},{9,13},{10,... | collective-permute-start | bytes 1916936 | tf_op jit(solution)/shard_map/ppermute | solution.py:374
  33.9 18.1 %collective-permute-start.8 = (bf16[1,2,1,2,2,24,1536]{6,5,4,3,2,1,0:T(8,128)(2,1)S(1)}, bf16[1,2,1,2,2,24,1536]{6,5,4,3,2,1,0:T(8,128)(2,1)S(1)}, u32[]{:S(2)}, u32[]{:S(2)}) collective-permute-start(bf16[1,2,1,2,2,24,1536]{6,5,4,3,2,1,0:T(8,128)(2,1)S(1)} %pad_maximum_fusion.7), channel_id=1, source_target_pairs={{0,2},{1,3},{2,0},{3,1},{4,6},{5,7},{6,4},{7,5},{8,10},{9,11},{10,... | collective-permute-start | bytes 1769480 | tf_op jit(solution)/shard_map/ppermute | solution.py:374
  38.6 21.8 %collective-permute-start.22 = (bf16[2,1,1,2,2,24,1152]{6,5,4,3,2,1,0:T(8,128)(2,1)S(1)}, bf16[2,1,1,2,2,24,1152]{6,5,4,3,2,1,0:T(8,128)(2,1)S(1)}, u32[]{:S(2)}, u32[]{:S(2)}) collective-permute-start(bf16[2,1,1,2,2,24,1152]{6,5,4,3,2,1,0:T(8,128)(2,1)S(1)} %pad_maximum_fusion.9), channel_id=1, source_target_pairs={{0,16},{1,17},{2,18},{3,19},{4,20},{5,21},{6,22},{7,23},{8,24},{9,... | collective-permute-start | bytes 1327112 | tf_op jit(solution)/shard_map/ppermute | solution.py:374
  40.5 20.2 %collective-permute-start.19 = (bf16[1,1,2,2,2,24,1152]{6,5,4,3,2,1,0:T(8,128)(2,1)S(1)}, bf16[1,1,2,2,2,24,1152]{6,5,4,3,2,1,0:T(8,128)(2,1)S(1)}, u32[]{:S(2)}, u32[]{:S(2)}) collective-permute-start(bf16[1,1,2,2,2,24,1152]{6,5,4,3,2,1,0:T(8,128)(2,1)S(1)} %pad_maximum_fusion.8), channel_id=1, source_target_pairs={{0,8},{1,9},{2,10},{3,11},{4,12},{5,13},{6,14},{7,15},{8,0},{9,1},... | collective-permute-start | bytes 1327112 | tf_op jit(solution)/shard_map/ppermute | solution.py:374
  51.9 20.9 %collective-permute-start.4 = (bf16[1,2,2,2,2,24,1664]{6,5,4,3,2,1,0:T(8,128)(2,1)S(1)}, bf16[1,2,2,2,2,24,1664]{6,5,4,3,2,1,0:T(8,128)(2,1)S(1)}, u32[]{:S(2)}, u32[]{:S(2)}) collective-permute-start(bf16[1,2,2,2,2,24,1664]{6,5,4,3,2,1,0:T(8,128)(2,1)S(1)} %pad_maximum_fusion.2), channel_id=1, source_target_pairs={{0,1},{1,0},{2,3},{3,2},{4,5},{5,4},{6,7},{7,6},{8,9},{9,8},{10,11... | collective-permute-start | bytes 3833864 | tf_op jit(solution)/shard_map/ppermute | solution.py:374
  52.2 20.2 %collective-permute-start.9 = (bf16[1,2,2,2,2,24,1536]{6,5,4,3,2,1,0:T(8,128)(2,1)S(1)}, bf16[1,2,2,2,2,24,1536]{6,5,4,3,2,1,0:T(8,128)(2,1)S(1)}, u32[]{:S(2)}, u32[]{:S(2)}) collective-permute-start(bf16[1,2,2,2,2,24,1536]{6,5,4,3,2,1,0:T(8,128)(2,1)S(1)} %pad_maximum_fusion.3), channel_id=1, source_target_pairs={{0,1},{1,0},{2,3},{3,2},{4,5},{5,4},{6,7},{7,6},{8,9},{9,8},{10,11... | collective-permute-start | bytes 3538952 | tf_op jit(solution)/shard_map/ppermute | solution.py:374
  60.5 21.0 %collective-permute-start.23 = (bf16[2,1,2,2,2,24,1152]{6,5,4,3,2,1,0:T(8,128)(2,1)S(1)}, bf16[2,1,2,2,2,24,1152]{6,5,4,3,2,1,0:T(8,128)(2,1)S(1)}, u32[]{:S(2)}, u32[]{:S(2)}) collective-permute-start(bf16[2,1,2,2,2,24,1152]{6,5,4,3,2,1,0:T(8,128)(2,1)S(1)} %pad_maximum_fusion.5), channel_id=1, source_target_pairs={{0,8},{1,9},{2,10},{3,11},{4,12},{5,13},{6,14},{7,15},{8,0},{9,1},... | collective-permute-start | bytes 2654216 | tf_op jit(solution)/shard_map/ppermute | solution.py:374
  60.8 26.0 %collective-permute-start.20 = (bf16[1,2,2,2,2,24,1152]{6,5,4,3,2,1,0:T(8,128)(2,1)S(1)}, bf16[1,2,2,2,2,24,1152]{6,5,4,3,2,1,0:T(8,128)(2,1)S(1)}, u32[]{:S(2)}, u32[]{:S(2)}) collective-permute-start(bf16[1,2,2,2,2,24,1152]{6,5,4,3,2,1,0:T(8,128)(2,1)S(1)} %pad_maximum_fusion.4), channel_id=1, source_target_pairs={{0,4},{1,5},{2,6},{3,7},{4,0},{5,1},{6,2},{7,3},{8,12},{9,13},{10,... | collective-permute-start | bytes 2654216 | tf_op jit(solution)/shard_map/ppermute | solution.py:374
  72.3 14.7 %collective-permute-start.14 = (bf16[192,768]{1,0:T(8,128)(2,1)S(1)}, bf16[192,768]{1,0:T(8,128)(2,1)S(1)}, u32[]{:S(2)}, u32[]{:S(2)}) collective-permute-start(bf16[192,768]{1,0:T(8,128)(2,1)S(1)} %get-tuple-element.74.refs_4_), channel_id=1, source_target_pairs={{0,1},{1,0},{2,3},{3,2},{4,5},{5,4},{6,7},{7,6},{8,9},{9,8},{10,11... | collective-permute-start | bytes 884744 | tf_op jit(solution)/shard_map/ppermute | solution.py:374
  72.3 14.7 %collective-permute-start.15 = (bf16[192,768]{1,0:T(8,128)(2,1)S(1)}, bf16[192,768]{1,0:T(8,128)(2,1)S(1)}, u32[]{:S(2)}, u32[]{:S(2)}) collective-permute-start(bf16[192,768]{1,0:T(8,128)(2,1)S(1)} %collective-permute-done.13.refs_5_), channel_id=1, source_target_pairs={{0,1},{1,0},{2,3},{3,2},{4,5},{5,4},{6,7},{7,6},{8,9},{9,8},{10,11... | collective-permute-start | bytes 884744 | tf_op jit(solution)/shard_map/ppermute | solution.py:374
  99.2 22.0 %collective-permute-start.43 = (bf16[1,2,2,2,2,24,1152]{6,5,4,3,2,1,0:T(8,128)(2,1)S(1)}, bf16[1,2,2,2,2,24,1152]{6,5,4,3,2,1,0:T(8,128)(2,1)S(1)}, u32[]{:S(2)}, u32[]{:S(2)}) collective-permute-start(bf16[1,2,2,2,2,24,1152]{6,5,4,3,2,1,0:T(8,128)(2,1)S(1)} %bitcast.77), channel_id=1, source_target_pairs={{0,4},{1,5},{2,6},{3,7},{4,0},{5,1},{6,2},{7,3},{8,12},{9,13},{10,... | collective-permute-start | bytes 2654216 | tf_op jit(solution)/shard_map/ppermute | solution.py:374
  101.4 22.0 %collective-permute-start.46 = (bf16[2,1,2,2,2,24,1152]{6,5,4,3,2,1,0:T(8,128)(2,1)S(1)}, bf16[2,1,2,2,2,24,1152]{6,5,4,3,2,1,0:T(8,128)(2,1)S(1)}, u32[]{:S(2)}, u32[]{:S(2)}) collective-permute-start(bf16[2,1,2,2,2,24,1152]{6,5,4,3,2,1,0:T(8,128)(2,1)S(1)} %bitcast.76), channel_id=1, source_target_pairs={{0,8},{1,9},{2,10},{3,11},{4,12},{5,13},{6,14},{7,15},{8,0},{9,1},... | collective-permute-start | bytes 2654216 | tf_op jit(solution)/shard_map/ppermute | solution.py:374
  104.0 48.5 %collective-permute-start.25 = (bf16[192,768]{1,0:T(8,128)(2,1)S(1)}, bf16[192,768]{1,0:T(8,128)(2,1)S(1)}, u32[]{:S(2)}, u32[]{:S(2)}) collective-permute-start(bf16[192,768]{1,0:T(8,128)(2,1)S(1)} %add_convert_fusion.13), channel_id=1, source_target_pairs={{0,2},{1,3},{2,0},{3,1},{4,6},{5,7},{6,4},{7,5},{8,10},{9,11},{10,... | collective-permute-start | bytes 884744 | tf_op jit(solution)/shard_map/ppermute | solution.py:374
  115.2 26.5 %collective-permute-start.38 = (bf16[1,2,2,2,2,24,768]{6,5,4,3,2,1,0:T(8,128)(2,1)S(1)}, bf16[1,2,2,2,2,24,768]{6,5,4,3,2,1,0:T(8,128)(2,1)S(1)}, u32[]{:S(2)}, u32[]{:S(2)}) collective-permute-start(bf16[1,2,2,2,2,24,768]{6,5,4,3,2,1,0:T(8,128)(2,1)S(1)} %bitcast.79), channel_id=1, source_target_pairs={{0,1},{1,0},{2,3},{3,2},{4,5},{5,4},{6,7},{7,6},{8,9},{9,8},{10,11... | collective-permute-start | bytes 1769480 | tf_op jit(solution)/shard_map/ppermute | solution.py:374
  121.4 20.2 %collective-permute-start.44 = (bf16[1,1,2,2,2,24,1152]{6,5,4,3,2,1,0:T(8,128)(2,1)S(1)}, bf16[1,1,2,2,2,24,1152]{6,5,4,3,2,1,0:T(8,128)(2,1)S(1)}, u32[]{:S(2)}, u32[]{:S(2)}) collective-permute-start(bf16[1,1,2,2,2,24,1152]{6,5,4,3,2,1,0:T(8,128)(2,1)S(1)} %get-tuple-element.126), channel_id=1, source_target_pairs={{0,8},{1,9},{2,10},{3,11},{4,12},{5,13},{6,14},{7,15},{8,0},{9,1},... | collective-permute-start | bytes 1327112 | tf_op jit(solution)/shard_map/ppermute | solution.py:374
  123.6 28.5 %collective-permute-start.47 = (bf16[2,1,1,2,2,24,1152]{6,5,4,3,2,1,0:T(8,128)(2,1)S(1)}, bf16[2,1,1,2,2,24,1152]{6,5,4,3,2,1,0:T(8,128)(2,1)S(1)}, u32[]{:S(2)}, u32[]{:S(2)}) collective-permute-start(bf16[2,1,1,2,2,24,1152]{6,5,4,3,2,1,0:T(8,128)(2,1)S(1)} %get-tuple-element.124), channel_id=1, source_target_pairs={{0,16},{1,17},{2,18},{3,19},{4,20},{5,21},{6,22},{7,23},{8,24},{9,... | collective-permute-start | bytes 1327112 | tf_op jit(solution)/shard_map/ppermute | solution.py:374
  137.1 23.6 %collective-permute-start.28 = (bf16[1,2,2,2,2,24,896]{6,5,4,3,2,1,0:T(8,128)(2,1)S(1)}, bf16[1,2,2,2,2,24,896]{6,5,4,3,2,1,0:T(8,128)(2,1)S(1)}, u32[]{:S(2)}, u32[]{:S(2)}) collective-permute-start(bf16[1,2,2,2,2,24,896]{6,5,4,3,2,1,0:T(8,128)(2,1)S(1)} %bitcast.78), channel_id=1, source_target_pairs={{0,1},{1,0},{2,3},{3,2},{4,5},{5,4},{6,7},{7,6},{8,9},{9,8},{10,11... | collective-permute-start | bytes 2064392 | tf_op jit(solution)/shard_map/ppermute | solution.py:374
  141.6 23.6 %collective-permute-start.33 = (bf16[1,2,2,2,2,24,1536]{6,5,4,3,2,1,0:T(8,128)(2,1)S(1)}, bf16[1,2,2,2,2,24,1536]{6,5,4,3,2,1,0:T(8,128)(2,1)S(1)}, u32[]{:S(2)}, u32[]{:S(2)}) collective-permute-start(bf16[1,2,2,2,2,24,1536]{6,5,4,3,2,1,0:T(8,128)(2,1)S(1)} %bitcast.75), channel_id=1, source_target_pairs={{0,1},{1,0},{2,3},{3,2},{4,5},{5,4},{6,7},{7,6},{8,9},{9,8},{10,11... | collective-permute-start | bytes 3538952 | tf_op jit(solution)/shard_map/ppermute | solution.py:374
  141.8 15.0 %collective-permute-start.45 = (bf16[1,1,1,2,2,24,1152]{6,5,4,3,2,1,0:T(8,128)(2,1)S(1)}, bf16[1,1,1,2,2,24,1152]{6,5,4,3,2,1,0:T(8,128)(2,1)S(1)}, u32[]{:S(2)}, u32[]{:S(2)}) collective-permute-start(bf16[1,1,1,2,2,24,1152]{6,5,4,3,2,1,0:T(8,128)(2,1)S(1)} %get-tuple-element.135), channel_id=1, source_target_pairs={{0,16},{1,17},{2,18},{3,19},{4,20},{5,21},{6,22},{7,23},{8,24},{9,... | collective-permute-start | bytes 663560 | tf_op jit(solution)/shard_map/ppermute | solution.py:374
  162.6 13.1 %collective-permute-start.50 = (bf16[2,24,2304]{2,1,0:T(8,128)(2,1)S(1)}, bf16[2,24,2304]{2,1,0:T(8,128)(2,1)S(1)}, u32[]{:S(2)}, u32[]{:S(2)}) collective-permute-start(bf16[2,24,2304]{2,1,0:T(8,128)(2,1)S(1)} %get-tuple-element.115), channel_id=1, source_target_pairs={{0,2},{1,3},{2,0},{3,1},{4,6},{5,7},{6,4},{7,5},{8,10},{9,11},{10,... | collective-permute-start | bytes 663560 | tf_op jit(solution)/shard_map/ppermute | solution.py:374
  165.6 20.4 %collective-permute-start.34 = (bf16[1,1,2,2,2,24,1536]{6,5,4,3,2,1,0:T(8,128)(2,1)S(1)}, bf16[1,1,2,2,2,24,1536]{6,5,4,3,2,1,0:T(8,128)(2,1)S(1)}, u32[]{:S(2)}, u32[]{:S(2)}) collective-permute-start(bf16[1,1,2,2,2,24,1536]{6,5,4,3,2,1,0:T(8,128)(2,1)S(1)} %get-tuple-element.122), channel_id=1, source_target_pairs={{0,4},{1,5},{2,6},{3,7},{4,0},{5,1},{6,2},{7,3},{8,12},{9,13},{10,... | collective-permute-start | bytes 1769480 | tf_op jit(solution)/shard_map/ppermute | solution.py:374
  172.4 15.7 %collective-permute-start.42 = (bf16[1,1,1,1,1,24,768]{6,5,4,3,2,1,0:T(8,128)(2,1)S(1)}, bf16[1,1,1,1,1,24,768]{6,5,4,3,2,1,0:T(8,128)(2,1)S(1)}, u32[]{:S(2)}, u32[]{:S(2)}) collective-permute-start(bf16[1,1,1,1,1,24,768]{6,5,4,3,2,1,0:T(8,128)(2,1)S(1)} %add_convert_fusion.32), channel_id=1, source_target_pairs={{0,16},{1,17},{2,18},{3,19},{4,20},{5,21},{6,22},{7,23},{8,24},{9,... | collective-permute-start | bytes 110600 | tf_op jit(solution)/shard_map/ppermute | solution.py:374
  (35 other events, 260.0 us)

commit v2 on v1

--- a/solution.py
+++ b/solution.py
@@ -11,8 +11,14 @@
 
 HD = 64
 LOW = (2, 1)
-PARTS = 2
-VMEM = 20 * 2**20
+PARTS = 4
+
+
+def cuts(hidden):
+    return (0, hidden, 2 * hidden, 2 * hidden + hidden // 2, 3 * hidden)
+
+
+VMEM = 24 * 2**20
 EPS = 1e-05
 MASKED = -1e30
 THETA = 10000.0
@@ -93,16 +99,14 @@
     rows, d = wq.shape
     low = me[0] % (2 * LOW[0])
     hidden = wgate.shape[1] // 4
-    fc = hidden // PARTS
     moves = [(attn_gain, gain1), (mlp_gain, gain2), (wq, qk.at[:, :d]), (wk, qk.at[:, d : 2 * d]),
              (wv, vo.at[:, :d]), (wo, vo.at[:, d:])]
     for ref, flip in ((keep, 0), (send, LOW[0])):
         for i, other in enumerate((0, LOW[1])):
             base = (low ^ (flip + other)) * hidden
-            for c in range(PARTS):
-                for m, w in enumerate((wgate, wup, wdown)):
-                    at = i * 3 * hidden + (c * 3 + m) * fc
-                    moves.append((w.at[:, pl.ds(pl.multiple_of(base + c * fc, 128), fc)], ref.at[:, at : at + fc]))
+            for m, w in enumerate((wgate, wup, wdown)):
+                at = (i * 3 + m) * hidden
+                moves.append((w.at[:, pl.ds(pl.multiple_of(base, 128), hidden)], ref.at[:, at : at + hidden]))
     copies = [pltpu.make_async_copy(src, dst, sems.at[i]) for i, (src, dst) in enumerate(moves)]
     for copy in copies:
         copy.start()
@@ -119,13 +123,10 @@
     parts, outs = [ref.at[i] for ref in refs[:2] for i in range(2)], refs[2:]
     low = me[0] % (2 * LOW[0])
     hidden = outs[0].shape[1] // 4
-    fc = hidden // PARTS
     for ref, flip in zip(parts, (0, LOW[1], LOW[0], LOW[0] + LOW[1])):
         base = (low ^ flip) * hidden
-        for c in range(PARTS):
-            for m, out in enumerate(outs):
-                at = (c * 3 + m) * fc
-                out[:, pl.ds(pl.multiple_of(base + c * fc, 128), fc)] = ref[:, at : at + fc].astype(f32)
+        for m, out in enumerate(outs):
+            out[:, pl.ds(pl.multiple_of(base, 128), hidden)] = ref[:, m * hidden : (m + 1) * hidden].astype(f32)
 
 
 def prep_kernel(me, tokens, cot, places, seq, cosine, sine, xp, gb, gbg, own_sel, group_sel, change, cos, sin):
@@ -158,20 +159,20 @@
 
 def fold2_kernel(me, kept, got, *parts):
     b = me[0] % 2
-    cols = parts[0].shape[3]
+    edges = cuts(kept.shape[2] // 3)
     for c, out in enumerate(parts):
         for at, ref in ((b, kept), (1 - b, got)):
-            out[pl.ds(at, 1)] = ref[:, :, c * cols : (c + 1) * cols][None]
+            out[pl.ds(at, 1)] = ref[:, :, edges[c] : edges[c + 1]][None]
 
 
 def unfold_kernel(me, *refs):
     terms, (keep, send) = refs[:-2], refs[-2:]
     b = me[0] % 2
-    cols = terms[0].shape[3]
+    edges = cuts(keep.shape[2] // 3)
     for c in range(PARTS):
         for at, ref in ((b, keep), (1 - b, send)):
             total = sum(v[pl.ds(at, 1)].astype(f32) for v in terms[2 * c : 2 * c + 2])
-            ref[:, :, c * cols : (c + 1) * cols] = total[0].astype(bf16)
+            ref[:, :, edges[c] : edges[c + 1]] = total[0].astype(bf16)
 
 
 def unfold2_kernel(me, kept, got, keep, send):
@@ -228,57 +229,51 @@
 
 
 def ff_kernel(*refs):
-    pieces, ws, (act, both, keep, send, n2, gb, acc) = refs[:8], refs[8 : 8 + PARTS], refs[8 + PARTS :]
+    pieces, (wg, wu, *wd), (act, dg, du, keep, send, n2, gb, acc) = refs[:8], refs[8:12], refs[12:]
     rows = pieces[0].shape[0]
     for i in range(4):
         n2[i * rows : (i + 1) * rows] = pieces[i][...]
         gb[i * rows : (i + 1) * rows] = pieces[4 + i][...]
     half = n2.shape[0] // 2
-    for c, w in enumerate(ws):
-        fc = w.shape[1] // 3
-        gate = nn(n2[...], w[:, :fc])
-        up = nn(n2[...], w[:, fc : 2 * fc])
-        dact = nn(gb[...], w[:, 2 * fc :])
+    fc = wd[0].shape[1]
+    for c in range(2):
+        cols = slice(c * fc, (c + 1) * fc)
+        gate = nn(n2[...], wg[:, cols])
+        up = nn(n2[...], wu[:, cols])
+        dact = nn(gb[...], wd[c][...])
         sig = jax.nn.sigmoid(gate)
         silu = gate * sig
-        act[:, c * fc : (c + 1) * fc] = (silu * up).astype(bf16)
-        at = 2 * c * fc
-        both[:, at : at + fc] = (dact * up * sig * (1.0 + gate * (1.0 - sig))).astype(bf16)
-        both[:, at + fc : at + 2 * fc] = (dact * silu).astype(bf16)
-        part = nt(both[:, at : at + 2 * fc], w[:, : 2 * fc])
+        act[:, cols] = (silu * up).astype(bf16)
+        dg[:, cols] = (dact * up * sig * (1.0 + gate * (1.0 - sig))).astype(bf16)
+        du[:, cols] = (dact * silu).astype(bf16)
+        part = nt(dg[:, cols], wg[:, cols]) + nt(du[:, cols], wu[:, cols])
         acc[...] = part if c == 0 else acc[...] + part
     keep[...] = acc[:half].astype(bf16)
     send[...] = acc[half:].astype(bf16)
 
 
 def ff_grad_kernel(*refs):
-    pieces, act, both, (n2t, gbt) = refs[:8], refs[8], refs[9], refs[-2:]
+    pieces, (act, dg, du), sides, (n2t, gbt) = refs[:8], refs[8:11], refs[11:-2], refs[-2:]
     rows = pieces[0].shape[0]
     for i in range(4):
         n2t[:, i * rows : (i + 1) * rows] = pieces[i][...].astype(f32).T.astype(bf16)
         gbt[:, i * rows : (i + 1) * rows] = pieces[4 + i][...].astype(f32).T.astype(bf16)
-    refs = refs[10:-2]
-    for c in range(PARTS):
-        keep, send = refs[2 * c : 2 * c + 2]
-        fc = keep.shape[1] // 3
-        runs = 2 ** c
+    fc = act.shape[1] // 2
+    for c, (left, right) in enumerate(((n2t, dg[...]), (n2t, du[...]), (gbt, act[:, :fc]), (gbt, act[:, fc:]))):
+        keep, send = sides[2 * c : 2 * c + 2]
+        runs = 1 + c % 2
         run = n2t.shape[0] // (2 * runs)
-        for left, right, cols in (
-            (n2t, both[:, 2 * c * fc : 2 * (c + 1) * fc], slice(0, 2 * fc)),
-            (gbt, act[:, c * fc : (c + 1) * fc], slice(2 * fc, 3 * fc)),
-        ):
-            dw = nn(left[...], right).astype(bf16)
-            for r in range(runs):
-                keep[r * run : (r + 1) * run, cols] = dw[2 * r * run : (2 * r + 1) * run]
-                send[r * run : (r + 1) * run, cols] = dw[(2 * r + 1) * run : (2 * r + 2) * run]
-
-
-def ff_out_kernel(act, *refs):
-    ws, (keep, send) = refs[:PARTS], refs[PARTS:]
+        dw = nn(left[...], right).astype(bf16)
+        for r in range(runs):
+            keep[r * run : (r + 1) * run] = dw[2 * r * run : (2 * r + 1) * run]
+            send[r * run : (r + 1) * run] = dw[(2 * r + 1) * run : (2 * r + 2) * run]
+
+
+def ff_out_kernel(act, w0, w1, keep, send):
     half = act.shape[0] // 2
-    fc = ws[0].shape[1] // 3
+    fc = w0.shape[1]
     for ref, rows in ((keep, slice(0, half)), (send, slice(half, 2 * half))):
-        ref[...] = sum(nt(act[rows, c * fc : (c + 1) * fc], w[:, 2 * fc :]) for c, w in enumerate(ws)).astype(bf16)
+        ref[...] = (nt(act[rows, :fc], w0[...]) + nt(act[rows, fc:], w1[...])).astype(bf16)
 
 
 def back_kernel(k1, g1, g2, hmid, gb, gains, vo0, vo1, ob, change, dh, dob, keep, send, dgain):
@@ -405,7 +400,9 @@
         rows = d // n
         ff = w_gate.shape[1]
         share = 2 ** len(LOW)
-        fc = ff // share // PARTS
+        hidden = ff // share
+        edges = cuts(hidden)
+        widths = [b - a for a, b in zip(edges, edges[1:])]
         half = d // 2
         me = lax.axis_index("dp")
 
@@ -419,20 +416,20 @@
         part_qk, part_vo, keep, send = call(
             pack_kernel, shards, me1, attn_gain[None, :], mlp_gain[None, :], w_query, w_key, w_value, w_output.T,
             w_gate, w_up, w_down.T, fetch=False, grant=3 * VMEM,
-            scratch_shapes=[pltpu.VMEM((1, rows), bf16)] * 2 + [pltpu.SemaphoreType.DMA((6 + 12 * PARTS,))])
+            scratch_shapes=[pltpu.VMEM((1, rows), bf16)] * 2 + [pltpu.SemaphoreType.DMA((18,))])
         mine = ff * 3 // share
         block = ((2, rows, mine), bf16)
         keep, send = call(fold_kernel, [block] * 2, me1, keep, swap(send, LOW[0]))
-        ws = call(fold2_kernel, [((2, 2, rows, 3 * fc), bf16)] * PARTS, me1, keep, swap(send, LOW[1]))
+        ws = call(fold2_kernel, [((2, 2, rows, v), bf16) for v in widths], me1, keep, swap(send, LOW[1]))
         qk = gather(part_qk, first)
         vo = gather(part_vo, second)
         wff = []
         for c in range(PARTS):
-            w = ws[c].reshape((1,) * len(high) + (2, 2, rows, 3 * fc))
-            for b in ff_orders[c]:
+            w = ws[c].reshape((1,) * len(high) + (2, 2, rows, widths[c]))
+            for b in ff_orders[c % 2]:
                 got = swap(w, b)
                 w = jnp.concatenate([w, got], axis=ff_axis[b])
-            wff.append(w.reshape(d, 3 * fc))
+            wff.append(w.reshape(d, widths[c]))
         freq = jnp.exp(jnp.arange(HD // 2, dtype=f32) * (-2.0 * math.log(THETA) / HD))
         angles = positions.astype(f32)[:, None] * freq[None, :]
         cosine, sine = jnp.cos(angles), jnp.sin(angles)
@@ -459,22 +456,21 @@
         hmid, n2g = call(mid_kernel, [wide, act], xp, ob, *vo, gains, change)
         n24 = group_gather(n2g)
         tg = share * toks
-        hidden = PARTS * fc
         pairs = [((tg // 2, d), bf16)] * 2
-        acts, both, keep, send = call(
-            ff_kernel, [((tg, hidden), bf16), ((tg, 2 * hidden), bf16)] + pairs, *n24, *gb4, *wff,
+        acts, dg, du, keep, send = call(
+            ff_kernel, [((tg, hidden), bf16)] * 3 + pairs, *n24, *gb4, *wff,
             scratch_shapes=[pltpu.VMEM((tg, d), bf16)] * 2 + [pltpu.VMEM((tg, d), f32)])
         dn2 = group_halve(keep, send)
         grads = call(
-            ff_grad_kernel, [((half, 3 * fc), bf16)] * (2 * PARTS), *n24, *gb4, acts, both,
+            ff_grad_kernel, [((half, v), bf16) for v in widths for _ in range(2)], *n24, *gb4, acts, dg, du,
             scratch_shapes=[pltpu.VMEM((d, tg), bf16)] * 2)
-        y = group_halve(*call(ff_out_kernel, pairs, acts, *wff))
+        y = group_halve(*call(ff_out_kernel, pairs, acts, *wff[2:]))
         parts = []
         for c in range(PARTS):
-            steps = tuple(reversed(ff_orders[c]))
-            shape = tuple(1 if b == steps[0] else 2 for b in ff_bits) + (rows, 3 * fc)
+            steps = tuple(reversed(ff_orders[c % 2]))
+            shape = tuple(1 if b == steps[0] else 2 for b in ff_bits) + (rows, widths[c])
             parts.append(reduce(*(v.reshape(shape) for v in grads[2 * c : 2 * c + 2]), steps, ff_axis, None))
-        terms = [v.reshape(2, 2, rows, 3 * fc) for pair in parts for v in pair]
+        terms = [v.reshape(2, 2, rows, -1) for pair in parts for v in pair]
         keep, send = call(unfold_kernel, [block] * 2, me1, *terms)
         keep, send = call(unfold2_kernel, [block] * 2, me1, keep, swap(send, LOW[1]))
         got = swap(send, LOW[0])

time: 206 us -> 241 us (1.17)
  waiting for transfers between devices: 103 us -> 132 us
  starting transfers between devices: 56.2 us -> 61.4 us
    ppermute x51 -> x63, waiting for transfers between devices: 103 us -> 132 us  [swap(): return lax.ppermute(a, 'dp', [(i, i ^ b) for i in range(n)])]
    ppermute x51 -> x63, starting transfers between devices: 56.2 us -> 61.4 us  [swap(): return lax.ppermute(a, 'dp', [(i, i ^ b) for i in range(n)])]
  transfers between devices with their start and end apart: 51 -> 63, of which waited for: 24 -> 28; matrix products, arithmetic and copies ran while one was open for 4% -> 3% of each run, Pallas kernels for 13% -> 10%
where the time goes in v2:
time: 241 us
  waiting for transfers between devices  132 us (55%)
  starting transfers between devices  61.4 us (25%)
  Pallas kernels  36.9 us (15%)
  other arithmetic  7.02 us (3%)
    ppermute x63, waiting for transfers between devices, swap(): return lax.ppermute(a, 'dp', [(i, i ^ b) for i in range(n)])  132 us
    ppermute x63, starting transfers between devices, swap(): return lax.ppermute(a, 'dp', [(i, i ^ b) for i in range(n)])  61.4 us
    pallas_call x16, Pallas kernels, call(): pl.pallas_call(kernel, out_shape=out_shape, in_specs=[smem if v.size == 1...  36.9 us
  transfers between devices with their start and end apart: 63, of which 28 were waited for; matrix products, arithmetic and copies ran while one was open for 3% of the time, Pallas kernels for 10%

profile of v2, /device:TPU:0, one launch (start us, length us, event | category | flops | bytes accessed | tf_op | source)
XLA Modules:
  0.0 240.8 jit_solution(105765568575885209)
XLA Ops:
  2.7 4.1 %collective-permute-start = (bf16[1,1,1,1,1,24,1664]{6,5,4,3,2,1,0:T(8,128)(2,1)}, bf16[1,1,1,1,1,24,1664]{6,5,4,3,2,1,0:T(8,128)(2,1)S(1)}, u32[]{:S(2)}, u32[]{:S(2)}) collective-permute-start(bf16[1,1,1,1,1,24,1664]{6,5,4,3,2,1,0:T(8,128)(2,1)} %bitcast.110), channel_id=1, source_target_pairs={{0,16},{1,17},{2,18},{3,19},{4,20},{5,21},{6,22},{7,23},{8,24},{9,... | collective-permute-start | bytes 239624 | tf_op jit(solution)/shard_map/ppermute | solution.py:369
  6.9 5.4 %collective-permute-done = bf16[1,1,1,1,1,24,1664]{6,5,4,3,2,1,0:T(8,128)(2,1)S(1)} collective-permute-done((bf16[1,1,1,1,1,24,1664]{6,5,4,3,2,1,0:T(8,128)(2,1)}, bf16[1,1,1,1,1,24,1664]{6,5,4,3,2,1,0:T(8,128)(2,1)S(1)}, u32[]{:S(2)}, u32[]{:S(2)}) %collective-permute-start) | collective-permute-done | bytes 79904 | tf_op jit(solution)/shard_map/ppermute | solution.py:369
  16.3 3.5 %collective-permute-done.1 = bf16[1,1,1,1,2,24,1664]{6,5,4,3,2,1,0:T(8,128)(2,1)S(1)} collective-permute-done((bf16[1,1,1,1,2,24,1664]{6,5,4,3,2,1,0:T(8,128)(2,1)S(1)}, bf16[1,1,1,1,2,24,1664]{6,5,4,3,2,1,0:T(8,128)(2,1)S(1)}, u32[]{:S(2)}, u32[]{:S(2)}) %collective-permute-start.1) | collective-permute-done | bytes 159776 | tf_op jit(solution)/shard_map/ppermute | solution.py:369
  25.3 4.0 %collective-permute-done.2 = bf16[1,1,1,2,2,24,1664]{6,5,4,3,2,1,0:T(8,128)(2,1)S(1)} collective-permute-done((bf16[1,1,1,2,2,24,1664]{6,5,4,3,2,1,0:T(8,128)(2,1)S(1)}, bf16[1,1,1,2,2,24,1664]{6,5,4,3,2,1,0:T(8,128)(2,1)S(1)}, u32[]{:S(2)}, u32[]{:S(2)}) %collective-permute-start.2) | collective-permute-done | bytes 319520 | tf_op jit(solution)/shard_map/ppermute | solution.py:369
  29.4 3.2 %collective-permute-start.3 = (bf16[1,1,2,2,2,24,1664]{6,5,4,3,2,1,0:T(8,128)(2,1)S(1)}, bf16[1,1,2,2,2,24,1664]{6,5,4,3,2,1,0:T(8,128)(2,1)S(1)}, u32[]{:S(2)}, u32[]{:S(2)}) collective-permute-start(bf16[1,1,2,2,2,24,1664]{6,5,4,3,2,1,0:T(8,128)(2,1)S(1)} %pad_maximum_fusion.4), channel_id=1, source_target_pairs={{0,4},{1,5},{2,6},{3,7},{4,0},{5,1},{6,2},{7,3},{8,12},{9,13},{10,... | collective-permute-start | bytes 1916936 | tf_op jit(solution)/shard_map/ppermute | solution.py:369
  34.8 4.9 %collective-permute-done.16.got = bf16[24,4608]{1,0:T(8,128)(2,1)S(1)} collective-permute-done((bf16[24,4608]{1,0:T(8,128)(2,1)S(1)}, bf16[24,4608]{1,0:T(8,128)(2,1)S(1)}, u32[]{:S(2)}, u32[]{:S(2)}) %collective-permute-start.16) | collective-permute-done | bytes 221216 | tf_op jit(solution)/shard_map/ppermute | solution.py:369
  46.7 7.8 %collective-permute-done.24 = bf16[1,1,1,2,2,24,384]{6,5,4,3,2,1,0:T(8,128)(2,1)S(1)} collective-permute-done((bf16[1,1,1,2,2,24,384]{6,5,4,3,2,1,0:T(8,128)(2,1)S(1)}, bf16[1,1,1,2,2,24,384]{6,5,4,3,2,1,0:T(8,128)(2,1)S(1)}, u32[]{:S(2)}, u32[]{:S(2)}) %collective-permute-start.24) | collective-permute-done | bytes 73760 | tf_op jit(solution)/shard_map/ppermute | solution.py:369
  58.6 10.6 %collective-permute-done.25 = bf16[1,1,2,2,2,24,384]{6,5,4,3,2,1,0:T(8,128)(2,1)S(1)} collective-permute-done((bf16[1,1,2,2,2,24,384]{6,5,4,3,2,1,0:T(8,128)(2,1)S(1)}, bf16[1,1,2,2,2,24,384]{6,5,4,3,2,1,0:T(8,128)(2,1)S(1)}, u32[]{:S(2)}, u32[]{:S(2)}) %collective-permute-start.25) | collective-permute-done | bytes 147488 | tf_op jit(solution)/shard_map/ppermute | solution.py:369
  69.3 5.9 %collective-permute-done.19 = bf16[1,1,2,2,2,24,768]{6,5,4,3,2,1,0:T(8,128)(2,1)S(1)} collective-permute-done((bf16[1,1,2,2,2,24,768]{6,5,4,3,2,1,0:T(8,128)(2,1)S(1)}, bf16[1,1,2,2,2,24,768]{6,5,4,3,2,1,0:T(8,128)(2,1)S(1)}, u32[]{:S(2)}, u32[]{:S(2)}) %collective-permute-start.19) | collective-permute-done | bytes 294944 | tf_op jit(solution)/shard_map/ppermute | solution.py:369
  83.4 3.8 %shard_map.223 = (bf16[768,192]{1,0:T(8,128)(2,1)S(1)}, bf16[192,768]{1,0:T(8,128)(2,1)S(1)}, bf16[192,768]{1,0:T(8,128)(2,1)S(1)}, bf16[192,768]{1,0:T(8,128)(2...) custom-call(bf16[192,768]{1,0:T(8,128)(2,1)S(1)} %get-tuple-element.72.xp, ...), custom_call_target="tpu_custom_call" | custom-call | tf_op jit(solution)/shard_map/pallas_call | solution.py:52
  89.0 10.9 %collective-permute-done.29 = bf16[2,1,2,2,2,24,384]{6,5,4,3,2,1,0:T(8,128)(2,1)S(1)} collective-permute-done((bf16[2,1,2,2,2,24,384]{6,5,4,3,2,1,0:T(8,128)(2,1)S(1)}, bf16[2,1,2,2,2,24,384]{6,5,4,3,2,1,0:T(8,128)(2,1)S(1)}, u32[]{:S(2)}, u32[]{:S(2)}) %collective-permute-start.29) | collective-permute-done | bytes 294944 | tf_op jit(solution)/shard_map/ppermute | solution.py:369
  102.3 7.5 %shard_map.227 = (bf16[768,768]{1,0:T(8,128)(2,1)S(1)}, bf16[768,768]{1,0:T(8,128)(2,1)S(1)}, bf16[768,768]{1,0:T(8,128)(2,1)S(1)}, bf16[384,768]{1,0:T(8,128)(2,1)S(1)}, bf16[384,768]{1,0:T(8,128)(2,1)S(1)}) custom-call(bf16[192,768]{1,0:T(8,128)(2,1)S(1)} %get-tuple-element.80.refs_0_, bf16[192,768]{1,0:T(8,128)(2,1)S(1)} %collective-permute-done.10.refs_1_, ...), custom_call_target="tpu_custom_call" | custom-call | tf_op jit(solution)/shard_map/pallas_call | solution.py:52
  109.8 3.7 %shard_map.233 = (bf16[384,768]{1,0:T(8,128)(2,1)S(1)}, bf16[384,768]{1,0:T(8,128)(2,1)S(1)}, bf16[384,768]{1,0:T(8,128)(2,1)S(1)}, bf16[384,768]{1,0:T(8,128)(2...) custom-call(bf16[192,768]{1,0:T(8,128)(2,1)S(1)} %get-tuple-element., ...), custom_call_target="tpu_custom_call" | custom-call | tf_op jit(solution)/shard_map/pallas_call | solution.py:52
  118.0 5.4 %collective-permute-done.55 = bf16[1,2,2,2,2,24,384]{6,5,4,3,2,1,0:T(8,128)(2,1)S(1)} collective-permute-done((bf16[1,2,2,2,2,24,384]{6,5,4,3,2,1,0:T(8,128)(2,1)S(1)}, bf16[1,2,2,2,2,24,384]{6,5,4,3,2,1,0:T(8,128)(2,1)S(1)}, u32[]{:S(2)}, u32[]{:S(2)}) %collective-permute-start.55) | collective-permute-done | bytes 294944 | tf_op jit(solution)/shard_map/ppermute | solution.py:369
  125.7 14.6 %collective-permute-done.56 = bf16[1,1,2,2,2,24,384]{6,5,4,3,2,1,0:T(8,128)(2,1)S(1)} collective-permute-done((bf16[1,1,2,2,2,24,384]{6,5,4,3,2,1,0:T(8,128)(2,1)S(1)}, bf16[1,1,2,2,2,24,384]{6,5,4,3,2,1,0:T(8,128)(2,1)S(1)}, u32[]{:S(2)}, u32[]{:S(2)}) %collective-permute-start.56) | collective-permute-done | bytes 147488 | tf_op jit(solution)/shard_map/ppermute | solution.py:369
  146.3 4.6 %collective-permute-done.59 = bf16[2,1,1,2,2,24,384]{6,5,4,3,2,1,0:T(8,128)(2,1)S(1)} collective-permute-done((bf16[2,1,1,2,2,24,384]{6,5,4,3,2,1,0:T(8,128)(2,1)S(1)}, bf16[2,1,1,2,2,24,384]{6,5,4,3,2,1,0:T(8,128)(2,1)S(1)}, u32[]{:S(2)}, u32[]{:S(2)}) %collective-permute-start.59) | collective-permute-done | bytes 147488 | tf_op jit(solution)/shard_map/ppermute | solution.py:369
  153.2 4.2 %collective-permute-done.50 = bf16[1,1,2,2,2,24,768]{6,5,4,3,2,1,0:T(8,128)(2,1)S(1)} collective-permute-done((bf16[1,1,2,2,2,24,768]{6,5,4,3,2,1,0:T(8,128)(2,1)S(1)}, bf16[1,1,2,2,2,24,768]{6,5,4,3,2,1,0:T(8,128)(2,1)S(1)}, u32[]{:S(2)}, u32[]{:S(2)}) %collective-permute-start.50) | collective-permute-done | bytes 294944 | tf_op jit(solution)/shard_map/ppermute | solution.py:369
  157.5 6.0 %collective-permute-done.53 = bf16[2,1,1,2,2,24,768]{6,5,4,3,2,1,0:T(8,128)(2,1)S(1)} collective-permute-done((bf16[2,1,1,2,2,24,768]{6,5,4,3,2,1,0:T(8,128)(2,1)S(1)}, bf16[2,1,1,2,2,24,768]{6,5,4,3,2,1,0:T(8,128)(2,1)S(1)}, u32[]{:S(2)}, u32[]{:S(2)}) %collective-permute-start.53) | collective-permute-done | bytes 294944 | tf_op jit(solution)/shard_map/ppermute | solution.py:369
  164.5 7.4 %shard_map.231 = (bf16[192,768]{1,0:T(8,128)(2,1)S(1)}, bf16[192,768]{1,0:T(8,128)(2,1)S(1)}, bf16[192,768]{1,0:T(8,128)(2,1)S(1)}, bf16[384,1536]{1,0:T(8,128)(2,1)S(1)}, bf16[384,1536]{1,0:T(8,128)(2,1)S(1)}) custom-call(bf16[192,768]{1,0:T(8,128)(2,1)S(1)} %get-tuple-element.96.qr, bf16[192,768]{1,0:T(8,128)(2,1)S(1)} %get-tuple-element.97.kr, ...), custom_call_target="tpu_custom_call" | custom-call | tf_op jit(solution)/shard_map/pallas_call | solution.py:52
  185.2 7.4 %collective-permute-done.62.refs_1_ = bf16[2,24,2304]{2,1,0:T(8,128)(2,1)S(1)} collective-permute-done((bf16[2,24,2304]{2,1,0:T(8,128)(2,1)S(1)}, bf16[2,24,2304]{2,1,0:T(8,128)(2,1)S(1)}, u32[]{:S(2)}, u32[]{:S(2)}) %collective-permute-start.62) | collective-permute-done | bytes 221216 | tf_op jit(solution)/shard_map/ppermute | solution.py:369
  198.9 4.4 %collective-permute-start.47 = (bf16[1,1,1,1,2,24,768]{6,5,4,3,2,1,0:T(8,128)(2,1)S(1)}, bf16[1,1,1,1,2,24,768]{6,5,4,3,2,1,0:T(8,128)(2,1)S(1)}, u32[]{:S(2)}, u32[]{:S(2)}) collective-permute-start(bf16[1,1,1,1,2,24,768]{6,5,4,3,2,1,0:T(8,128)(2,1)S(1)} %get-tuple-element.168), channel_id=1, source_target_pairs={{0,8},{1,9},{2,10},{3,11},{4,12},{5,13},{6,14},{7,15},{8,0},{9,1},... | collective-permute-start | bytes 221192 | tf_op jit(solution)/shard_map/ppermute | solution.py:369
  207.7 12.9 %collective-permute-done.36 = bf16[1,1,1,2,2,24,896]{6,5,4,3,2,1,0:T(8,128)(2,1)S(1)} collective-permute-done((bf16[1,1,1,2,2,24,896]{6,5,4,3,2,1,0:T(8,128)(2,1)S(1)}, bf16[1,1,1,2,2,24,896]{6,5,4,3,2,1,0:T(8,128)(2,1)S(1)}, u32[]{:S(2)}, u32[]{:S(2)}) %collective-permute-start.36) | collective-permute-done | bytes 172064 | tf_op jit(solution)/shard_map/ppermute | solution.py:369
  222.4 3.2 %collective-permute-done.37 = bf16[1,1,1,1,2,24,896]{6,5,4,3,2,1,0:T(8,128)(2,1)S(1)} collective-permute-done((bf16[1,1,1,1,2,24,896]{6,5,4,3,2,1,0:T(8,128)(2,1)S(1)}, bf16[1,1,1,1,2,24,896]{6,5,4,3,2,1,0:T(8,128)(2,1)S(1)}, u32[]{:S(2)}, u32[]{:S(2)}) %collective-permute-start.37) | collective-permute-done | bytes 86048 | tf_op jit(solution)/shard_map/ppermute | solution.py:369
  234.8 5.3 %collective-permute-done.43 = bf16[1,1,1,1,1,24,1536]{6,5,4,3,2,1,0:T(8,128)(2,1)S(1)} collective-permute-done((bf16[1,1,1,1,1,24,1536]{6,5,4,3,2,1,0:T(8,128)(2,1)S(1)}, bf16[1,1,1,1,1,24,1536]{6,5,4,3,2,1,0:T(8,128)(2,1)S(1)}, u32[]{:S(2)}, u32[]{:S(2)}) %collective-permute-start.43) | collective-permute-done | bytes 73760 | tf_op jit(solution)/shard_map/ppermute | solution.py:369
  (187 shorter events, 88.8 us)
Async XLA Ops:
  29.4 16.3 %collective-permute-start.3 = (bf16[1,1,2,2,2,24,1664]{6,5,4,3,2,1,0:T(8,128)(2,1)S(1)}, bf16[1,1,2,2,2,24,1664]{6,5,4,3,2,1,0:T(8,128)(2,1)S(1)}, u32[]{:S(2)}, u32[]{:S(2)}) collective-permute-start(bf16[1,1,2,2,2,24,1664]{6,5,4,3,2,1,0:T(8,128)(2,1)S(1)} %pad_maximum_fusion.4), channel_id=1, source_target_pairs={{0,4},{1,5},{2,6},{3,7},{4,0},{5,1},{6,2},{7,3},{8,12},{9,13},{10,... | collective-permute-start | bytes 1916936 | tf_op jit(solution)/shard_map/ppermute | solution.py:369
  46.5 34.9 %collective-permute-start.4 = (bf16[1,2,2,2,2,24,1664]{6,5,4,3,2,1,0:T(8,128)(2,1)S(1)}, bf16[1,2,2,2,2,24,1664]{6,5,4,3,2,1,0:T(8,128)(2,1)S(1)}, u32[]{:S(2)}, u32[]{:S(2)}) collective-permute-start(bf16[1,2,2,2,2,24,1664]{6,5,4,3,2,1,0:T(8,128)(2,1)S(1)} %pad_maximum_fusion), channel_id=1, source_target_pairs={{0,1},{1,0},{2,3},{3,2},{4,5},{5,4},{6,7},{7,6},{8,9},{9,8},{10,11... | collective-permute-start | bytes 3833864 | tf_op jit(solution)/shard_map/ppermute | solution.py:369
  54.5 25.4 %collective-permute-start.9 = (bf16[1,2,2,2,2,24,1536]{6,5,4,3,2,1,0:T(8,128)(2,1)S(1)}, bf16[1,2,2,2,2,24,1536]{6,5,4,3,2,1,0:T(8,128)(2,1)S(1)}, u32[]{:S(2)}, u32[]{:S(2)}) collective-permute-start(bf16[1,2,2,2,2,24,1536]{6,5,4,3,2,1,0:T(8,128)(2,1)S(1)} %pad_maximum_fusion.1), channel_id=1, source_target_pairs={{0,1},{1,0},{2,3},{3,2},{4,5},{5,4},{6,7},{7,6},{8,9},{9,8},{10,11... | collective-permute-start | bytes 3538952 | tf_op jit(solution)/shard_map/ppermute | solution.py:369
  54.5 14.7 %collective-permute-start.25 = (bf16[1,1,2,2,2,24,384]{6,5,4,3,2,1,0:T(8,128)(2,1)S(1)}, bf16[1,1,2,2,2,24,384]{6,5,4,3,2,1,0:T(8,128)(2,1)S(1)}, u32[]{:S(2)}, u32[]{:S(2)}) collective-permute-start(bf16[1,1,2,2,2,24,384]{6,5,4,3,2,1,0:T(8,128)(2,1)S(1)} %pad_maximum_fusion.18), channel_id=1, source_target_pairs={{0,8},{1,9},{2,10},{3,11},{4,12},{5,13},{6,14},{7,15},{8,0},{9,1},... | collective-permute-start | bytes 442376 | tf_op jit(solution)/shard_map/ppermute | solution.py:369
  54.9 20.2 %collective-permute-start.19 = (bf16[1,1,2,2,2,24,768]{6,5,4,3,2,1,0:T(8,128)(2,1)S(1)}, bf16[1,1,2,2,2,24,768]{6,5,4,3,2,1,0:T(8,128)(2,1)S(1)}, u32[]{:S(2)}, u32[]{:S(2)}) collective-permute-start(bf16[1,1,2,2,2,24,768]{6,5,4,3,2,1,0:T(8,128)(2,1)S(1)} %pad_maximum_fusion.12), channel_id=1, source_target_pairs={{0,8},{1,9},{2,10},{3,11},{4,12},{5,13},{6,14},{7,15},{8,0},{9,1},... | collective-permute-start | bytes 884744 | tf_op jit(solution)/shard_map/ppermute | solution.py:369
  56.8 19.2 %collective-permute-start.22 = (bf16[2,1,1,2,2,24,768]{6,5,4,3,2,1,0:T(8,128)(2,1)S(1)}, bf16[2,1,1,2,2,24,768]{6,5,4,3,2,1,0:T(8,128)(2,1)S(1)}, u32[]{:S(2)}, u32[]{:S(2)}) collective-permute-start(bf16[2,1,1,2,2,24,768]{6,5,4,3,2,1,0:T(8,128)(2,1)S(1)} %pad_maximum_fusion.13), channel_id=1, source_target_pairs={{0,16},{1,17},{2,18},{3,19},{4,20},{5,21},{6,22},{7,23},{8,24},{9,... | collective-permute-start | bytes 884744 | tf_op jit(solution)/shard_map/ppermute | solution.py:369
  75.2 13.2 %collective-permute-start.26 = (bf16[1,2,2,2,2,24,384]{6,5,4,3,2,1,0:T(8,128)(2,1)S(1)}, bf16[1,2,2,2,2,24,384]{6,5,4,3,2,1,0:T(8,128)(2,1)S(1)}, u32[]{:S(2)}, u32[]{:S(2)}) collective-permute-start(bf16[1,2,2,2,2,24,384]{6,5,4,3,2,1,0:T(8,128)(2,1)S(1)} %pad_maximum_fusion.14), channel_id=1, source_target_pairs={{0,4},{1,5},{2,6},{3,7},{4,0},{5,1},{6,2},{7,3},{8,12},{9,13},{10,... | collective-permute-start | bytes 884744 | tf_op jit(solution)/shard_map/ppermute | solution.py:369
  76.0 23.9 %collective-permute-start.20 = (bf16[1,2,2,2,2,24,768]{6,5,4,3,2,1,0:T(8,128)(2,1)S(1)}, bf16[1,2,2,2,2,24,768]{6,5,4,3,2,1,0:T(8,128)(2,1)S(1)}, u32[]{:S(2)}, u32[]{:S(2)}) collective-permute-start(bf16[1,2,2,2,2,24,768]{6,5,4,3,2,1,0:T(8,128)(2,1)S(1)} %pad_maximum_fusion.6), channel_id=1, source_target_pairs={{0,4},{1,5},{2,6},{3,7},{4,0},{5,1},{6,2},{7,3},{8,12},{9,13},{10,... | collective-permute-start | bytes 1769480 | tf_op jit(solution)/shard_map/ppermute | solution.py:369
  79.6 21.1 %collective-permute-start.23 = (bf16[2,1,2,2,2,24,768]{6,5,4,3,2,1,0:T(8,128)(2,1)S(1)}, bf16[2,1,2,2,2,24,768]{6,5,4,3,2,1,0:T(8,128)(2,1)S(1)}, u32[]{:S(2)}, u32[]{:S(2)}) collective-permute-start(bf16[2,1,2,2,2,24,768]{6,5,4,3,2,1,0:T(8,128)(2,1)S(1)} %pad_maximum_fusion.7), channel_id=1, source_target_pairs={{0,8},{1,9},{2,10},{3,11},{4,12},{5,13},{6,14},{7,15},{8,0},{9,1},... | collective-permute-start | bytes 1769480 | tf_op jit(solution)/shard_map/ppermute | solution.py:369
  81.4 18.4 %collective-permute-start.29 = (bf16[2,1,2,2,2,24,384]{6,5,4,3,2,1,0:T(8,128)(2,1)S(1)}, bf16[2,1,2,2,2,24,384]{6,5,4,3,2,1,0:T(8,128)(2,1)S(1)}, u32[]{:S(2)}, u32[]{:S(2)}) collective-permute-start(bf16[2,1,2,2,2,24,384]{6,5,4,3,2,1,0:T(8,128)(2,1)S(1)} %pad_maximum_fusion.15), channel_id=1, source_target_pairs={{0,8},{1,9},{2,10},{3,11},{4,12},{5,13},{6,14},{7,15},{8,0},{9,1},... | collective-permute-start | bytes 884744 | tf_op jit(solution)/shard_map/ppermute | solution.py:369
  116.0 47.6 %collective-permute-start.30 = (bf16[384,768]{1,0:T(8,128)(2,1)S(1)}, bf16[384,768]{1,0:T(8,128)(2,1)S(1)}, u32[]{:S(2)}, u32[]{:S(2)}) collective-permute-start(bf16[384,768]{1,0:T(8,128)(2,1)S(1)} %get-tuple-element.92), channel_id=1, source_target_pairs={{0,1},{1,0},{2,3},{3,2},{4,5},{5,4},{6,7},{7,6},{8,9},{9,8},{10,11... | collective-permute-start | bytes 1769480 | tf_op jit(solution)/shard_map/ppermute | solution.py:369
  116.1 26.3 %collective-permute-start.32 = (bf16[384,768]{1,0:T(8,128)(2,1)S(1)}, bf16[384,768]{1,0:T(8,128)(2,1)S(1)}, u32[]{:S(2)}, u32[]{:S(2)}) collective-permute-start(bf16[384,768]{1,0:T(8,128)(2,1)S(1)} %get-tuple-element.100), channel_id=1, source_target_pairs={{0,1},{1,0},{2,3},{3,2},{4,5},{5,4},{6,7},{7,6},{8,9},{9,8},{10,11... | collective-permute-start | bytes 1769480 | tf_op jit(solution)/shard_map/ppermute | solution.py:369
  116.6 26.8 %collective-permute-start.49 = (bf16[1,2,2,2,2,24,768]{6,5,4,3,2,1,0:T(8,128)(2,1)S(1)}, bf16[1,2,2,2,2,24,768]{6,5,4,3,2,1,0:T(8,128)(2,1)S(1)}, u32[]{:S(2)}, u32[]{:S(2)}) collective-permute-start(bf16[1,2,2,2,2,24,768]{6,5,4,3,2,1,0:T(8,128)(2,1)S(1)} %bitcast.107), channel_id=1, source_target_pairs={{0,4},{1,5},{2,6},{3,7},{4,0},{5,1},{6,2},{7,3},{8,12},{9,13},{10,... | collective-permute-start | bytes 1769480 | tf_op jit(solution)/shard_map/ppermute | solution.py:369
  123.4 21.9 %collective-permute-start.52 = (bf16[2,1,2,2,2,24,768]{6,5,4,3,2,1,0:T(8,128)(2,1)S(1)}, bf16[2,1,2,2,2,24,768]{6,5,4,3,2,1,0:T(8,128)(2,1)S(1)}, u32[]{:S(2)}, u32[]{:S(2)}) collective-permute-start(bf16[2,1,2,2,2,24,768]{6,5,4,3,2,1,0:T(8,128)(2,1)S(1)} %bitcast.106), channel_id=1, source_target_pairs={{0,8},{1,9},{2,10},{3,11},{4,12},{5,13},{6,14},{7,15},{8,0},{9,1},... | collective-permute-start | bytes 1769480 | tf_op jit(solution)/shard_map/ppermute | solution.py:369
  124.0 16.3 %collective-permute-start.56 = (bf16[1,1,2,2,2,24,384]{6,5,4,3,2,1,0:T(8,128)(2,1)S(1)}, bf16[1,1,2,2,2,24,384]{6,5,4,3,2,1,0:T(8,128)(2,1)S(1)}, u32[]{:S(2)}, u32[]{:S(2)}) collective-permute-start(bf16[1,1,2,2,2,24,384]{6,5,4,3,2,1,0:T(8,128)(2,1)S(1)} %get-tuple-element.152), channel_id=1, source_target_pairs={{0,8},{1,9},{2,10},{3,11},{4,12},{5,13},{6,14},{7,15},{8,0},{9,1},... | collective-permute-start | bytes 442376 | tf_op jit(solution)/shard_map/ppermute | solution.py:369
  142.4 32.3 %collective-permute-start.57 = (bf16[1,1,1,2,2,24,384]{6,5,4,3,2,1,0:T(8,128)(2,1)S(1)}, bf16[1,1,1,2,2,24,384]{6,5,4,3,2,1,0:T(8,128)(2,1)S(1)}, u32[]{:S(2)}, u32[]{:S(2)}) collective-permute-start(bf16[1,1,1,2,2,24,384]{6,5,4,3,2,1,0:T(8,128)(2,1)S(1)} %get-tuple-element.165), channel_id=1, source_target_pairs={{0,16},{1,17},{2,18},{3,19},{4,20},{5,21},{6,22},{7,23},{8,24},{9,... | collective-permute-start | bytes 221192 | tf_op jit(solution)/shard_map/ppermute | solution.py:369
  150.9 25.3 %collective-permute-start.60 = (bf16[1,1,1,2,2,24,384]{6,5,4,3,2,1,0:T(8,128)(2,1)S(1)}, bf16[1,1,1,2,2,24,384]{6,5,4,3,2,1,0:T(8,128)(2,1)S(1)}, u32[]{:S(2)}, u32[]{:S(2)}) collective-permute-start(bf16[1,1,1,2,2,24,384]{6,5,4,3,2,1,0:T(8,128)(2,1)S(1)} %get-tuple-element.163), channel_id=1, source_target_pairs={{0,4},{1,5},{2,6},{3,7},{4,0},{5,1},{6,2},{7,3},{8,12},{9,13},{10,... | collective-permute-start | bytes 221192 | tf_op jit(solution)/shard_map/ppermute | solution.py:369
  157.4 19.5 %collective-permute-start.44 = (bf16[1,2,2,2,2,24,768]{6,5,4,3,2,1,0:T(8,128)(2,1)S(1)}, bf16[1,2,2,2,2,24,768]{6,5,4,3,2,1,0:T(8,128)(2,1)S(1)}, u32[]{:S(2)}, u32[]{:S(2)}) collective-permute-start(bf16[1,2,2,2,2,24,768]{6,5,4,3,2,1,0:T(8,128)(2,1)S(1)} %bitcast.105), channel_id=1, source_target_pairs={{0,1},{1,0},{2,3},{3,2},{4,5},{5,4},{6,7},{7,6},{8,9},{9,8},{10,11... | collective-permute-start | bytes 1769480 | tf_op jit(solution)/shard_map/ppermute | solution.py:369
  176.2 18.7 %collective-permute-start.34 = (bf16[1,2,2,2,2,24,896]{6,5,4,3,2,1,0:T(8,128)(2,1)S(1)}, bf16[1,2,2,2,2,24,896]{6,5,4,3,2,1,0:T(8,128)(2,1)S(1)}, u32[]{:S(2)}, u32[]{:S(2)}) collective-permute-start(bf16[1,2,2,2,2,24,896]{6,5,4,3,2,1,0:T(8,128)(2,1)S(1)} %bitcast.104), channel_id=1, source_target_pairs={{0,1},{1,0},{2,3},{3,2},{4,5},{5,4},{6,7},{7,6},{8,9},{9,8},{10,11... | collective-permute-start | bytes 2064392 | tf_op jit(solution)/shard_map/ppermute | solution.py:369
  176.2 27.0 %collective-permute-start.39 = (bf16[1,2,2,2,2,24,1536]{6,5,4,3,2,1,0:T(8,128)(2,1)S(1)}, bf16[1,2,2,2,2,24,1536]{6,5,4,3,2,1,0:T(8,128)(2,1)S(1)}, u32[]{:S(2)}, u32[]{:S(2)}) collective-permute-start(bf16[1,2,2,2,2,24,1536]{6,5,4,3,2,1,0:T(8,128)(2,1)S(1)} %bitcast.103), channel_id=1, source_target_pairs={{0,1},{1,0},{2,3},{3,2},{4,5},{5,4},{6,7},{7,6},{8,9},{9,8},{10,11... | collective-permute-start | bytes 3538952 | tf_op jit(solution)/shard_map/ppermute | solution.py:369
  177.2 16.4 %collective-permute-start.45 = (bf16[1,2,1,2,2,24,768]{6,5,4,3,2,1,0:T(8,128)(2,1)S(1)}, bf16[1,2,1,2,2,24,768]{6,5,4,3,2,1,0:T(8,128)(2,1)S(1)}, u32[]{:S(2)}, u32[]{:S(2)}) collective-permute-start(bf16[1,2,1,2,2,24,768]{6,5,4,3,2,1,0:T(8,128)(2,1)S(1)} %get-tuple-element.144), channel_id=1, source_target_pairs={{0,2},{1,3},{2,0},{3,1},{4,6},{5,7},{6,4},{7,5},{8,10},{9,11},{10,... | collective-permute-start | bytes 884744 | tf_op jit(solution)/shard_map/ppermute | solution.py:369
  203.6 17.4 %collective-permute-start.40 = (bf16[1,1,2,2,2,24,1536]{6,5,4,3,2,1,0:T(8,128)(2,1)S(1)}, bf16[1,1,2,2,2,24,1536]{6,5,4,3,2,1,0:T(8,128)(2,1)S(1)}, u32[]{:S(2)}, u32[]{:S(2)}) collective-permute-start(bf16[1,1,2,2,2,24,1536]{6,5,4,3,2,1,0:T(8,128)(2,1)S(1)} %get-tuple-element.136), channel_id=1, source_target_pairs={{0,4},{1,5},{2,6},{3,7},{4,0},{5,1},{6,2},{7,3},{8,12},{9,13},{10,... | collective-permute-start | bytes 1769480 | tf_op jit(solution)/shard_map/ppermute | solution.py:369
  205.8 14.8 %collective-permute-start.36 = (bf16[1,1,1,2,2,24,896]{6,5,4,3,2,1,0:T(8,128)(2,1)S(1)}, bf16[1,1,1,2,2,24,896]{6,5,4,3,2,1,0:T(8,128)(2,1)S(1)}, u32[]{:S(2)}, u32[]{:S(2)}) collective-permute-start(bf16[1,1,1,2,2,24,896]{6,5,4,3,2,1,0:T(8,128)(2,1)S(1)} %get-tuple-element.148), channel_id=1, source_target_pairs={{0,4},{1,5},{2,6},{3,7},{4,0},{5,1},{6,2},{7,3},{8,12},{9,13},{10,... | collective-permute-start | bytes 516104 | tf_op jit(solution)/shard_map/ppermute | solution.py:369
  205.9 15.9 %collective-permute-start.48 = (bf16[1,1,1,1,1,24,768]{6,5,4,3,2,1,0:T(8,128)(2,1)S(1)}, bf16[1,1,1,1,1,24,768]{6,5,4,3,2,1,0:T(8,128)(2,1)S(1)}, u32[]{:S(2)}, u32[]{:S(2)}) collective-permute-start(bf16[1,1,1,1,1,24,768]{6,5,4,3,2,1,0:T(8,128)(2,1)S(1)} %add_convert_fusion.40), channel_id=1, source_target_pairs={{0,16},{1,17},{2,18},{3,19},{4,20},{5,21},{6,22},{7,23},{8,24},{9,... | collective-permute-start | bytes 110600 | tf_op jit(solution)/shard_map/ppermute | solution.py:369
  (48 other events, 511.3 us)

commit v3 on v2

--- a/solution.py
+++ b/solution.py
@@ -9,6 +9,7 @@
 from jax.sharding import PartitionSpec as P
 
 
+H = 12
 HD = 64
 LOW = (2, 1)
 PARTS = 4
@@ -182,7 +183,7 @@
         send[i : i + 1] = ref[pl.ds(1 - b, 1)]
 
 
-def attn_kernel(xp, qk0, qk1, vo0, vo1, cos, sin, seq_row, n1t, qr, kr, vb, ob, gains, n1):
+def attn_kernel(xp, qk0, qk1, vo0, vo1, cos, sin, seq_row, n1t, qr, kr, vb, ob, probs, gains, n1):
     d = xp.shape[1]
     qk, vo = (qk0, qk1), (vo0, vo1)
     gt = jnp.concatenate([p[:, 2 * d :] for p in qk], axis=0).astype(f32).T
@@ -211,11 +212,12 @@
         cols = slice(b * pair, (b + 1) * pair)
         q, k, v = qr[:, cols], kr[:, cols], vb[:, cols]
         outs = []
-        for mine in (low, ~low):
+        for h, mine in enumerate((low, ~low)):
             s = nt(jnp.where(mine, q, jnp.zeros_like(q)), k)
             logits = jnp.where(allowed, s * scale, MASKED)
             e = jnp.exp(logits - jnp.max(logits, axis=-1, keepdims=True))
             p = e / jnp.sum(e, axis=-1, keepdims=True)
+            probs[2 * b + h] = p
             outs.append(nn(p.astype(bf16), v))
         ob[:, cols] = jnp.where(low, outs[0], outs[1]).astype(bf16)
 
@@ -256,8 +258,8 @@
     pieces, (act, dg, du), sides, (n2t, gbt) = refs[:8], refs[8:11], refs[11:-2], refs[-2:]
     rows = pieces[0].shape[0]
     for i in range(4):
-        n2t[:, i * rows : (i + 1) * rows] = pieces[i][...].astype(f32).T.astype(bf16)
-        gbt[:, i * rows : (i + 1) * rows] = pieces[4 + i][...].astype(f32).T.astype(bf16)
+        n2t[:, i * rows : (i + 1) * rows] = pieces[i][...].T
+        gbt[:, i * rows : (i + 1) * rows] = pieces[4 + i][...].T
     fc = act.shape[1] // 2
     for c, (left, right) in enumerate(((n2t, dg[...]), (n2t, du[...]), (gbt, act[:, :fc]), (gbt, act[:, fc:]))):
         keep, send = sides[2 * c : 2 * c + 2]
@@ -293,7 +295,7 @@
     send[...] = dw[half:]
 
 
-def attn_back_kernel(qr, kr, vb, dob, n1t, cos, sin, seq_row, dq, dk, dv, keep, send):
+def attn_back_kernel(qr, kr, vb, dob, probs, n1t, cos, sin, seq_row, dq, dk, dv, keep, send):
     t, d = qr.shape
     half = d // 2
     pair = 2 * HD
@@ -304,11 +306,8 @@
         cols = slice(b * pair, (b + 1) * pair)
         q, k, v, do = qr[:, cols], kr[:, cols], vb[:, cols], dob[:, cols]
         dqs, dks, dvs = [], [], []
-        for mine in (low, ~low):
-            s = nt(jnp.where(mine, q, jnp.zeros_like(q)), k)
-            logits = jnp.where(allowed, s * scale, MASKED)
-            e = jnp.exp(logits - jnp.max(logits, axis=-1, keepdims=True))
-            p = e / jnp.sum(e, axis=-1, keepdims=True)
+        for h, mine in enumerate((low, ~low)):
+            p = probs[2 * b + h]
             dp = nt(jnp.where(mine, do, jnp.zeros_like(do)), v)
             dlogit = p * (dp - jnp.sum(dp * p, axis=-1, keepdims=True))
             ds = jnp.where(allowed, dlogit * scale, 0.0)
@@ -450,8 +449,8 @@
         xp, gb, gbg, own_sel, group_sel, change, cos2, sin2 = call(
             prep_kernel, [act] * 3 + [square] * 3 + [table] * 2, me1, tokens, cotangent, places, seq_row, cosine, sine)
         gb4 = group_gather(gbg)
-        n1t, qr, kr, vb, ob, gains, _ = call(
-            attn_kernel, [mat, act, act, act, act, ((8, d), f32), act],
+        n1t, qr, kr, vb, ob, probs, gains, _ = call(
+            attn_kernel, [mat, act, act, act, act, ((H, toks, toks), f32), ((8, d), f32), act],
             xp, *qk, *vo, cos2, sin2, seq_row)
         hmid, n2g = call(mid_kernel, [wide, act], xp, ob, *vo, gains, change)
         n24 = group_gather(n2g)
@@ -482,15 +481,17 @@
         d_wo = scatter(keep, send, second)
         dq, dk, dv, keep, send = call(
             attn_back_kernel, [act, act, act, ((half, 2 * d), bf16), ((half, 2 * d), bf16)],
-            qr, kr, vb, dob, n1t, cos2, sin2, seq_row)
+            qr, kr, vb, dob, probs, n1t, cos2, sin2, seq_row)
         d_vq = scatter(keep, send, first)
         dtok, keep, send = call(
             last_kernel, [act, ((half, d + 128), bf16), ((half, d + 128), bf16)],
             dq, dk, dv, *qk, *vo, n1t, xp, dh, gains, dgain2, own_sel)
         d_kg = scatter(keep, send, second)
         (out,) = call(out_kernel, [act], *y, hmid, own_sel, group_sel)
-        ends = (d_kg[:, d], d_vq[:, d:], d_kg[:, :d], d_vq[:, :d], d_wo.T, d_kg[:, d + 1])
-        return (out, dtok, *ends, d_gate, d_up, d_down.T)
+        gain_one, key, gain_two = d_kg[:, d], d_kg[:, :d], d_kg[:, d + 1]
+        query, value = d_vq[:, d:], d_vq[:, :d]
+        output = d_wo.T
+        return (out, dtok, gain_one, query, key, value, output, gain_two, d_gate, d_up, d_down.T)
 
     return on_device
 

time: 241 us -> 238 us (0.988)
  Pallas kernels: 36.9 us -> 34.1 us
    pallas_call x16, Pallas kernels: 36.9 us -> 34.1 us  [call(): pl.pallas_call(kernel, out_shape=out_shape, in_specs=[smem if v.size == 1...]
  transfers between devices with their start and end apart: 63 -> 63, of which waited for: 28 -> 28; matrix products, arithmetic and copies ran while one was open for 3% -> 4% of each run, Pallas kernels for 10% -> 9%
where the time goes in v3:
time: 238 us
  waiting for transfers between devices  132 us (55%)
  starting transfers between devices  61.2 us (26%)
  Pallas kernels  34.1 us (14%)
  other arithmetic  7.04 us (3%)
    ppermute x63, waiting for transfers between devices, swap(): return lax.ppermute(a, 'dp', [(i, i ^ b) for i in range(n)])  132 us
    ppermute x63, starting transfers between devices, swap(): return lax.ppermute(a, 'dp', [(i, i ^ b) for i in range(n)])  61.2 us
    pallas_call x16, Pallas kernels, call(): pl.pallas_call(kernel, out_shape=out_shape, in_specs=[smem if v.size == 1...  34.1 us
  transfers between devices with their start and end apart: 63, of which 28 were waited for; matrix products, arithmetic and copies ran while one was open for 4% of the time, Pallas kernels for 9%

profile of v3, /device:TPU:0, one launch (start us, length us, event | category | flops | bytes accessed | tf_op | source)
XLA Modules:
  0.0 237.9 jit_solution(13183773754788675294)
XLA Ops:
  2.7 4.1 %collective-permute-start = (bf16[1,1,1,1,1,24,1664]{6,5,4,3,2,1,0:T(8,128)(2,1)}, bf16[1,1,1,1,1,24,1664]{6,5,4,3,2,1,0:T(8,128)(2,1)S(1)}, u32[]{:S(2)}, u32[]{:S(2)}) collective-permute-start(bf16[1,1,1,1,1,24,1664]{6,5,4,3,2,1,0:T(8,128)(2,1)} %bitcast.110), channel_id=1, source_target_pairs={{0,16},{1,17},{2,18},{3,19},{4,20},{5,21},{6,22},{7,23},{8,24},{9,... | collective-permute-start | bytes 239624 | tf_op jit(solution)/shard_map/ppermute | solution.py:368
  6.9 5.4 %collective-permute-done = bf16[1,1,1,1,1,24,1664]{6,5,4,3,2,1,0:T(8,128)(2,1)S(1)} collective-permute-done((bf16[1,1,1,1,1,24,1664]{6,5,4,3,2,1,0:T(8,128)(2,1)}, bf16[1,1,1,1,1,24,1664]{6,5,4,3,2,1,0:T(8,128)(2,1)S(1)}, u32[]{:S(2)}, u32[]{:S(2)}) %collective-permute-start) | collective-permute-done | bytes 79904 | tf_op jit(solution)/shard_map/ppermute | solution.py:368
  16.3 3.5 %collective-permute-done.1 = bf16[1,1,1,1,2,24,1664]{6,5,4,3,2,1,0:T(8,128)(2,1)S(1)} collective-permute-done((bf16[1,1,1,1,2,24,1664]{6,5,4,3,2,1,0:T(8,128)(2,1)S(1)}, bf16[1,1,1,1,2,24,1664]{6,5,4,3,2,1,0:T(8,128)(2,1)S(1)}, u32[]{:S(2)}, u32[]{:S(2)}) %collective-permute-start.1) | collective-permute-done | bytes 159776 | tf_op jit(solution)/shard_map/ppermute | solution.py:368
  25.3 4.0 %collective-permute-done.2 = bf16[1,1,1,2,2,24,1664]{6,5,4,3,2,1,0:T(8,128)(2,1)S(1)} collective-permute-done((bf16[1,1,1,2,2,24,1664]{6,5,4,3,2,1,0:T(8,128)(2,1)S(1)}, bf16[1,1,1,2,2,24,1664]{6,5,4,3,2,1,0:T(8,128)(2,1)S(1)}, u32[]{:S(2)}, u32[]{:S(2)}) %collective-permute-start.2) | collective-permute-done | bytes 319520 | tf_op jit(solution)/shard_map/ppermute | solution.py:368
  29.4 3.2 %collective-permute-start.3 = (bf16[1,1,2,2,2,24,1664]{6,5,4,3,2,1,0:T(8,128)(2,1)S(1)}, bf16[1,1,2,2,2,24,1664]{6,5,4,3,2,1,0:T(8,128)(2,1)S(1)}, u32[]{:S(2)}, u32[]{:S(2)}) collective-permute-start(bf16[1,1,2,2,2,24,1664]{6,5,4,3,2,1,0:T(8,128)(2,1)S(1)} %pad_maximum_fusion.4), channel_id=1, source_target_pairs={{0,4},{1,5},{2,6},{3,7},{4,0},{5,1},{6,2},{7,3},{8,12},{9,13},{10,... | collective-permute-start | bytes 1916936 | tf_op jit(solution)/shard_map/ppermute | solution.py:368
  34.8 4.9 %collective-permute-done.16.got = bf16[24,4608]{1,0:T(8,128)(2,1)S(1)} collective-permute-done((bf16[24,4608]{1,0:T(8,128)(2,1)S(1)}, bf16[24,4608]{1,0:T(8,128)(2,1)S(1)}, u32[]{:S(2)}, u32[]{:S(2)}) %collective-permute-start.16) | collective-permute-done | bytes 221216 | tf_op jit(solution)/shard_map/ppermute | solution.py:368
  46.7 7.8 %collective-permute-done.24 = bf16[1,1,1,2,2,24,384]{6,5,4,3,2,1,0:T(8,128)(2,1)S(1)} collective-permute-done((bf16[1,1,1,2,2,24,384]{6,5,4,3,2,1,0:T(8,128)(2,1)S(1)}, bf16[1,1,1,2,2,24,384]{6,5,4,3,2,1,0:T(8,128)(2,1)S(1)}, u32[]{:S(2)}, u32[]{:S(2)}) %collective-permute-start.24) | collective-permute-done | bytes 73760 | tf_op jit(solution)/shard_map/ppermute | solution.py:368
  58.6 10.6 %collective-permute-done.25 = bf16[1,1,2,2,2,24,384]{6,5,4,3,2,1,0:T(8,128)(2,1)S(1)} collective-permute-done((bf16[1,1,2,2,2,24,384]{6,5,4,3,2,1,0:T(8,128)(2,1)S(1)}, bf16[1,1,2,2,2,24,384]{6,5,4,3,2,1,0:T(8,128)(2,1)S(1)}, u32[]{:S(2)}, u32[]{:S(2)}) %collective-permute-start.25) | collective-permute-done | bytes 147488 | tf_op jit(solution)/shard_map/ppermute | solution.py:368
  69.3 5.9 %collective-permute-done.19 = bf16[1,1,2,2,2,24,768]{6,5,4,3,2,1,0:T(8,128)(2,1)S(1)} collective-permute-done((bf16[1,1,2,2,2,24,768]{6,5,4,3,2,1,0:T(8,128)(2,1)S(1)}, bf16[1,1,2,2,2,24,768]{6,5,4,3,2,1,0:T(8,128)(2,1)S(1)}, u32[]{:S(2)}, u32[]{:S(2)}) %collective-permute-start.19) | collective-permute-done | bytes 294944 | tf_op jit(solution)/shard_map/ppermute | solution.py:368
  83.4 4.0 %shard_map.223 = (bf16[768,192]{1,0:T(8,128)(2,1)S(1)}, bf16[192,768]{1,0:T(8,128)(2,1)S(1)}, bf16[192,768]{1,0:T(8,128)(2,1)S(1)}, bf16[192,768]{1,0:T(8,128)(2...) custom-call(bf16[192,768]{1,0:T(8,128)(2,1)S(1)} %get-tuple-element., ...), custom_call_target="tpu_custom_call" | custom-call | tf_op jit(solution)/shard_map/pallas_call | solution.py:53
  89.1 10.7 %collective-permute-done.29 = bf16[2,1,2,2,2,24,384]{6,5,4,3,2,1,0:T(8,128)(2,1)S(1)} collective-permute-done((bf16[2,1,2,2,2,24,384]{6,5,4,3,2,1,0:T(8,128)(2,1)S(1)}, bf16[2,1,2,2,2,24,384]{6,5,4,3,2,1,0:T(8,128)(2,1)S(1)}, u32[]{:S(2)}, u32[]{:S(2)}) %collective-permute-start.29) | collective-permute-done | bytes 294944 | tf_op jit(solution)/shard_map/ppermute | solution.py:368
  102.3 7.5 %shard_map.227 = (bf16[768,768]{1,0:T(8,128)(2,1)S(1)}, bf16[768,768]{1,0:T(8,128)(2,1)S(1)}, bf16[768,768]{1,0:T(8,128)(2,1)S(1)}, bf16[384,768]{1,0:T(8,128)(2,1)S(1)}, bf16[384,768]{1,0:T(8,128)(2,1)S(1)}) custom-call(bf16[192,768]{1,0:T(8,128)(2,1)S(1)} %get-tuple-element.81.refs_0_, bf16[192,768]{1,0:T(8,128)(2,1)S(1)} %collective-permute-done.10.refs_1_, ...), custom_call_target="tpu_custom_call" | custom-call | tf_op jit(solution)/shard_map/pallas_call | solution.py:53
  109.8 3.5 %shard_map.233 = (bf16[384,768]{1,0:T(8,128)(2,1)S(1)}, bf16[384,768]{1,0:T(8,128)(2,1)S(1)}, bf16[384,768]{1,0:T(8,128)(2,1)S(1)}, bf16[384,768]{1,0:T(8,128)(2...) custom-call(bf16[192,768]{1,0:T(8,128)(2,1)S(1)} %get-tuple-element., ...), custom_call_target="tpu_custom_call" | custom-call | tf_op jit(solution)/shard_map/pallas_call | solution.py:53
  117.8 5.4 %collective-permute-done.55 = bf16[1,2,2,2,2,24,384]{6,5,4,3,2,1,0:T(8,128)(2,1)S(1)} collective-permute-done((bf16[1,2,2,2,2,24,384]{6,5,4,3,2,1,0:T(8,128)(2,1)S(1)}, bf16[1,2,2,2,2,24,384]{6,5,4,3,2,1,0:T(8,128)(2,1)S(1)}, u32[]{:S(2)}, u32[]{:S(2)}) %collective-permute-start.55) | collective-permute-done | bytes 294944 | tf_op jit(solution)/shard_map/ppermute | solution.py:368
  125.5 14.6 %collective-permute-done.56 = bf16[1,1,2,2,2,24,384]{6,5,4,3,2,1,0:T(8,128)(2,1)S(1)} collective-permute-done((bf16[1,1,2,2,2,24,384]{6,5,4,3,2,1,0:T(8,128)(2,1)S(1)}, bf16[1,1,2,2,2,24,384]{6,5,4,3,2,1,0:T(8,128)(2,1)S(1)}, u32[]{:S(2)}, u32[]{:S(2)}) %collective-permute-start.56) | collective-permute-done | bytes 147488 | tf_op jit(solution)/shard_map/ppermute | solution.py:368
  146.1 4.6 %collective-permute-done.59 = bf16[2,1,1,2,2,24,384]{6,5,4,3,2,1,0:T(8,128)(2,1)S(1)} collective-permute-done((bf16[2,1,1,2,2,24,384]{6,5,4,3,2,1,0:T(8,128)(2,1)S(1)}, bf16[2,1,1,2,2,24,384]{6,5,4,3,2,1,0:T(8,128)(2,1)S(1)}, u32[]{:S(2)}, u32[]{:S(2)}) %collective-permute-start.59) | collective-permute-done | bytes 147488 | tf_op jit(solution)/shard_map/ppermute | solution.py:368
  153.0 4.2 %collective-permute-done.50 = bf16[1,1,2,2,2,24,768]{6,5,4,3,2,1,0:T(8,128)(2,1)S(1)} collective-permute-done((bf16[1,1,2,2,2,24,768]{6,5,4,3,2,1,0:T(8,128)(2,1)S(1)}, bf16[1,1,2,2,2,24,768]{6,5,4,3,2,1,0:T(8,128)(2,1)S(1)}, u32[]{:S(2)}, u32[]{:S(2)}) %collective-permute-start.50) | collective-permute-done | bytes 294944 | tf_op jit(solution)/shard_map/ppermute | solution.py:368
  157.3 6.0 %collective-permute-done.53 = bf16[2,1,1,2,2,24,768]{6,5,4,3,2,1,0:T(8,128)(2,1)S(1)} collective-permute-done((bf16[2,1,1,2,2,24,768]{6,5,4,3,2,1,0:T(8,128)(2,1)S(1)}, bf16[2,1,1,2,2,24,768]{6,5,4,3,2,1,0:T(8,128)(2,1)S(1)}, u32[]{:S(2)}, u32[]{:S(2)}) %collective-permute-start.53) | collective-permute-done | bytes 294944 | tf_op jit(solution)/shard_map/ppermute | solution.py:368
  164.3 4.6 %shard_map.231 = (bf16[192,768]{1,0:T(8,128)(2,1)S(1)}, bf16[192,768]{1,0:T(8,128)(2,1)S(1)}, bf16[192,768]{1,0:T(8,128)(2,1)S(1)}, bf16[384,1536]{1,0:T(8,128)(2,1)S(1)}, bf16[384,1536]{1,0:T(8,128)(2,1)S(1)}) custom-call(bf16[192,768]{1,0:T(8,128)(2,1)S(1)} %get-tuple-element.97.qr, bf16[192,768]{1,0:T(8,128)(2,1)S(1)} %get-tuple-element.98.kr, ...), custom_call_target="tpu_custom_call" | custom-call | tf_op jit(solution)/shard_map/pallas_call | solution.py:53
  182.4 7.3 %collective-permute-done.62.refs_1_ = bf16[2,24,2304]{2,1,0:T(8,128)(2,1)S(1)} collective-permute-done((bf16[2,24,2304]{2,1,0:T(8,128)(2,1)S(1)}, bf16[2,24,2304]{2,1,0:T(8,128)(2,1)S(1)}, u32[]{:S(2)}, u32[]{:S(2)}) %collective-permute-start.62) | collective-permute-done | bytes 221216 | tf_op jit(solution)/shard_map/ppermute | solution.py:368
  196.0 4.3 %collective-permute-start.47 = (bf16[1,1,1,1,2,24,768]{6,5,4,3,2,1,0:T(8,128)(2,1)S(1)}, bf16[1,1,1,1,2,24,768]{6,5,4,3,2,1,0:T(8,128)(2,1)S(1)}, u32[]{:S(2)}, u32[]{:S(2)}) collective-permute-start(bf16[1,1,1,1,2,24,768]{6,5,4,3,2,1,0:T(8,128)(2,1)S(1)} %get-tuple-element.170), channel_id=1, source_target_pairs={{0,8},{1,9},{2,10},{3,11},{4,12},{5,13},{6,14},{7,15},{8,0},{9,1},... | collective-permute-start | bytes 221192 | tf_op jit(solution)/shard_map/ppermute | solution.py:368
  204.8 12.9 %collective-permute-done.36 = bf16[1,1,1,2,2,24,896]{6,5,4,3,2,1,0:T(8,128)(2,1)S(1)} collective-permute-done((bf16[1,1,1,2,2,24,896]{6,5,4,3,2,1,0:T(8,128)(2,1)S(1)}, bf16[1,1,1,2,2,24,896]{6,5,4,3,2,1,0:T(8,128)(2,1)S(1)}, u32[]{:S(2)}, u32[]{:S(2)}) %collective-permute-start.36) | collective-permute-done | bytes 172064 | tf_op jit(solution)/shard_map/ppermute | solution.py:368
  219.5 3.2 %collective-permute-done.37 = bf16[1,1,1,1,2,24,896]{6,5,4,3,2,1,0:T(8,128)(2,1)S(1)} collective-permute-done((bf16[1,1,1,1,2,24,896]{6,5,4,3,2,1,0:T(8,128)(2,1)S(1)}, bf16[1,1,1,1,2,24,896]{6,5,4,3,2,1,0:T(8,128)(2,1)S(1)}, u32[]{:S(2)}, u32[]{:S(2)}) %collective-permute-start.37) | collective-permute-done | bytes 86048 | tf_op jit(solution)/shard_map/ppermute | solution.py:368
  231.9 5.3 %collective-permute-done.43 = bf16[1,1,1,1,1,24,1536]{6,5,4,3,2,1,0:T(8,128)(2,1)S(1)} collective-permute-done((bf16[1,1,1,1,1,24,1536]{6,5,4,3,2,1,0:T(8,128)(2,1)S(1)}, bf16[1,1,1,1,1,24,1536]{6,5,4,3,2,1,0:T(8,128)(2,1)S(1)}, u32[]{:S(2)}, u32[]{:S(2)}) %collective-permute-start.43) | collective-permute-done | bytes 73760 | tf_op jit(solution)/shard_map/ppermute | solution.py:368
  (187 shorter events, 89.0 us)
Async XLA Ops:
  29.4 16.3 %collective-permute-start.3 = (bf16[1,1,2,2,2,24,1664]{6,5,4,3,2,1,0:T(8,128)(2,1)S(1)}, bf16[1,1,2,2,2,24,1664]{6,5,4,3,2,1,0:T(8,128)(2,1)S(1)}, u32[]{:S(2)}, u32[]{:S(2)}) collective-permute-start(bf16[1,1,2,2,2,24,1664]{6,5,4,3,2,1,0:T(8,128)(2,1)S(1)} %pad_maximum_fusion.4), channel_id=1, source_target_pairs={{0,4},{1,5},{2,6},{3,7},{4,0},{5,1},{6,2},{7,3},{8,12},{9,13},{10,... | collective-permute-start | bytes 1916936 | tf_op jit(solution)/shard_map/ppermute | solution.py:368
  46.5 34.9 %collective-permute-start.4 = (bf16[1,2,2,2,2,24,1664]{6,5,4,3,2,1,0:T(8,128)(2,1)S(1)}, bf16[1,2,2,2,2,24,1664]{6,5,4,3,2,1,0:T(8,128)(2,1)S(1)}, u32[]{:S(2)}, u32[]{:S(2)}) collective-permute-start(bf16[1,2,2,2,2,24,1664]{6,5,4,3,2,1,0:T(8,128)(2,1)S(1)} %pad_maximum_fusion), channel_id=1, source_target_pairs={{0,1},{1,0},{2,3},{3,2},{4,5},{5,4},{6,7},{7,6},{8,9},{9,8},{10,11... | collective-permute-start | bytes 3833864 | tf_op jit(solution)/shard_map/ppermute | solution.py:368
  54.5 25.4 %collective-permute-start.9 = (bf16[1,2,2,2,2,24,1536]{6,5,4,3,2,1,0:T(8,128)(2,1)S(1)}, bf16[1,2,2,2,2,24,1536]{6,5,4,3,2,1,0:T(8,128)(2,1)S(1)}, u32[]{:S(2)}, u32[]{:S(2)}) collective-permute-start(bf16[1,2,2,2,2,24,1536]{6,5,4,3,2,1,0:T(8,128)(2,1)S(1)} %pad_maximum_fusion.1), channel_id=1, source_target_pairs={{0,1},{1,0},{2,3},{3,2},{4,5},{5,4},{6,7},{7,6},{8,9},{9,8},{10,11... | collective-permute-start | bytes 3538952 | tf_op jit(solution)/shard_map/ppermute | solution.py:368
  54.5 14.7 %collective-permute-start.25 = (bf16[1,1,2,2,2,24,384]{6,5,4,3,2,1,0:T(8,128)(2,1)S(1)}, bf16[1,1,2,2,2,24,384]{6,5,4,3,2,1,0:T(8,128)(2,1)S(1)}, u32[]{:S(2)}, u32[]{:S(2)}) collective-permute-start(bf16[1,1,2,2,2,24,384]{6,5,4,3,2,1,0:T(8,128)(2,1)S(1)} %pad_maximum_fusion.18), channel_id=1, source_target_pairs={{0,8},{1,9},{2,10},{3,11},{4,12},{5,13},{6,14},{7,15},{8,0},{9,1},... | collective-permute-start | bytes 442376 | tf_op jit(solution)/shard_map/ppermute | solution.py:368
  54.9 20.2 %collective-permute-start.19 = (bf16[1,1,2,2,2,24,768]{6,5,4,3,2,1,0:T(8,128)(2,1)S(1)}, bf16[1,1,2,2,2,24,768]{6,5,4,3,2,1,0:T(8,128)(2,1)S(1)}, u32[]{:S(2)}, u32[]{:S(2)}) collective-permute-start(bf16[1,1,2,2,2,24,768]{6,5,4,3,2,1,0:T(8,128)(2,1)S(1)} %pad_maximum_fusion.12), channel_id=1, source_target_pairs={{0,8},{1,9},{2,10},{3,11},{4,12},{5,13},{6,14},{7,15},{8,0},{9,1},... | collective-permute-start | bytes 884744 | tf_op jit(solution)/shard_map/ppermute | solution.py:368
  56.8 19.2 %collective-permute-start.22 = (bf16[2,1,1,2,2,24,768]{6,5,4,3,2,1,0:T(8,128)(2,1)S(1)}, bf16[2,1,1,2,2,24,768]{6,5,4,3,2,1,0:T(8,128)(2,1)S(1)}, u32[]{:S(2)}, u32[]{:S(2)}) collective-permute-start(bf16[2,1,1,2,2,24,768]{6,5,4,3,2,1,0:T(8,128)(2,1)S(1)} %pad_maximum_fusion.13), channel_id=1, source_target_pairs={{0,16},{1,17},{2,18},{3,19},{4,20},{5,21},{6,22},{7,23},{8,24},{9,... | collective-permute-start | bytes 884744 | tf_op jit(solution)/shard_map/ppermute | solution.py:368
  75.2 13.4 %collective-permute-start.26 = (bf16[1,2,2,2,2,24,384]{6,5,4,3,2,1,0:T(8,128)(2,1)S(1)}, bf16[1,2,2,2,2,24,384]{6,5,4,3,2,1,0:T(8,128)(2,1)S(1)}, u32[]{:S(2)}, u32[]{:S(2)}) collective-permute-start(bf16[1,2,2,2,2,24,384]{6,5,4,3,2,1,0:T(8,128)(2,1)S(1)} %pad_maximum_fusion.14), channel_id=1, source_target_pairs={{0,4},{1,5},{2,6},{3,7},{4,0},{5,1},{6,2},{7,3},{8,12},{9,13},{10,... | collective-permute-start | bytes 884744 | tf_op jit(solution)/shard_map/ppermute | solution.py:368
  76.0 23.9 %collective-permute-start.20 = (bf16[1,2,2,2,2,24,768]{6,5,4,3,2,1,0:T(8,128)(2,1)S(1)}, bf16[1,2,2,2,2,24,768]{6,5,4,3,2,1,0:T(8,128)(2,1)S(1)}, u32[]{:S(2)}, u32[]{:S(2)}) collective-permute-start(bf16[1,2,2,2,2,24,768]{6,5,4,3,2,1,0:T(8,128)(2,1)S(1)} %pad_maximum_fusion.6), channel_id=1, source_target_pairs={{0,4},{1,5},{2,6},{3,7},{4,0},{5,1},{6,2},{7,3},{8,12},{9,13},{10,... | collective-permute-start | bytes 1769480 | tf_op jit(solution)/shard_map/ppermute | solution.py:368
  79.6 21.1 %collective-permute-start.23 = (bf16[2,1,2,2,2,24,768]{6,5,4,3,2,1,0:T(8,128)(2,1)S(1)}, bf16[2,1,2,2,2,24,768]{6,5,4,3,2,1,0:T(8,128)(2,1)S(1)}, u32[]{:S(2)}, u32[]{:S(2)}) collective-permute-start(bf16[2,1,2,2,2,24,768]{6,5,4,3,2,1,0:T(8,128)(2,1)S(1)} %pad_maximum_fusion.7), channel_id=1, source_target_pairs={{0,8},{1,9},{2,10},{3,11},{4,12},{5,13},{6,14},{7,15},{8,0},{9,1},... | collective-permute-start | bytes 1769480 | tf_op jit(solution)/shard_map/ppermute | solution.py:368
  81.4 18.4 %collective-permute-start.29 = (bf16[2,1,2,2,2,24,384]{6,5,4,3,2,1,0:T(8,128)(2,1)S(1)}, bf16[2,1,2,2,2,24,384]{6,5,4,3,2,1,0:T(8,128)(2,1)S(1)}, u32[]{:S(2)}, u32[]{:S(2)}) collective-permute-start(bf16[2,1,2,2,2,24,384]{6,5,4,3,2,1,0:T(8,128)(2,1)S(1)} %pad_maximum_fusion.15), channel_id=1, source_target_pairs={{0,8},{1,9},{2,10},{3,11},{4,12},{5,13},{6,14},{7,15},{8,0},{9,1},... | collective-permute-start | bytes 884744 | tf_op jit(solution)/shard_map/ppermute | solution.py:368
  115.8 47.5 %collective-permute-start.30 = (bf16[384,768]{1,0:T(8,128)(2,1)S(1)}, bf16[384,768]{1,0:T(8,128)(2,1)S(1)}, u32[]{:S(2)}, u32[]{:S(2)}) collective-permute-start(bf16[384,768]{1,0:T(8,128)(2,1)S(1)} %get-tuple-element.93), channel_id=1, source_target_pairs={{0,1},{1,0},{2,3},{3,2},{4,5},{5,4},{6,7},{7,6},{8,9},{9,8},{10,11... | collective-permute-start | bytes 1769480 | tf_op jit(solution)/shard_map/ppermute | solution.py:368
  115.9 26.3 %collective-permute-start.32 = (bf16[384,768]{1,0:T(8,128)(2,1)S(1)}, bf16[384,768]{1,0:T(8,128)(2,1)S(1)}, u32[]{:S(2)}, u32[]{:S(2)}) collective-permute-start(bf16[384,768]{1,0:T(8,128)(2,1)S(1)} %get-tuple-element.101), channel_id=1, source_target_pairs={{0,1},{1,0},{2,3},{3,2},{4,5},{5,4},{6,7},{7,6},{8,9},{9,8},{10,11... | collective-permute-start | bytes 1769480 | tf_op jit(solution)/shard_map/ppermute | solution.py:368
  116.4 26.8 %collective-permute-start.49 = (bf16[1,2,2,2,2,24,768]{6,5,4,3,2,1,0:T(8,128)(2,1)S(1)}, bf16[1,2,2,2,2,24,768]{6,5,4,3,2,1,0:T(8,128)(2,1)S(1)}, u32[]{:S(2)}, u32[]{:S(2)}) collective-permute-start(bf16[1,2,2,2,2,24,768]{6,5,4,3,2,1,0:T(8,128)(2,1)S(1)} %bitcast.107), channel_id=1, source_target_pairs={{0,4},{1,5},{2,6},{3,7},{4,0},{5,1},{6,2},{7,3},{8,12},{9,13},{10,... | collective-permute-start | bytes 1769480 | tf_op jit(solution)/shard_map/ppermute | solution.py:368
  123.2 21.9 %collective-permute-start.52 = (bf16[2,1,2,2,2,24,768]{6,5,4,3,2,1,0:T(8,128)(2,1)S(1)}, bf16[2,1,2,2,2,24,768]{6,5,4,3,2,1,0:T(8,128)(2,1)S(1)}, u32[]{:S(2)}, u32[]{:S(2)}) collective-permute-start(bf16[2,1,2,2,2,24,768]{6,5,4,3,2,1,0:T(8,128)(2,1)S(1)} %bitcast.106), channel_id=1, source_target_pairs={{0,8},{1,9},{2,10},{3,11},{4,12},{5,13},{6,14},{7,15},{8,0},{9,1},... | collective-permute-start | bytes 1769480 | tf_op jit(solution)/shard_map/ppermute | solution.py:368
  123.7 16.3 %collective-permute-start.56 = (bf16[1,1,2,2,2,24,384]{6,5,4,3,2,1,0:T(8,128)(2,1)S(1)}, bf16[1,1,2,2,2,24,384]{6,5,4,3,2,1,0:T(8,128)(2,1)S(1)}, u32[]{:S(2)}, u32[]{:S(2)}) collective-permute-start(bf16[1,1,2,2,2,24,384]{6,5,4,3,2,1,0:T(8,128)(2,1)S(1)} %get-tuple-element.154), channel_id=1, source_target_pairs={{0,8},{1,9},{2,10},{3,11},{4,12},{5,13},{6,14},{7,15},{8,0},{9,1},... | collective-permute-start | bytes 442376 | tf_op jit(solution)/shard_map/ppermute | solution.py:368
  142.2 29.6 %collective-permute-start.57 = (bf16[1,1,1,2,2,24,384]{6,5,4,3,2,1,0:T(8,128)(2,1)S(1)}, bf16[1,1,1,2,2,24,384]{6,5,4,3,2,1,0:T(8,128)(2,1)S(1)}, u32[]{:S(2)}, u32[]{:S(2)}) collective-permute-start(bf16[1,1,1,2,2,24,384]{6,5,4,3,2,1,0:T(8,128)(2,1)S(1)} %get-tuple-element.167), channel_id=1, source_target_pairs={{0,16},{1,17},{2,18},{3,19},{4,20},{5,21},{6,22},{7,23},{8,24},{9,... | collective-permute-start | bytes 221192 | tf_op jit(solution)/shard_map/ppermute | solution.py:368
  150.7 22.6 %collective-permute-start.60 = (bf16[1,1,1,2,2,24,384]{6,5,4,3,2,1,0:T(8,128)(2,1)S(1)}, bf16[1,1,1,2,2,24,384]{6,5,4,3,2,1,0:T(8,128)(2,1)S(1)}, u32[]{:S(2)}, u32[]{:S(2)}) collective-permute-start(bf16[1,1,1,2,2,24,384]{6,5,4,3,2,1,0:T(8,128)(2,1)S(1)} %get-tuple-element.165), channel_id=1, source_target_pairs={{0,4},{1,5},{2,6},{3,7},{4,0},{5,1},{6,2},{7,3},{8,12},{9,13},{10,... | collective-permute-start | bytes 221192 | tf_op jit(solution)/shard_map/ppermute | solution.py:368
  157.2 16.9 %collective-permute-start.44 = (bf16[1,2,2,2,2,24,768]{6,5,4,3,2,1,0:T(8,128)(2,1)S(1)}, bf16[1,2,2,2,2,24,768]{6,5,4,3,2,1,0:T(8,128)(2,1)S(1)}, u32[]{:S(2)}, u32[]{:S(2)}) collective-permute-start(bf16[1,2,2,2,2,24,768]{6,5,4,3,2,1,0:T(8,128)(2,1)S(1)} %bitcast.105), channel_id=1, source_target_pairs={{0,1},{1,0},{2,3},{3,2},{4,5},{5,4},{6,7},{7,6},{8,9},{9,8},{10,11... | collective-permute-start | bytes 1769480 | tf_op jit(solution)/shard_map/ppermute | solution.py:368
  173.3 18.6 %collective-permute-start.34 = (bf16[1,2,2,2,2,24,896]{6,5,4,3,2,1,0:T(8,128)(2,1)S(1)}, bf16[1,2,2,2,2,24,896]{6,5,4,3,2,1,0:T(8,128)(2,1)S(1)}, u32[]{:S(2)}, u32[]{:S(2)}) collective-permute-start(bf16[1,2,2,2,2,24,896]{6,5,4,3,2,1,0:T(8,128)(2,1)S(1)} %bitcast.104), channel_id=1, source_target_pairs={{0,1},{1,0},{2,3},{3,2},{4,5},{5,4},{6,7},{7,6},{8,9},{9,8},{10,11... | collective-permute-start | bytes 2064392 | tf_op jit(solution)/shard_map/ppermute | solution.py:368
  173.3 27.0 %collective-permute-start.39 = (bf16[1,2,2,2,2,24,1536]{6,5,4,3,2,1,0:T(8,128)(2,1)S(1)}, bf16[1,2,2,2,2,24,1536]{6,5,4,3,2,1,0:T(8,128)(2,1)S(1)}, u32[]{:S(2)}, u32[]{:S(2)}) collective-permute-start(bf16[1,2,2,2,2,24,1536]{6,5,4,3,2,1,0:T(8,128)(2,1)S(1)} %bitcast.103), channel_id=1, source_target_pairs={{0,1},{1,0},{2,3},{3,2},{4,5},{5,4},{6,7},{7,6},{8,9},{9,8},{10,11... | collective-permute-start | bytes 3538952 | tf_op jit(solution)/shard_map/ppermute | solution.py:368
  174.2 16.5 %collective-permute-start.45 = (bf16[1,2,1,2,2,24,768]{6,5,4,3,2,1,0:T(8,128)(2,1)S(1)}, bf16[1,2,1,2,2,24,768]{6,5,4,3,2,1,0:T(8,128)(2,1)S(1)}, u32[]{:S(2)}, u32[]{:S(2)}) collective-permute-start(bf16[1,2,1,2,2,24,768]{6,5,4,3,2,1,0:T(8,128)(2,1)S(1)} %get-tuple-element.146), channel_id=1, source_target_pairs={{0,2},{1,3},{2,0},{3,1},{4,6},{5,7},{6,4},{7,5},{8,10},{9,11},{10,... | collective-permute-start | bytes 884744 | tf_op jit(solution)/shard_map/ppermute | solution.py:368
  200.8 17.3 %collective-permute-start.40 = (bf16[1,1,2,2,2,24,1536]{6,5,4,3,2,1,0:T(8,128)(2,1)S(1)}, bf16[1,1,2,2,2,24,1536]{6,5,4,3,2,1,0:T(8,128)(2,1)S(1)}, u32[]{:S(2)}, u32[]{:S(2)}) collective-permute-start(bf16[1,1,2,2,2,24,1536]{6,5,4,3,2,1,0:T(8,128)(2,1)S(1)} %get-tuple-element.138), channel_id=1, source_target_pairs={{0,4},{1,5},{2,6},{3,7},{4,0},{5,1},{6,2},{7,3},{8,12},{9,13},{10,... | collective-permute-start | bytes 1769480 | tf_op jit(solution)/shard_map/ppermute | solution.py:368
  202.9 14.7 %collective-permute-start.36 = (bf16[1,1,1,2,2,24,896]{6,5,4,3,2,1,0:T(8,128)(2,1)S(1)}, bf16[1,1,1,2,2,24,896]{6,5,4,3,2,1,0:T(8,128)(2,1)S(1)}, u32[]{:S(2)}, u32[]{:S(2)}) collective-permute-start(bf16[1,1,1,2,2,24,896]{6,5,4,3,2,1,0:T(8,128)(2,1)S(1)} %get-tuple-element.150), channel_id=1, source_target_pairs={{0,4},{1,5},{2,6},{3,7},{4,0},{5,1},{6,2},{7,3},{8,12},{9,13},{10,... | collective-permute-start | bytes 516104 | tf_op jit(solution)/shard_map/ppermute | solution.py:368
  203.0 15.8 %collective-permute-start.48 = (bf16[1,1,1,1,1,24,768]{6,5,4,3,2,1,0:T(8,128)(2,1)S(1)}, bf16[1,1,1,1,1,24,768]{6,5,4,3,2,1,0:T(8,128)(2,1)S(1)}, u32[]{:S(2)}, u32[]{:S(2)}) collective-permute-start(bf16[1,1,1,1,1,24,768]{6,5,4,3,2,1,0:T(8,128)(2,1)S(1)} %add_convert_fusion.40), channel_id=1, source_target_pairs={{0,16},{1,17},{2,18},{3,19},{4,20},{5,21},{6,22},{7,23},{8,24},{9,... | collective-permute-start | bytes 110600 | tf_op jit(solution)/shard_map/ppermute | solution.py:368
  (48 other events, 506.0 us)
